TPU v7x, 32 devices: a whole 2x2x4 slice. The times are simulated.
32 devices in a mesh: gx: 2 (over y), gy: 16 (over z, x, core).
Axes of the slice: x: 2, y: 2, z: 4, core: 2. Of those that a mesh axis runs over, the one named last changes fastest.
Arguments:
- density: float32 [16, 256, 128], P('gx', 'gy'), may hold values from -3 to 3
- populations: float32 [19, 8, 64, 128], P(None, 'gx', 'gy'), may hold values from 0 to 0.6, as said below
Outputs:
- density_next: float32 [16, 256, 128], P('gx', 'gy')
- populations_next: float32 [19, 8, 64, 128], P(None, 'gx', 'gy')
Inputs may be any that keep to these rules, and one draw needn't show every extreme that they name: `populations`: each population is its lattice weight times a factor between 0.4 and 1.6.
All inputs are finite; a program needn't handle non-finite values.
Results may differ from a plain program's by a relative error of at most 0.00023.
Values sent between devices are 32-bit elements; how exact they have to be, the bound alone decides.
No kernel may reach another device: no remote copies, remote signals or barrier semaphores. Data moves between devices by JAX's collectives and lax.ppermute only.
A program may use at most 64 MiB of HBM per device.

v0:
```python
import jax
import jax.numpy as jnp
from jax import lax
from jax.sharding import PartitionSpec as P

DENSITY_SUBSTEPS = 2


coupled_time_step = 0.0008
force_unit = 0.005
speed_unit = 2000.0
relax_time = 0.8
quench_depth = -0.25


def padded(block, sides, width):
    for axis, dim in sides:
        count = lax.axis_size(axis)
        forward = [(i, i + 1) for i in range(count - 1)]
        forward.append((count - 1, 0))
        backward = [(target, source) for source, target in forward]
        low = lax.ppermute(
            lax.slice_in_dim(block, block.shape[dim] - width, None, axis=dim), axis, forward
        )
        high = lax.ppermute(lax.slice_in_dim(block, 0, width, axis=dim), axis, backward)
        block = jnp.concatenate([low, block, high], axis=dim)
    return block


def lattice():
    speeds = [
        (0, 0, 0),
        (1, 0, 0),
        (-1, 0, 0),
        (0, 1, 0),
        (0, -1, 0),
        (0, 0, 1),
        (0, 0, -1),
        (1, 1, 0),
        (-1, -1, 0),
        (1, -1, 0),
        (-1, 1, 0),
        (1, 0, 1),
        (-1, 0, -1),
        (1, 0, -1),
        (-1, 0, 1),
        (0, 1, 1),
        (0, -1, -1),
        (0, 1, -1),
        (0, -1, 1),
    ]
    weights = [1.0 / 3.0] + [1.0 / 18.0] * 6 + [1.0 / 36.0] * 12
    return (speeds, weights)


def laplace_ext(grid_field):
    center = grid_field[1:-1, 1:-1]
    running = -6.0 * center
    running = running + grid_field[:-2, 1:-1] + grid_field[2:, 1:-1]
    running = running + grid_field[1:-1, :-2] + grid_field[1:-1, 2:]
    running = running + jnp.roll(center, 1, 2) + jnp.roll(center, -1, 2)
    return running


def potential_ext(grid_field):
    first_lap = laplace_ext(grid_field)
    core_part = grid_field[2:-2, 2:-2]
    return (
        quench_depth * core_part
        + core_part
        + 2.0 * first_lap[1:-1, 1:-1]
        + laplace_ext(first_lap)
        + core_part * core_part * core_part
    )


def central_ext(grid_field, dimension):
    if dimension == 0:
        return (grid_field[2:, 1:-1] - grid_field[:-2, 1:-1]) * 0.5
    if dimension == 1:
        return (grid_field[1:-1, 2:] - grid_field[1:-1, :-2]) * 0.5
    center = grid_field[1:-1, 1:-1]
    return (jnp.roll(center, -1, 2) - jnp.roll(center, 1, 2)) * 0.5


def coarse_mean(grid_field):
    size_x, size_y, extent_along_z = grid_field.shape
    return grid_field.reshape(size_x // 2, 2, size_y // 2, 2, extent_along_z // 2, 2).mean(
        axis=(1, 3, 5)
    )


def collide(populations, coarse_force):
    speeds, weights = lattice()
    speed_table = jnp.array(speeds, jnp.float32)
    weight_table = jnp.array(weights, jnp.float32)[:, None, None, None]
    fluid_mass = jnp.sum(populations, axis=0)
    moment = jnp.einsum("qc,qxzy->cxzy", speed_table, populations, precision=lax.Precision.HIGHEST)
    flow_velocity = (moment + 0.5 * coarse_force) / fluid_mass
    speed_square = (
        flow_velocity[0] * flow_velocity[0]
        + flow_velocity[1] * flow_velocity[1]
        + flow_velocity[2] * flow_velocity[2]
    )
    force_velocity = (
        flow_velocity[0] * coarse_force[0]
        + flow_velocity[1] * coarse_force[1]
        + flow_velocity[2] * coarse_force[2]
    )
    column_x = speed_table[:, 0][:, None, None, None]
    column_y = speed_table[:, 1][:, None, None, None]
    column_z = speed_table[:, 2][:, None, None, None]
    projected = (
        column_x * flow_velocity[0] + column_y * flow_velocity[1] + column_z * flow_velocity[2]
    )
    force_along = (
        column_x * coarse_force[0] + column_y * coarse_force[1] + column_z * coarse_force[2]
    )
    balance = (
        weight_table
        * fluid_mass
        * (1.0 + 3.0 * projected + 4.5 * projected * projected - 1.5 * speed_square)
    )
    source_gain = 1.0 - 0.5 / relax_time
    relaxed = (
        populations
        - (populations - balance) / relax_time
        + source_gain
        * weight_table
        * (3.0 * (force_along - force_velocity) + 9.0 * projected * force_along)
    )
    return (relaxed, flow_velocity)


def stream_full(relaxed):
    speeds, weights = lattice()
    count_x = relaxed.shape[1]
    count_z = relaxed.shape[2]
    extended = padded(relaxed, (("gx", 1), ("gy", 2)), 1)
    passed = []
    for member in range(len(speeds)):
        jump_x, jump_y, jump_z = speeds[member]
        piece_now = extended[
            member, 1 - jump_x : 1 - jump_x + count_x, 1 - jump_z : 1 - jump_z + count_z
        ]
        passed.append(jnp.roll(piece_now, jump_y, 2))
    return jnp.stack(passed)


def local(density, populations):
    size_x, size_y, extent_along_z = density.shape
    current = density
    fine_velocity = None
    populations_next = None
    for inner_substep in range(DENSITY_SUBSTEPS):
        extended = padded(current, (("gx", 0), ("gy", 1)), 3)
        potential = potential_ext(extended)
        nearby = extended[2:-2, 2:-2]
        interior = nearby[1:-1, 1:-1]
        if inner_substep == 0:
            pieces = []
            for dimension in range(3):
                pieces.append(
                    force_unit
                    * coarse_mean(-interior * central_ext(potential, dimension)).transpose(0, 2, 1)
                )
            coarse_force = lax.all_to_all(
                jnp.stack(pieces), "gy", split_axis=2, concat_axis=3, tiled=True
            )
            relaxed, flow_velocity = collide(populations, coarse_force)
            populations_next = stream_full(relaxed)
            returned = lax.all_to_all(
                speed_unit * flow_velocity, "gy", split_axis=3, concat_axis=2, tiled=True
            )
            returned = returned.transpose(0, 1, 3, 2)
            half_x, half_y, half_z = (returned.shape[1], returned.shape[2], returned.shape[3])
            fine_velocity = jnp.broadcast_to(
                returned[:, :, None, :, None, :, None], (3, half_x, 2, half_y, 2, half_z, 2)
            ).reshape(3, size_x, size_y, extent_along_z)
        advect = (
            fine_velocity[0] * central_ext(nearby, 0)
            + fine_velocity[1] * central_ext(nearby, 1)
            + fine_velocity[2] * central_ext(nearby, 2)
        )
        current = interior + coupled_time_step * (laplace_ext(potential) - advect)
    return (current, populations_next)


def solution(mesh):
    return jax.shard_map(
        local,
        mesh=mesh,
        in_specs=(P("gx", "gy", None), P(None, "gx", "gy", None)),
        out_specs=(P("gx", "gy", None), P(None, "gx", "gy", None)),
        check_vma=False,
    )
```

profile of v0, /device:TPU:0, one launch (start us, length us, event | category | flops | bytes accessed | tf_op | source)
XLA Modules:
  0.0 109.6 jit_solution(18116291648104101732)
XLA Ops:
  1.4 3.0 %collective-permute-start = (f32[3,16,128]{2,1,0:T(8,128)S(1)}, f32[3,16,128]{2,1,0:T(8,128)S(1)}, u32[]{:S(2)}, u32[]{:S(2)}) collective-permute-start(f32[3,16,128]{2,1,0:T(8,128)S(1)} %get-tuple-element.70), channel_id=1, source_target_pairs={{0,16},{16,0},{1,17},{17,1},{2,18},{18,2},{3,19},{19,3},{4,20},{20... | collective-permute-start | bytes 73736 | tf_op jit(solution)/shard_map/ppermute | solution.py:22
  4.5 1.2 %fusion = f32[3,4,4,128]{3,0,2,1:T(4,128)S(1)} fusion(f32[19,3,1,1]{0,1,3,2:T(4,128)} %constant.55, f32[19,4,4,128]{3,2,1,0:T(4,128)} %param.5), kind=kOutput, calls=%fused_computation.1 | convolution fusion | flops 1400832 | bytes 180452 | tf_op jit(solution)/shard_map/qc,qxzy->cxzy/dot_general | solution.py:98
  7.1 1.2 %collective-permute-done.1 = f32[3,16,128]{2,1,0:T(8,128)S(1)} collective-permute-done((f32[3,16,128]{2,1,0:T(8,128)S(1)}, f32[3,16,128]{2,1,0:T(8,128)S(1)}, u32[]{:S(2)}, u32[]{:S(2)}) %collective-permute-start.1) | collective-permute-done | bytes 24608 | tf_op jit(solution)/shard_map/ppermute | solution.py:25
  8.4 4.4 %collective-permute-start.3 = (f32[14,3,128]{2,1,0:T(4,128)S(1)}, f32[14,3,128]{2,1,0:T(4,128)S(1)}, u32[]{:S(2)}, u32[]{:S(2)}) collective-permute-start(f32[14,3,128]{2,1,0:T(4,128)S(1)} %get-tuple-element.57), channel_id=1, source_target_pairs={{1,0},{2,1},{3,2},{4,3},{5,4},{6,5},{7,6},{8,7},{9,8},{10,9},{11,1... | collective-permute-start | bytes 64520 | tf_op jit(solution)/shard_map/ppermute | solution.py:25
  12.8 1.0 fusion.81
  15.4 5.6 %reshape.50 = f32[4,2,8,2,64,2]{5,4,3,2,1,0:T(8,128)} reshape(f32[8,16,128]{2,1,0:T(8,128)S(1)} %get-tuple-element.24) | data formatting | bytes 131072 | tf_op jit(solution)/shard_map/reshape | solution.py:88
  21.0 5.5 %reshape.51 = f32[4,2,8,2,64,2]{5,4,3,2,1,0:T(8,128)} reshape(f32[8,16,128]{2,1,0:T(8,128)S(1)} %get-tuple-element.68) | data formatting | bytes 131072 | tf_op jit(solution)/shard_map/reshape | solution.py:88
  26.5 2.5 %reduce_sum.37 = f32[4,8,64]{2,1,0:T(8,128)S(1)} reduce(f32[4,2,8,2,64,2]{5,4,3,2,1,0:T(8,128)} %reshape.50, f32[]{:T(128)} %constant.9.clone.1), dimensions={1,3,5}, to_apply=%region_1.2 | reduce | flops 14336 | bytes 73732 | tf_op jit(solution)/shard_map/reduce_sum | solution.py:88
  29.1 2.5 %reduce_sum.38 = f32[4,8,64]{2,1,0:T(8,128)S(1)} reduce(f32[4,2,8,2,64,2]{5,4,3,2,1,0:T(8,128)} %reshape.51, f32[]{:T(128)} %constant.9.clone.1), dimensions={1,3,5}, to_apply=%region_2.3 | reduce | flops 14336 | bytes 73732 | tf_op jit(solution)/shard_map/reduce_sum | solution.py:88
  31.6 5.5 %reshape.49 = f32[4,2,8,2,64,2]{5,4,3,2,1,0:T(8,128)} reshape(f32[8,16,128]{2,1,0:T(8,128)S(1)} %get-tuple-element.23) | data formatting | bytes 131072 | tf_op jit(solution)/shard_map/reshape | solution.py:88
  37.2 2.6 %reduce_sum.36 = f32[4,8,64]{2,1,0:T(8,128)S(1)} reduce(f32[4,2,8,2,64,2]{5,4,3,2,1,0:T(8,128)} %reshape.49, f32[]{:T(128)} %constant.9.clone.1), dimensions={1,3,5}, to_apply=%region_0.1 | reduce | flops 14336 | bytes 73732 | tf_op jit(solution)/shard_map/reduce_sum | solution.py:88
  40.1 1.0 reshape.53
  41.1 5.8 %all-to-all-start = ((f32[16,1,384]{2,1,0:T(1,128)}), f32[16,1,384]{2,1,0:T(1,128)S(1)}, u32[]{:S(2)}, u32[]{:S(2)}) async-start(f32[16,1,384]{2,1,0:T(1,128)} %reshape.53), calls=%async_computation | async-start | bytes 49152 | tf_op jit(solution)/shard_map/all_to_all | solution.py:167
  47.0 6.4 %all-to-all-done = f32[16,1,384]{2,1,0:T(1,128)S(1)} async-done(((f32[16,1,384]{2,1,0:T(1,128)}), f32[16,1,384]{2,1,0:T(1,128)S(1)}, u32[]{:S(2)}, u32[]{:S(2)}) %all-to-all-start) | async-done | bytes 24608 | tf_op jit(solution)/shard_map/all_to_all | solution.py:167
  57.4 0.9 collective-permute-start.8
  58.3 1.2 %collective-permute-start.9 = (f32[19,1,4,128]{3,2,1,0:T(4,128)S(1)}, f32[19,1,4,128]{3,2,1,0:T(4,128)S(1)}, u32[]{:S(2)}, u32[]{:S(2)}) collective-permute-start(f32[19,1,4,128]{3,2,1,0:T(4,128)S(1)} %get-tuple-element.36), channel_id=1, source_target_pairs={{16,0},{0,16},{17,1},{1,17},{18,2},{2,18},{19,3},{3,19},{20,4},{4,... | collective-permute-start | bytes 116744 | tf_op jit(solution)/shard_map/ppermute | solution.py:25
  59.9 1.5 %reshape.55 = f32[16,1,384]{2,1,0:T(1,128)} reshape(f32[128,3,4,4]{3,2,1,0:T(4,128)S(1)} %bitcast.134) | data formatting | bytes 49152
  61.3 3.5 %all-to-all-start.1 = ((f32[16,1,384]{2,1,0:T(1,128)}), f32[16,1,384]{2,1,0:T(1,128)S(1)}, u32[]{:S(2)}, u32[]{:S(2)}) async-start(f32[16,1,384]{2,1,0:T(1,128)} %reshape.55), calls=%async_computation.1 | async-start | bytes 49152 | tf_op jit(solution)/shard_map/all_to_all | solution.py:172
  65.5 4.3 %collective-permute-start.11 = (f32[19,6,1,128]{3,2,1,0:T(1,128)S(1)}, f32[19,6,1,128]{3,2,1,0:T(1,128)S(1)}, u32[]{:S(2)}, u32[]{:S(2)}) collective-permute-start(f32[19,6,1,128]{3,2,1,0:T(1,128)S(1)} %get-tuple-element.13), channel_id=1, source_target_pairs={{1,0},{2,1},{3,2},{4,3},{5,4},{6,5},{7,6},{8,7},{9,8},{10,9},{11,1... | collective-permute-start | bytes 175112 | tf_op jit(solution)/shard_map/ppermute | solution.py:25
  69.9 1.7 %all-to-all-done.1 = f32[16,1,384]{2,1,0:T(1,128)S(1)} async-done(((f32[16,1,384]{2,1,0:T(1,128)}), f32[16,1,384]{2,1,0:T(1,128)S(1)}, u32[]{:S(2)}, u32[]{:S(2)}) %all-to-all-start.1) | async-done | bytes 24608 | tf_op jit(solution)/shard_map/all_to_all | solution.py:172
  72.3 1.0 reshape.56
  73.3 1.3 %copy.86 = f32[3,4,4,16,8]{4,3,2,1,0:T(8,128)S(1)} copy(f32[3,4,4,16,8]{2,1,0,4,3:T(4,128)S(1)} %bitcast.135) | data formatting | bytes 49152 | tf_op jit(solution)/shard_map/all_to_all | solution.py:172
  74.9 2.6 %broadcast_in_dim.21 = f32[4,2,8,2,64,2]{5,4,3,2,1,0:T(8,128)} broadcast(f32[4,8,64]{2,1,0:T(8,128)S(1)} %copy.74), dimensions={0,2,4} | broadcast | bytes 73728 | tf_op jit(solution)/shard_map/broadcast_in_dim | solution.py:177
  77.5 4.0 %broadcast_in_dim.22 = f32[8,16,128]{2,1,0:T(8,128)S(1)} reshape(f32[4,2,8,2,64,2]{5,4,3,2,1,0:T(8,128)} %broadcast_in_dim.21) | data formatting | bytes 131072 | tf_op jit(solution)/shard_map/broadcast_in_dim | solution.py:177
  81.6 2.6 %broadcast_in_dim.23 = f32[4,2,8,2,64,2]{5,4,3,2,1,0:T(8,128)} broadcast(f32[4,8,64]{2,1,0:T(8,128)S(1)} %copy.75), dimensions={0,2,4} | broadcast | bytes 73728 | tf_op jit(solution)/shard_map/broadcast_in_dim | solution.py:177
  84.1 4.0 %broadcast_in_dim.24 = f32[8,16,128]{2,1,0:T(8,128)S(1)} reshape(f32[4,2,8,2,64,2]{5,4,3,2,1,0:T(8,128)} %broadcast_in_dim.23) | data formatting | bytes 131072 | tf_op jit(solution)/shard_map/broadcast_in_dim | solution.py:177
  88.2 2.6 %broadcast_in_dim.25 = f32[4,2,8,2,64,2]{5,4,3,2,1,0:T(8,128)} broadcast(f32[4,8,64]{2,1,0:T(8,128)S(1)} %copy.76), dimensions={0,2,4} | broadcast | bytes 73728 | tf_op jit(solution)/shard_map/broadcast_in_dim | solution.py:177
  90.8 4.0 %broadcast_in_dim.26 = f32[8,16,128]{2,1,0:T(8,128)S(1)} reshape(f32[4,2,8,2,64,2]{5,4,3,2,1,0:T(8,128)} %broadcast_in_dim.25) | data formatting | bytes 131072 | tf_op jit(solution)/shard_map/broadcast_in_dim | solution.py:177
  95.9 1.2 %collective-permute-start.5 = (f32[3,16,128]{2,1,0:T(8,128)S(1)}, f32[3,16,128]{2,1,0:T(8,128)S(1)}, u32[]{:S(2)}, u32[]{:S(2)}) collective-permute-start(f32[3,16,128]{2,1,0:T(8,128)S(1)} %get-tuple-element.63), channel_id=1, source_target_pairs={{16,0},{0,16},{17,1},{1,17},{18,2},{2,18},{19,3},{3,19},{20,4},{4,... | collective-permute-start | bytes 73736 | tf_op jit(solution)/shard_map/ppermute | solution.py:25
  97.2 1.7 %collective-permute-done.4 = f32[3,16,128]{2,1,0:T(8,128)S(1)} collective-permute-done((f32[3,16,128]{2,1,0:T(8,128)S(1)}, f32[3,16,128]{2,1,0:T(8,128)S(1)}, u32[]{:S(2)}, u32[]{:S(2)}) %collective-permute-start.4) | collective-permute-done | bytes 24608 | tf_op jit(solution)/shard_map/ppermute | solution.py:22
  99.8 4.4 %collective-permute-start.7 = (f32[14,3,128]{2,1,0:T(4,128)S(1)}, f32[14,3,128]{2,1,0:T(4,128)S(1)}, u32[]{:S(2)}, u32[]{:S(2)}) collective-permute-start(f32[14,3,128]{2,1,0:T(4,128)S(1)} %get-tuple-element.54), channel_id=1, source_target_pairs={{1,0},{2,1},{3,2},{4,3},{5,4},{6,5},{7,6},{8,7},{9,8},{10,9},{11,1... | collective-permute-start | bytes 64520 | tf_op jit(solution)/shard_map/ppermute | solution.py:25
  104.3 1.5 %collective-permute-done.6 = f32[14,3,128]{2,1,0:T(4,128)S(1)} collective-permute-done((f32[14,3,128]{2,1,0:T(4,128)S(1)}, f32[14,3,128]{2,1,0:T(4,128)S(1)}, u32[]{:S(2)}, u32[]{:S(2)}) %collective-permute-start.6) | collective-permute-done | bytes 21536 | tf_op jit(solution)/shard_map/ppermute | solution.py:22
  (124 shorter events, 16.2 us)
Async XLA Ops:
  0.6 14.7 %copy-start = (f32[8,16,128]{2,1,0:T(8,128)S(1)}, f32[8,16,128]{2,1,0:T(8,128)}, u32[]{:S(2)}) copy-start(f32[8,16,128]{2,1,0:T(8,128)} %param.4) | copy-start | bytes 196612
  1.4 4.8 %collective-permute-start = (f32[3,16,128]{2,1,0:T(8,128)S(1)}, f32[3,16,128]{2,1,0:T(8,128)S(1)}, u32[]{:S(2)}, u32[]{:S(2)}) collective-permute-start(f32[3,16,128]{2,1,0:T(8,128)S(1)} %get-tuple-element.70), channel_id=1, source_target_pairs={{0,16},{16,0},{1,17},{17,1},{2,18},{18,2},{3,19},{19,3},{4,20},{20... | collective-permute-start | bytes 73736 | tf_op jit(solution)/shard_map/ppermute | solution.py:22
  4.4 3.8 %collective-permute-start.1 = (f32[3,16,128]{2,1,0:T(8,128)S(1)}, f32[3,16,128]{2,1,0:T(8,128)S(1)}, u32[]{:S(2)}, u32[]{:S(2)}) collective-permute-start(f32[3,16,128]{2,1,0:T(8,128)S(1)} %get-tuple-element.69), channel_id=1, source_target_pairs={{16,0},{0,16},{17,1},{1,17},{18,2},{2,18},{19,3},{3,19},{20,4},{4,... | collective-permute-start | bytes 73736 | tf_op jit(solution)/shard_map/ppermute | solution.py:25
  8.3 6.0 %collective-permute-start.2 = (f32[14,3,128]{2,1,0:T(4,128)S(1)}, f32[14,3,128]{2,1,0:T(4,128)S(1)}, u32[]{:S(2)}, u32[]{:S(2)}) collective-permute-start(f32[14,3,128]{2,1,0:T(4,128)S(1)} %get-tuple-element.56), channel_id=1, source_target_pairs={{0,1},{1,2},{2,3},{3,4},{4,5},{5,6},{6,7},{7,8},{8,9},{9,10},{10,1... | collective-permute-start | bytes 64520 | tf_op jit(solution)/shard_map/ppermute | solution.py:22
  8.4 6.0 %collective-permute-start.3 = (f32[14,3,128]{2,1,0:T(4,128)S(1)}, f32[14,3,128]{2,1,0:T(4,128)S(1)}, u32[]{:S(2)}, u32[]{:S(2)}) collective-permute-start(f32[14,3,128]{2,1,0:T(4,128)S(1)} %get-tuple-element.57), channel_id=1, source_target_pairs={{1,0},{2,1},{3,2},{4,3},{5,4},{6,5},{7,6},{8,7},{9,8},{10,9},{11,1... | collective-permute-start | bytes 64520 | tf_op jit(solution)/shard_map/ppermute | solution.py:25
  31.6 15.4 %copy-start.1 = (f32[19,4,4,128]{3,2,1,0:T(4,128)S(1)}, f32[19,4,4,128]{3,2,1,0:T(4,128)}, u32[]{:S(2)}) copy-start(f32[19,4,4,128]{3,2,1,0:T(4,128)} %param.5) | copy-start | bytes 466948
  37.2 19.8 %copy-start.2 = (f32[19]{0:T(128)S(1)}, f32[19]{0:T(128)}, u32[]{:S(2)}) copy-start(f32[19]{0:T(128)} %constant.46.clone) | copy-start | bytes 232
  37.2 19.8 %copy-start.3 = (f32[19]{0:T(128)S(1)}, f32[19]{0:T(128)}, u32[]{:S(2)}) copy-start(f32[19]{0:T(128)} %constant.49) | copy-start | bytes 232
  37.2 19.8 %copy-start.4 = (f32[19]{0:T(128)S(1)}, f32[19]{0:T(128)}, u32[]{:S(2)}) copy-start(f32[19]{0:T(128)} %constant.51) | copy-start | bytes 232
  37.2 19.8 %copy-start.5 = (f32[19]{0:T(128)S(1)}, f32[19]{0:T(128)}, u32[]{:S(2)}) copy-start(f32[19]{0:T(128)} %constant.53) | copy-start | bytes 232
  37.2 19.8 %copy-start.6 = (f32[19]{0:T(128)S(1)}, f32[19]{0:T(128)}, u32[]{:S(2)}) copy-start(f32[19]{0:T(128)} %constant.54) | copy-start | bytes 232
  41.1 12.4 %all-to-all-start = ((f32[16,1,384]{2,1,0:T(1,128)}), f32[16,1,384]{2,1,0:T(1,128)S(1)}, u32[]{:S(2)}, u32[]{:S(2)}) async-start(f32[16,1,384]{2,1,0:T(1,128)} %reshape.53), calls=%async_computation | async-start | bytes 49152 | tf_op jit(solution)/shard_map/all_to_all | solution.py:167
  57.4 7.4 %collective-permute-start.8 = (f32[19,1,4,128]{3,2,1,0:T(4,128)S(1)}, f32[19,1,4,128]{3,2,1,0:T(4,128)S(1)}, u32[]{:S(2)}, u32[]{:S(2)}) collective-permute-start(f32[19,1,4,128]{3,2,1,0:T(4,128)S(1)} %get-tuple-element.37), channel_id=1, source_target_pairs={{0,16},{16,0},{1,17},{17,1},{2,18},{18,2},{3,19},{19,3},{4,20},{20... | collective-permute-start | bytes 116744 | tf_op jit(solution)/shard_map/ppermute | solution.py:22
  58.3 6.5 %collective-permute-start.9 = (f32[19,1,4,128]{3,2,1,0:T(4,128)S(1)}, f32[19,1,4,128]{3,2,1,0:T(4,128)S(1)}, u32[]{:S(2)}, u32[]{:S(2)}) collective-permute-start(f32[19,1,4,128]{3,2,1,0:T(4,128)S(1)} %get-tuple-element.36), channel_id=1, source_target_pairs={{16,0},{0,16},{17,1},{1,17},{18,2},{2,18},{19,3},{3,19},{20,4},{4,... | collective-permute-start | bytes 116744 | tf_op jit(solution)/shard_map/ppermute | solution.py:25
  61.3 10.2 %all-to-all-start.1 = ((f32[16,1,384]{2,1,0:T(1,128)}), f32[16,1,384]{2,1,0:T(1,128)S(1)}, u32[]{:S(2)}, u32[]{:S(2)}) async-start(f32[16,1,384]{2,1,0:T(1,128)} %reshape.55), calls=%async_computation.1 | async-start | bytes 49152 | tf_op jit(solution)/shard_map/all_to_all | solution.py:172
  65.1 42.4 %collective-permute-start.10 = (f32[19,6,1,128]{3,2,1,0:T(1,128)S(1)}, f32[19,6,1,128]{3,2,1,0:T(1,128)S(1)}, u32[]{:S(2)}, u32[]{:S(2)}) collective-permute-start(f32[19,6,1,128]{3,2,1,0:T(1,128)S(1)} %get-tuple-element.14), channel_id=1, source_target_pairs={{0,1},{1,2},{2,3},{3,4},{4,5},{5,6},{6,7},{7,8},{8,9},{9,10},{10,1... | collective-permute-start | bytes 175112 | tf_op jit(solution)/shard_map/ppermute | solution.py:22
  65.5 42.1 %collective-permute-start.11 = (f32[19,6,1,128]{3,2,1,0:T(1,128)S(1)}, f32[19,6,1,128]{3,2,1,0:T(1,128)S(1)}, u32[]{:S(2)}, u32[]{:S(2)}) collective-permute-start(f32[19,6,1,128]{3,2,1,0:T(1,128)S(1)} %get-tuple-element.13), channel_id=1, source_target_pairs={{1,0},{2,1},{3,2},{4,3},{5,4},{6,5},{7,6},{8,7},{9,8},{10,9},{11,1... | collective-permute-start | bytes 175112 | tf_op jit(solution)/shard_map/ppermute | solution.py:25
  95.0 3.9 %collective-permute-start.4 = (f32[3,16,128]{2,1,0:T(8,128)S(1)}, f32[3,16,128]{2,1,0:T(8,128)S(1)}, u32[]{:S(2)}, u32[]{:S(2)}) collective-permute-start(f32[3,16,128]{2,1,0:T(8,128)S(1)} %get-tuple-element.62), channel_id=1, source_target_pairs={{0,16},{16,0},{1,17},{17,1},{2,18},{18,2},{3,19},{19,3},{4,20},{20... | collective-permute-start | bytes 73736 | tf_op jit(solution)/shard_map/ppermute | solution.py:22
  95.9 3.8 %collective-permute-start.5 = (f32[3,16,128]{2,1,0:T(8,128)S(1)}, f32[3,16,128]{2,1,0:T(8,128)S(1)}, u32[]{:S(2)}, u32[]{:S(2)}) collective-permute-start(f32[3,16,128]{2,1,0:T(8,128)S(1)} %get-tuple-element.63), channel_id=1, source_target_pairs={{16,0},{0,16},{17,1},{1,17},{18,2},{2,18},{19,3},{3,19},{20,4},{4,... | collective-permute-start | bytes 73736 | tf_op jit(solution)/shard_map/ppermute | solution.py:25
  99.8 6.0 %collective-permute-start.6 = (f32[14,3,128]{2,1,0:T(4,128)S(1)}, f32[14,3,128]{2,1,0:T(4,128)S(1)}, u32[]{:S(2)}, u32[]{:S(2)}) collective-permute-start(f32[14,3,128]{2,1,0:T(4,128)S(1)} %get-tuple-element.55), channel_id=1, source_target_pairs={{0,1},{1,2},{2,3},{3,4},{4,5},{5,6},{6,7},{7,8},{8,9},{9,10},{10,1... | collective-permute-start | bytes 64520 | tf_op jit(solution)/shard_map/ppermute | solution.py:22
  99.8 6.0 %collective-permute-start.7 = (f32[14,3,128]{2,1,0:T(4,128)S(1)}, f32[14,3,128]{2,1,0:T(4,128)S(1)}, u32[]{:S(2)}, u32[]{:S(2)}) collective-permute-start(f32[14,3,128]{2,1,0:T(4,128)S(1)} %get-tuple-element.54), channel_id=1, source_target_pairs={{1,0},{2,1},{3,2},{4,3},{5,4},{6,5},{7,6},{8,7},{9,8},{10,9},{11,1... | collective-permute-start | bytes 64520 | tf_op jit(solution)/shard_map/ppermute | solution.py:25
  108.9 0.7 copy-start.7
where the time goes:
time: 110 us
  local copies, waits for them, and re-layouts  50.3 us (46%)
  starting transfers between devices  30.1 us (27%)
  waiting for transfers between devices  14.5 us (13%)
  other arithmetic  12.3 us (11%)
  matrix products  1.18 us (1%)
  between operations  1.14 us (1%)
    broadcast_in_dim x6, local copies, waits for them, and re-layouts, local(): jnp.broadcast_to(returned[:, :, None, :, None, :, None], (3, half_x, 2, h...  19.7 us
    reshape x3, local copies, waits for them, and re-layouts, coarse_mean(): grid_field.reshape(size_x // 2, 2, size_y // 2, 2, extent_along_z // 2, 2)  16.7 us
    ppermute x6, starting transfers between devices, padded(): lax.ppermute(lax.slice_in_dim(block, 0, width, axis=dim), axis, backward)  15.5 us
    reduce_sum x3, other arithmetic, coarse_mean(): grid_field.reshape(size_x // 2, 2, size_y // 2, 2, extent_along_z // 2, 2)  7.69 us
    all_to_all x1, waiting for transfers between devices, local(): lax.all_to_all(jnp.stack(pieces), 'gy', split_axis=2, concat_axis=3, tile...  6.44 us
    all_to_all x1, starting transfers between devices, local(): lax.all_to_all(jnp.stack(pieces), 'gy', split_axis=2, concat_axis=3, tile...  5.81 us
    unnamed x23, local copies, waits for them, and re-layouts  5.56 us
    ppermute x6, starting transfers between devices, padded(): lax.ppermute(lax.slice_in_dim(block, block.shape[dim] - width, None, axis...  5.3 us
  transfers between devices with their start and end apart: 14, of which 8 were waited for; matrix products, arithmetic and copies ran while one was open for 28% of the time, Pallas kernels for 0%

commit v1 on v0

v1 whole, which is shorter than its diff:
```python
import functools

import jax
import jax.numpy as jnp
from jax import lax
from jax.experimental import pallas as pl
from jax.experimental.pallas import tpu as pltpu
from jax.sharding import PartitionSpec as P

DENSITY_SUBSTEPS = 2

coupled_time_step = 0.0008
force_unit = 0.005
speed_unit = 2000.0
relax_time = 0.8
quench_depth = -0.25

LANES = 128
ROWS = 8
WINDOW_HALO = 5
WINDOW_ROWS = 24

SPEEDS = (
    (0, 0, 0),
    (1, 0, 0),
    (-1, 0, 0),
    (0, 1, 0),
    (0, -1, 0),
    (0, 0, 1),
    (0, 0, -1),
    (1, 1, 0),
    (-1, -1, 0),
    (1, -1, 0),
    (-1, 1, 0),
    (1, 0, 1),
    (-1, 0, -1),
    (1, 0, -1),
    (-1, 0, 1),
    (0, 1, 1),
    (0, -1, -1),
    (0, 1, -1),
    (0, -1, 1),
)
WEIGHTS = (1.0 / 3.0,) + (1.0 / 18.0,) * 6 + (1.0 / 36.0,) * 12
MOMENTS = 4


def moving(jump_x=None, jump_z=None):
    return [
        q
        for q, (cx, _, cz) in enumerate(SPEEDS)
        if (jump_x is None or cx == jump_x) and (jump_z is None or cz == jump_z)
    ]


class Plan:
    def __init__(self, count_x, count_y, density, populations):
        self.gx, self.gy = count_x, count_y
        self.x, self.y, self.z = density.shape
        _, self.xc, self.zc, self.yc = populations.shape
        self.yb = self.y // 2
        self.zf = 2 * self.zc
        self.window = self.zf + 2 * WINDOW_HALO
        self.half = self.zc // 2
        self.rows = WINDOW_ROWS
        self.pair = count_x == 2
        self.blocks = 2 if self.pair else 3
        self.planes = self.yc // LANES
        self.layers = self.blocks * self.x
        self.coarse_layers = self.blocks * self.xc
        assert self.x * self.y == LANES and MOMENTS * self.xc * self.yb == LANES
        assert self.z == LANES and self.yc % LANES == 0 and self.zc % 2 == 0
        assert self.window + self.zc + self.half <= WINDOW_ROWS and self.zc + 2 <= ROWS
        wide = self.planes
        self.rows_x = self.x * self.y + 2 * 9 * self.zc * wide
        self.rows_y = self.x * ROWS + 9 * self.xc * wide
        self.rows_d = self.x * ROWS + 2 * 5 * wide

    def layer(self, x):
        return x % self.layers if self.pair else x + self.x

    def coarse_layer(self, x):
        return x % self.coarse_layers if self.pair else x + self.xc

    def span(self, low, high):
        seen = {}
        for x in range(low, high):
            seen.setdefault(self.layer(x), x)
        return list(seen.values())


def butterfly(arrays, granule):
    count = LANES // granule
    lane = lax.broadcasted_iota(jnp.int32, arrays[0].shape, 1) // granule
    bit = 1
    while bit < count:
        upper = (lane & bit) != 0
        turned = list(arrays)
        for a in range(count):
            if a & bit:
                continue
            low, high = arrays[a], arrays[a | bit]
            turned[a] = jnp.where(upper, pltpu.roll(high, bit * granule, 1), low)
            turned[a | bit] = jnp.where(upper, high, pltpu.roll(low, LANES - bit * granule, 1))
        arrays = turned
        bit *= 2
    return arrays


def roll(value, shift, dimension):
    size = value.shape[dimension]
    return pltpu.roll(value, shift % size, dimension)


def moments_of(members):
    total = functools.reduce(lambda a, b: a + b, members)
    out = [total]
    for axis in range(3):
        plus = [members[q] for q, c in enumerate(SPEEDS) if c[axis] == 1]
        minus = [members[q] for q, c in enumerate(SPEEDS) if c[axis] == -1]
        out.append(
            functools.reduce(lambda a, b: a + b, plus) - functools.reduce(lambda a, b: a + b, minus)
        )
    return out


def put(buffer, at, value):
    rows, width = value.shape
    for plane in range(width // LANES):
        buffer[at : at + rows, :] = value[:, plane * LANES : (plane + 1) * LANES]
        at += rows
    return at


def take(buffer, at, rows, planes):
    parts = [buffer[at + k * rows : at + (k + 1) * rows, :] for k in range(planes)]
    return parts[0] if planes == 1 else jnp.concatenate(parts, axis=1)


def pack_kernel(plan, density, populations, send, moments, window):
    rows = []
    for x in range(plan.x):
        for parity in range(2):
            rows.append(density[x, pl.ds(parity, plan.yb, stride=2), :])
    turned = jnp.concatenate(rows, axis=0).T
    halo = WINDOW_HALO
    window[halo : halo + plan.z, :] = turned
    window[0:halo, :] = turned[plan.z - halo :, :]
    window[halo + plan.z : 2 * halo + plan.z, :] = turned[:halo, :]
    copies = plan.gx if plan.pair else 1
    for target in range(plan.gy):
        piece = window[plan.zf * target : plan.zf * target + plan.window, :]
        for copy in range(copies):
            send[copy, target, 0 : plan.window, :] = piece
    fields = [[None] * plan.xc for _ in range(MOMENTS)]
    for x in range(plan.xc):
        for f, value in enumerate(moments_of([populations[q, x] for q in range(len(SPEEDS))])):
            fields[f][x] = value
            moments[f, x] = value
    pieces = []
    for plane in range(plan.planes):
        span = slice(plane * LANES, (plane + 1) * LANES)
        pieces += butterfly([value[:, span] for row in fields for value in row], plan.yb)
    y = lax.broadcasted_iota(jnp.int32, (plan.half, LANES), 1) % plan.yb
    y_all = lax.broadcasted_iota(jnp.int32, (plan.zc, LANES), 1) % plan.yb
    for target in range(plan.gy):
        before, after = pieces[(target - 1) % plan.gy], pieces[(target + 1) % plan.gy]
        beside = jnp.where(y_all >= plan.yb // 2, before, after)
        first, second = beside[: plan.half], beside[plan.half :]
        packed = jnp.where(
            (y < 2) | (y >= plan.yb - 2),
            first,
            jnp.where(y < 4, roll(second, 2, 1), roll(second, -2, 1)),
        )
        at = plan.window
        for copy in range(copies):
            send[copy, target, at : at + plan.zc, :] = pieces[target]
            send[copy, target, at + plan.zc : at + plan.zc + plan.half, :] = packed
            left = plan.rows - (at + plan.zc + plan.half)
            if left:
                send[copy, target, plan.rows - left :, :] = jnp.zeros((left, LANES), jnp.float32)


def edge_kernel(plan, density, populations, moments, to_x, up, down, up_x, down_x):
    for x in range(plan.x):
        to_x[x * plan.y : (x + 1) * plan.y, :] = density[x]
        for buffer in (up, up_x):
            buffer[x * ROWS : (x + 1) * ROWS, :] = density[x, plan.y - ROWS :, :]
        for buffer in (down, down_x):
            buffer[x * ROWS : (x + 1) * ROWS, :] = density[x, :ROWS, :]
    at = plan.x * plan.y
    for x, jump in ((plan.xc - 1, 1), (0, -1)):
        for f in range(MOMENTS):
            at = put(to_x, at, moments[f, x])
        for q in moving(jump_x=jump):
            at = put(to_x, at, populations[q, x])
    for buffer, z, jump in ((up, plan.zc - 1, 1), (down, 0, -1)):
        at = plan.x * ROWS
        for x in range(plan.xc):
            for f in range(MOMENTS):
                at = put(buffer, at, moments[f, x, z : z + 1])
            for q in moving(jump_z=jump):
                at = put(buffer, at, populations[q, x, z : z + 1])
    for buffer, z, jump in ((up_x, plan.zc - 1, 1), (down_x, 0, -1)):
        at = plan.x * ROWS
        for x, jump_x in ((plan.xc - 1, 1), (0, -1)):
            for f in range(MOMENTS):
                at = put(buffer, at, moments[f, x, z : z + 1])
            for q in moving(jump_x=jump_x, jump_z=jump):
                at = put(buffer, at, populations[q, x, z : z + 1])


def solvent_part(plan, place, received, populations, moments, halo, out, work):
    grid, lap, pot, pooled, field, member = work
    from_low, from_high, from_below, from_above, below_low, below_high, above_low, above_high = halo
    width = plan.planes
    for block in range(plan.blocks):
        for plane in range(width):
            for tile in range(WINDOW_ROWS // ROWS):
                rows = slice(tile * ROWS, (tile + 1) * ROWS)
                senders = LANES // plan.yb
                arrays = [
                    received[place(block), plane * senders + t, rows, :] for t in range(senders)
                ]
                for g, value in enumerate(butterfly(arrays, plan.yb)):
                    grid[block * plan.x + g // 2, g % 2, rows, plane * LANES : (plane + 1) * LANES] = value

    def laplace(source, x):
        here, low, high = plan.layer(x), plan.layer(x - 1), plan.layer(x + 1)
        even, odd = source[here, 0], source[here, 1]
        sides = ((odd, roll(odd, 1, 1)), (even, roll(even, -1, 1)))
        out = []
        for parity, value in enumerate((even, odd)):
            running = -6.0 * value + source[low, parity] + source[high, parity]
            running = running + sides[parity][0] + sides[parity][1]
            out.append(running + roll(value, 1, 0) + roll(value, -1, 0))
        return out

    for x in plan.span(-4, plan.x + 4):
        for parity, value in enumerate(laplace(grid, x)):
            lap[plan.layer(x), parity] = value
    for x in plan.span(-3, plan.x + 3):
        for parity, second in enumerate(laplace(lap, x)):
            here = plan.layer(x)
            value = grid[here, parity]
            pot[here, parity] = (
                (quench_depth + 1.0) * value + 2.0 * lap[here, parity] + second + value * value * value
            )
    for coarse in range(-1, plan.xc + 1):
        total = None
        for x in (2 * coarse, 2 * coarse + 1):
            here, low, high = plan.layer(x), plan.layer(x - 1), plan.layer(x + 1)
            even, odd = grid[here, 0], grid[here, 1]
            pot_even, pot_odd = pot[here, 0], pot[here, 1]
            along_x = even * (pot[high, 0] - pot[low, 0]) + odd * (pot[high, 1] - pot[low, 1])
            along_y = even * (pot_odd - roll(pot_odd, 1, 1)) + odd * (roll(pot_even, -1, 1) - pot_even)
            along_z = even * (roll(pot_even, -1, 0) - roll(pot_even, 1, 0)) + odd * (
                roll(pot_odd, -1, 0) - roll(pot_odd, 1, 0)
            )
            now = (along_x, along_y, along_z)
            total = now if total is None else tuple(a + b for a, b in zip(total, now))
        for c in range(3):
            for plane in range(width):
                pooled[c, plane, coarse + 1] = total[c][:, plane * LANES : (plane + 1) * LANES]

    def store(target, lead, value_own, value_below, value_above):
        if value_own is not None:
            target[lead + (slice(0, plan.zc),)] = value_own
        if value_below is not None:
            target[lead + (slice(ROWS - 1, ROWS),)] = value_below
        if value_above is not None:
            target[lead + (slice(plan.zc, plan.zc + 1),)] = value_above

    for x in range(plan.xc):
        at = plan.x * ROWS + x * 9 * width
        for f in range(MOMENTS):
            store(
                field,
                (f, x + 1),
                moments[f, x],
                take(from_below, at, 1, width),
                take(from_above, at, 1, width),
            )
            at += width
        at_plus = at_minus = at
        for q, (_, _, jump_z) in enumerate(SPEEDS):
            below = above = None
            if jump_z == 1:
                below = take(from_below, at_plus, 1, width)
                at_plus += width
            if jump_z == -1:
                above = take(from_above, at_minus, 1, width)
                at_minus += width
            store(member, (q, x + 1), populations[q, x], below, above)
    for slot, block, first, low, high, jump in (
        (0, from_low, True, below_low, above_low, 1),
        (plan.xc + 1, from_high, False, below_high, above_high, -1),
    ):
        at = plan.x * plan.y + (0 if first else 9 * plan.zc * width)
        corner = plan.x * ROWS + (0 if first else 5 * width)
        for f in range(MOMENTS):
            store(
                field,
                (f, slot),
                take(block, at, plan.zc, width),
                take(low, corner, 1, width),
                take(high, corner, 1, width),
            )
            at += plan.zc * width
            corner += width
        for q in moving(jump_x=jump):
            jump_z = SPEEDS[q][2]
            store(
                member,
                (q, slot),
                take(block, at, plan.zc, width),
                take(low, corner, 1, width) if jump_z == 1 else None,
                take(high, corner, 1, width) if jump_z == -1 else None,
            )
            at += plan.zc * width

    start = WINDOW_HALO - 2
    for slot in range(plan.xc + 2):
        x = slot - 1
        force = []
        for c in range(3):
            both = jnp.concatenate(
                [
                    pooled[c, plane, slot, pl.ds(start, ROWS, stride=2), :]
                    + pooled[c, plane, slot, pl.ds(start + 1, ROWS, stride=2), :]
                    for plane in range(width)
                ],
                axis=1,
            )
            force.append(roll(both * (-0.5 * force_unit / 8.0), -1, 0))
        mass = field[0, slot]
        inverse = 1.0 / mass
        speed = [(field[c + 1, slot] + 0.5 * force[c]) * inverse for c in range(3)]
        square = speed[0] * speed[0] + speed[1] * speed[1] + speed[2] * speed[2]
        work_rate = speed[0] * force[0] + speed[1] * force[1] + speed[2] * force[2]
        rate = 1.0 / relax_time
        gain = 1.0 - 0.5 / relax_time
        base = mass * (rate - 1.5 * rate * square) - (3.0 * gain) * work_rate

        def emit(q, even, odd):
            jump_x, jump_y, jump_z = SPEEDS[q]
            target = x + jump_x
            if not 0 <= target < plan.xc:
                return
            value = member[q, slot] * (1.0 - rate) + WEIGHTS[q] * (even if odd is None else even + odd)
            if jump_z:
                value = roll(value, jump_z, 0)
            value = value[: plan.zc]
            if jump_y:
                value = roll(value, jump_y, 1)
            out[q, target] = value

        emit(0, base, None)
        for q in range(1, len(SPEEDS), 2):
            projected = along = None
            for c in range(3):
                if SPEEDS[q][c]:
                    s, g = SPEEDS[q][c] * speed[c], SPEEDS[q][c] * force[c]
                    projected = s if projected is None else projected + s
                    along = g if along is None else along + g
            even = base + (4.5 * rate) * mass * projected * projected + (9.0 * gain) * projected * along
            odd = (3.0 * rate) * mass * projected + (3.0 * gain) * along
            emit(q, even, odd)
            emit(q + 1, even, -odd)


def density_part(plan, place, received, density, halo, out, work):
    grid, lap, pot, flow, column, beside = work
    from_low, from_high, from_below, from_above, below_low, below_high, above_low, above_high = halo
    sets = [(0, None, from_below, from_above)]
    if plan.pair:
        sets.append((plan.x, from_low, below_low, above_low))
    else:
        sets.append((-plan.x, from_low, below_low, above_low))
        sets.append((plan.x, from_high, below_high, above_high))
    for first, block, below, above in sets:
        for x in range(plan.x):
            here = plan.layer(first + x)
            grid[here, ROWS : ROWS + plan.y] = (
                density[x] if block is None else block[x * plan.y : (x + 1) * plan.y, :]
            )
            grid[here, :ROWS] = below[x * ROWS : (x + 1) * ROWS, :]
            grid[here, ROWS + plan.y :] = above[x * ROWS : (x + 1) * ROWS, :]

    def spread(source, period, offset):
        count = source.shape[0]
        row = lax.broadcasted_iota(jnp.int32, (count, plan.z), 0)
        cell = lax.broadcasted_iota(jnp.int32, (count, plan.z), 1) // 2
        chosen = (row // period) * plan.zc + row % period + offset == cell
        return lax.dot_general(
            source.T,
            chosen.astype(jnp.float32),
            (((1,), (0,)), ((), ())),
            precision=lax.Precision.HIGHEST,
            preferred_element_type=jnp.float32,
        )

    for block in range(plan.blocks):
        at = plan.window
        for j in range(plan.gy):
            column[j * plan.zc : (j + 1) * plan.zc, :] = received[place(block), j, at : at + plan.zc, :]
            beside[j * plan.half : (j + 1) * plan.half, :] = received[
                place(block), j, at + plan.zc : at + plan.zc + plan.half, :
            ]
        own = spread(column[...], plan.zc, 0)
        first = spread(beside[...], plan.half, 0)
        second = spread(beside[...], plan.half, plan.half)
        yb = plan.yb
        for f in range(MOMENTS):
            for x in range(plan.xc):
                at = (f * plan.xc + x) * yb
                lead = (f, block * plan.xc + x)
                after = first[at : at + 2] + second[at + 2 : at + 4]
                before = first[at + yb - 2 : at + yb] + second[at + yb - 4 : at + yb - 2]
                for parity in range(2):
                    flow[lead + (pl.ds(ROWS + parity, yb, stride=2),)] = own[at : at + yb]
                    flow[lead + (pl.ds(ROWS + plan.y + parity, 2, stride=2),)] = after
                    flow[lead + (pl.ds(ROWS - 4 + parity, 2, stride=2),)] = before

    def laplace(source, x):
        value = source[plan.layer(x)]
        running = -6.0 * value + source[plan.layer(x - 1)] + source[plan.layer(x + 1)]
        running = running + roll(value, 1, 0) + roll(value, -1, 0)
        return running + roll(value, 1, 1) + roll(value, -1, 1)

    def potential(reach):
        for x in plan.span(-reach, plan.x + reach):
            lap[plan.layer(x)] = laplace(grid, x)
        for x in plan.span(1 - reach, plan.x + reach - 1):
            here = plan.layer(x)
            value = grid[here]
            pot[here] = (
                (quench_depth + 1.0) * value + 2.0 * lap[here] + laplace(lap, x) + value * value * value
            )

    def central(source, x, c):
        if c == 0:
            return source[plan.layer(x + 1)] - source[plan.layer(x - 1)]
        value = source[plan.layer(x)]
        return roll(value, -1, c - 1) - roll(value, 1, c - 1)

    shape = grid.shape[1:]
    odd = [(lax.broadcasted_iota(jnp.int32, shape, c) & 1) != 0 for c in range(2)]

    potential(6)
    seen = set()
    for coarse in range(-2, plan.xc + 2):
        slot = plan.coarse_layer(coarse)
        if slot in seen:
            continue
        seen.add(slot)
        inverse = (0.5 * speed_unit) / flow[0, slot]
        for c in range(3):
            total = None
            for x in (2 * coarse, 2 * coarse + 1):
                now = grid[plan.layer(x)] * central(pot, x, c)
                total = now if total is None else total + now
            for dimension in range(2):
                total = total + jnp.where(
                    odd[dimension], roll(total, 1, dimension), roll(total, -1, dimension)
                )
            flow[c + 1, slot] = (flow[c + 1, slot] + total * (-0.25 * force_unit / 8.0)) * inverse

    def advance(x):
        slot = plan.coarse_layer(x // 2)
        change = laplace(pot, x)
        for c in range(3):
            change = change - flow[c + 1, slot] * central(grid, x, c)
        return grid[plan.layer(x)] + coupled_time_step * change

    reach = 3 * (DENSITY_SUBSTEPS - 1)
    for inner_substep in range(DENSITY_SUBSTEPS):
        if inner_substep:
            potential(reach + 2)
        if reach == 0:
            for x in range(plan.x):
                out[x] = advance(x)[ROWS : ROWS + plan.y]
        else:
            moved = {}
            for x in plan.span(-reach, plan.x + reach):
                lap[plan.layer(x)] = advance(x)
                moved[plan.layer(x)] = None
            for here in moved:
                grid[here] = lap[here]
            reach -= 3


def update_kernel(plan, index, density, populations, moments, received, *rest):
    neighbours = 5 if plan.pair else 8
    buffers, rest = rest[:neighbours], rest[neighbours:]
    (density_next, populations_next), work = rest[:2], rest[2:]
    if plan.pair:
        other, below, above, below_x, above_x = buffers
        halo = (other, other, below, above, below_x, below_x, above_x, above_x)
    else:
        halo = buffers
    mine = index[0]

    def place(block):
        if not plan.pair:
            return block
        return mine if block == 0 else 1 - mine

    solvent_part(plan, place, received, populations, moments, halo, populations_next, work[:6])
    density_part(plan, place, received, density, halo, density_next, work[6:])


def call(kernel, outputs, scratch, arguments, smem=0):
    return pl.pallas_call(
        kernel,
        out_shape=[jax.ShapeDtypeStruct(shape, jnp.float32) for shape in outputs],
        in_specs=[pl.BlockSpec(memory_space=pltpu.SMEM)] * smem
        + [pl.BlockSpec(memory_space=pltpu.VMEM)] * (len(arguments) - smem),
        out_specs=[pl.BlockSpec(memory_space=pltpu.VMEM)] * len(outputs),
        scratch_shapes=[pltpu.VMEM(shape, jnp.float32) for shape in scratch],
        compiler_params=pltpu.CompilerParams(vmem_limit_bytes=16 * 1024 * 1024),
    )(*arguments)


def exchange(plan, send, to_x, up, down, up_x, down_x):
    everywhere = ("gx", "gy")

    def shifted(value, step_x, step_y):
        pairs = [
            (a * plan.gy + b, ((a + step_x) % plan.gx) * plan.gy + (b + step_y) % plan.gy)
            for a in range(plan.gx)
            for b in range(plan.gy)
        ]
        return lax.ppermute(value, everywhere, pairs)

    if plan.pair:
        whole = lax.all_to_all(
            send.reshape(plan.gx * plan.gy, plan.rows, LANES), everywhere, 0, 0, tiled=True
        )
        received = whole.reshape(plan.gx, plan.gy, plan.rows, LANES)
        halo = (
            shifted(to_x, 1, 0),
            shifted(up, 0, 1),
            shifted(down, 0, -1),
            shifted(up_x, 1, 1),
            shifted(down_x, 1, -1),
        )
        return received, halo
    send = send[0]
    three = jnp.stack([shifted(send, 1, 0), send, shifted(send, -1, 0)], axis=1)
    three = lax.all_to_all(three, "gy", 0, 0, tiled=True)
    halo = (
        shifted(to_x, 1, 0),
        shifted(to_x, -1, 0),
        shifted(up, 0, 1),
        shifted(down, 0, -1),
        shifted(up_x, 1, 1),
        shifted(up_x, -1, 1),
        shifted(down_x, 1, -1),
        shifted(down_x, -1, -1),
    )
    return three.transpose(1, 0, 2, 3), halo


def local(density, populations):
    plan = Plan(lax.axis_size("gx"), lax.axis_size("gy"), density, populations)
    copies = plan.gx if plan.pair else 1
    send, moments = call(
        functools.partial(pack_kernel, plan),
        [
            (copies, plan.gy, plan.rows, LANES),
            (MOMENTS, plan.xc, plan.zc, plan.yc),
        ],
        [(plan.z + 2 * ROWS, LANES)],
        [density, populations],
    )
    edges = call(
        functools.partial(edge_kernel, plan),
        [(plan.rows_x, LANES)] + [(plan.rows_y, LANES)] * 2 + [(plan.rows_d, LANES)] * 2,
        [],
        [density, populations, moments],
    )
    received, halo = exchange(plan, send, *edges)
    index = lax.axis_index("gx").reshape(1).astype(jnp.int32)
    arguments = [index, density, populations, moments, received, *halo]
    side = (plan.layers, 2, WINDOW_ROWS, plan.yc)
    tall = (plan.layers, plan.y + 2 * ROWS, plan.z)
    return call(
        functools.partial(update_kernel, plan),
        [density.shape, populations.shape],
        [
            side,
            side,
            side,
            (3, plan.planes, plan.xc + 2, WINDOW_ROWS, LANES),
            (MOMENTS, plan.xc + 2, ROWS, plan.yc),
            (len(SPEEDS), plan.xc + 2, ROWS, plan.yc),
            tall,
            tall,
            tall,
            (MOMENTS, plan.coarse_layers, plan.y + 2 * ROWS, plan.z),
            (plan.zc * plan.gy, LANES),
            (plan.half * plan.gy, LANES),
        ],
        arguments,
        smem=1,
    )


def solution(mesh):
    return jax.shard_map(
        lambda density, populations: tuple(local(density, populations)),
        mesh=mesh,
        in_specs=(P("gx", "gy", None), P(None, "gx", "gy", None)),
        out_specs=(P("gx", "gy", None), P(None, "gx", "gy", None)),
        check_vma=False,
    )
```

time: 110 us -> 29.4 us (0.27)
  local copies, waits for them, and re-layouts: 50.3 us -> 1.75 us
  waiting for transfers between devices: 14.5 us -> 2.19 us
  other arithmetic: 12.3 us -> 0 us
  starting transfers between devices: 30.1 us -> 18.9 us
  Pallas kernels: 0 us -> 5.56 us
  matrix products: 1.18 us -> 0 us
    broadcast_in_dim x6 -> x0, local copies, waits for them, and re-layouts: 19.7 us -> none  [local(): jnp.broadcast_to(returned[:, :, None, :, None, :, None], (3, half_x, 2, h...]
    reshape x3 -> x0, local copies, waits for them, and re-layouts: 16.7 us -> none  [coarse_mean(): grid_field.reshape(size_x // 2, 2, size_y // 2, 2, extent_along_z // 2, 2)]
    ppermute x12 -> x5, starting transfers between devices: 20.8 us -> 11.6 us  [shifted(): return lax.ppermute(value, everywhere, pairs)]
    all_to_all x2 -> x1, waiting for transfers between devices: 8.09 us -> 0.01 us  [exchange(): lax.all_to_all(send.reshape(plan.gx * plan.gy, plan.rows, LANES), everywh...]
    reduce_sum x4 -> x0, other arithmetic: 7.73 us -> none  [the longest x3 7.69 us: coarse_mean(): grid_field.reshape(size_x // 2, 2, size_y // 2, 2, extent_along_z // 2, 2)]
    pallas_call x0 -> x3, Pallas kernels: none -> 5.56 us  [call(): pl.pallas_call(kernel, out_shape=[jax.ShapeDtypeStruct(shape, jnp.float32...]
    slice x38 -> x0, local copies, waits for them, and re-layouts: 4.46 us -> none  [the longest x4 1.23 us: central_ext(): return (jnp.roll(center, -1, 2) - jnp.roll(center, 1, 2)) * 0.5]
    ppermute x12 -> x5, waiting for transfers between devices: 6.37 us -> 2.19 us  [shifted(): return lax.ppermute(value, everywhere, pairs)]
  transfers between devices with their start and end apart: 14 -> 6, of which waited for: 8 -> 1; matrix products, arithmetic and copies ran while one was open for 28% -> 0% of each run, Pallas kernels for 0% -> 0%
where the time goes in v1:
time: 29.4 us; the launch traced here: 29.1 us
  starting transfers between devices  18.9 us (64%)
  Pallas kernels  5.56 us (19%)
  waiting for transfers between devices  2.19 us (7%)
  local copies, waits for them, and re-layouts  1.75 us (6%)
  between operations  0.69 us (2%)
    ppermute x5, starting transfers between devices, shifted(): return lax.ppermute(value, everywhere, pairs)  11.6 us
    all_to_all x1, starting transfers between devices, exchange(): lax.all_to_all(send.reshape(plan.gx * plan.gy, plan.rows, LANES), everywh...  7.33 us
    pallas_call x3, Pallas kernels, call(): pl.pallas_call(kernel, out_shape=[jax.ShapeDtypeStruct(shape, jnp.float32...  5.56 us
    ppermute x5, waiting for transfers between devices, shifted(): return lax.ppermute(value, everywhere, pairs)  2.19 us
    unnamed x8, local copies, waits for them, and re-layouts  1.75 us
  transfers between devices with their start and end apart: 6, of which 1 were waited for; matrix products, arithmetic and copies ran while one was open for 0% of the time, Pallas kernels for 0%

profile of v1, /device:TPU:0, one launch (start us, length us, event | category | flops | bytes accessed | tf_op | source)
XLA Modules:
  0.0 29.1 jit_solution(8354303841610944635)
XLA Ops:
  0.6 0.0 copy-start
  0.6 0.9 %copy-done = f32[19,4,4,128]{3,2,1,0:T(4,128)S(1)} copy-done((f32[19,4,4,128]{3,2,1,0:T(4,128)S(1)}, f32[19,4,4,128]{3,2,1,0:T(4,128)}, u32[]{:S(2)}) %copy-start) | copy-done | bytes 155672
  1.5 0.0 copy-start.2
  1.5 0.8 %copy-done.2 = f32[8,16,128]{2,1,0:T(8,128)S(1)} copy-done((f32[8,16,128]{2,1,0:T(8,128)S(1)}, f32[8,16,128]{2,1,0:T(8,128)}, u32[]{:S(2)}) %copy-start.2) | copy-done | bytes 65560
  2.4 1.2 %shard_map.41 = (f32[2,16,24,128]{3,2,1,0:T(8,128)}, f32[4,4,4,128]{3,2,1,0:T(4,128)S(1)}) custom-call(f32[8,16,128]{2,1,0:T(8,128)S(1)} %copy-done.2, f32[19,4,4,128]{3,2,1,0:T(4,128)S(1)} %copy-done), custom_call_target="tpu_custom_call" | custom-call | tf_op jit(solution)/shard_map/pallas_call | solution.py:514
  3.6 0.0 copy-start.1
  3.6 0.0 copy-start.3
  3.6 7.3 %all-to-all-start = ((f32[32,24,128]{2,1,0:T(8,128)}), f32[32,24,128]{2,1,0:T(8,128)S(1)}, u32[]{:S(2)}, u32[]{:S(2)}) async-start(f32[32,24,128]{2,1,0:T(8,128)} %bitcast.1), calls=%async_computation | async-start | bytes 786432 | tf_op jit(solution)/shard_map/all_to_all | solution.py:537
  10.9 0.0 copy-done.1
  10.9 0.0 copy-done.3
  11.0 1.8 %collective-permute-start = (f32[200,128]{1,0:T(8,128)S(1)}, f32[200,128]{1,0:T(8,128)S(1)}, u32[]{:S(2)}, u32[]{:S(2)}) collective-permute-start(f32[200,128]{1,0:T(8,128)S(1)} %get-tuple-element.11), channel_id=1, source_target_pairs={{0,16},{1,17},{2,18},{3,19},{4,20},{5,21},{6,22},{7,23},{8,24},{9,... | collective-permute-start | bytes 307208 | tf_op jit(solution)/shard_map/ppermute | solution.py:534
  12.8 0.0 collective-permute-start.1
  12.8 4.4 %collective-permute-start.2 = (f32[100,128]{1,0:T(8,128)S(1)}, f32[100,128]{1,0:T(8,128)S(1)}, u32[]{:S(2)}, u32[]{:S(2)}) collective-permute-start(f32[100,128]{1,0:T(8,128)S(1)} %get-tuple-element.13), channel_id=1, source_target_pairs={{0,15},{1,0},{2,1},{3,2},{4,3},{5,4},{6,5},{7,6},{8,7},{9,8},{10,9... | collective-permute-start | bytes 153608 | tf_op jit(solution)/shard_map/ppermute | solution.py:534
  17.3 0.0 collective-permute-start.3
  17.3 5.3 %collective-permute-start.4 = (f32[74,128]{1,0:T(8,128)S(1)}, f32[74,128]{1,0:T(8,128)S(1)}, u32[]{:S(2)}, u32[]{:S(2)}) collective-permute-start(f32[74,128]{1,0:T(8,128)S(1)} %get-tuple-element.15), channel_id=1, source_target_pairs={{0,31},{1,16},{2,17},{3,18},{4,19},{5,20},{6,21},{7,22},{8,23},{9,... | collective-permute-start | bytes 113672 | tf_op jit(solution)/shard_map/ppermute | solution.py:534
  22.6 2.2 %collective-permute-done.3.rest_3_ = f32[74,128]{1,0:T(8,128)S(1)} collective-permute-done((f32[74,128]{1,0:T(8,128)S(1)}, f32[74,128]{1,0:T(8,128)S(1)}, u32[]{:S(2)}, u32[]{:S(2)}) %collective-permute-start.3) | collective-permute-done | bytes 37920 | tf_op jit(solution)/shard_map/ppermute | solution.py:534
  24.8 0.0 collective-permute-done.4.rest_4_
  24.8 0.0 collective-permute-done.1.rest_1_
  24.8 0.0 collective-permute-done.2.rest_2_
  24.8 0.0 collective-permute-done.rest_0_
  24.8 0.0 all-to-all-done
  24.8 4.3 %shard_map.43 = (f32[8,16,128]{2,1,0:T(8,128)}, f32[19,4,4,128]{3,2,1,0:T(4,128)}) custom-call(s32[1]{0:T(128)} %bitcast.index, f32[8,16,128]{2,1,0:T(8,128)S(1)} %copy-done.3, f32[19,4,4,128]{3,2,1,0:T(4,128)S(1)} %copy-done.1, f32[4,4,4,128]{3,2,1,0:T(4,128)S(1)} %get-tuple-element.9.moments, f32[2,16,24,128]{3,2,1,0:T(8,128)S(1)} %bitcast.3, ...), custom_call_target="tpu_custom_call" | custom-call | tf_op jit(solution)/shard_map/pallas_call | solution.py:514
  (1 shorter events, 0.0 us)
Async XLA Ops:
  0.6 0.9 %copy-start = (f32[19,4,4,128]{3,2,1,0:T(4,128)S(1)}, f32[19,4,4,128]{3,2,1,0:T(4,128)}, u32[]{:S(2)}) copy-start(f32[19,4,4,128]{3,2,1,0:T(4,128)} %populations.5) | copy-start | bytes 466948
  1.5 0.8 %copy-start.2 = (f32[8,16,128]{2,1,0:T(8,128)S(1)}, f32[8,16,128]{2,1,0:T(8,128)}, u32[]{:S(2)}) copy-start(f32[8,16,128]{2,1,0:T(8,128)} %density.5) | copy-start | bytes 196612
  3.6 7.3 %copy-start.1 = (f32[19,4,4,128]{3,2,1,0:T(4,128)S(1)}, f32[19,4,4,128]{3,2,1,0:T(4,128)}, u32[]{:S(2)}) copy-start(f32[19,4,4,128]{3,2,1,0:T(4,128)} %populations.5) | copy-start | bytes 466948
  3.6 7.3 %copy-start.3 = (f32[8,16,128]{2,1,0:T(8,128)S(1)}, f32[8,16,128]{2,1,0:T(8,128)}, u32[]{:S(2)}) copy-start(f32[8,16,128]{2,1,0:T(8,128)} %density.5) | copy-start | bytes 196612
  3.6 21.2 %all-to-all-start = ((f32[32,24,128]{2,1,0:T(8,128)}), f32[32,24,128]{2,1,0:T(8,128)S(1)}, u32[]{:S(2)}, u32[]{:S(2)}) async-start(f32[32,24,128]{2,1,0:T(8,128)} %bitcast.1), calls=%async_computation | async-start | bytes 786432 | tf_op jit(solution)/shard_map/all_to_all | solution.py:537
  11.0 13.8 %collective-permute-start = (f32[200,128]{1,0:T(8,128)S(1)}, f32[200,128]{1,0:T(8,128)S(1)}, u32[]{:S(2)}, u32[]{:S(2)}) collective-permute-start(f32[200,128]{1,0:T(8,128)S(1)} %get-tuple-element.11), channel_id=1, source_target_pairs={{0,16},{1,17},{2,18},{3,19},{4,20},{5,21},{6,22},{7,23},{8,24},{9,... | collective-permute-start | bytes 307208 | tf_op jit(solution)/shard_map/ppermute | solution.py:534
  12.8 12.0 %collective-permute-start.1 = (f32[100,128]{1,0:T(8,128)S(1)}, f32[100,128]{1,0:T(8,128)S(1)}, u32[]{:S(2)}, u32[]{:S(2)}) collective-permute-start(f32[100,128]{1,0:T(8,128)S(1)} %get-tuple-element.12), channel_id=1, source_target_pairs={{0,1},{1,2},{2,3},{3,4},{4,5},{5,6},{6,7},{7,8},{8,9},{9,10},{10,1... | collective-permute-start | bytes 153608 | tf_op jit(solution)/shard_map/ppermute | solution.py:534
  12.8 12.0 %collective-permute-start.2 = (f32[100,128]{1,0:T(8,128)S(1)}, f32[100,128]{1,0:T(8,128)S(1)}, u32[]{:S(2)}, u32[]{:S(2)}) collective-permute-start(f32[100,128]{1,0:T(8,128)S(1)} %get-tuple-element.13), channel_id=1, source_target_pairs={{0,15},{1,0},{2,1},{3,2},{4,3},{5,4},{6,5},{7,6},{8,7},{9,8},{10,9... | collective-permute-start | bytes 153608 | tf_op jit(solution)/shard_map/ppermute | solution.py:534
  17.3 7.5 %collective-permute-start.3 = (f32[74,128]{1,0:T(8,128)S(1)}, f32[74,128]{1,0:T(8,128)S(1)}, u32[]{:S(2)}, u32[]{:S(2)}) collective-permute-start(f32[74,128]{1,0:T(8,128)S(1)} %get-tuple-element.14), channel_id=1, source_target_pairs={{0,17},{1,18},{2,19},{3,20},{4,21},{5,22},{6,23},{7,24},{8,25},{9,... | collective-permute-start | bytes 113672 | tf_op jit(solution)/shard_map/ppermute | solution.py:534
  17.3 7.5 %collective-permute-start.4 = (f32[74,128]{1,0:T(8,128)S(1)}, f32[74,128]{1,0:T(8,128)S(1)}, u32[]{:S(2)}, u32[]{:S(2)}) collective-permute-start(f32[74,128]{1,0:T(8,128)S(1)} %get-tuple-element.15), channel_id=1, source_target_pairs={{0,31},{1,16},{2,17},{3,18},{4,19},{5,20},{6,21},{7,22},{8,23},{9,... | collective-permute-start | bytes 113672 | tf_op jit(solution)/shard_map/ppermute | solution.py:534

commit v2 on v1

v2 whole, which is shorter than its diff:
```python
import functools

import jax
import jax.numpy as jnp
from jax import lax
from jax.experimental import pallas as pl
from jax.experimental.pallas import tpu as pltpu
from jax.sharding import PartitionSpec as P

DENSITY_SUBSTEPS = 2

coupled_time_step = 0.0008
force_unit = 0.005
speed_unit = 2000.0
relax_time = 0.8
quench_depth = -0.25

LANES = 128
ROWS = 8
WINDOW_HALO = 5
WINDOW_ROWS = 24

SPEEDS = (
    (0, 0, 0),
    (1, 0, 0),
    (-1, 0, 0),
    (0, 1, 0),
    (0, -1, 0),
    (0, 0, 1),
    (0, 0, -1),
    (1, 1, 0),
    (-1, -1, 0),
    (1, -1, 0),
    (-1, 1, 0),
    (1, 0, 1),
    (-1, 0, -1),
    (1, 0, -1),
    (-1, 0, 1),
    (0, 1, 1),
    (0, -1, -1),
    (0, 1, -1),
    (0, -1, 1),
)
WEIGHTS = (1.0 / 3.0,) + (1.0 / 18.0,) * 6 + (1.0 / 36.0,) * 12
MOMENTS = 4


def moving(jump_x=None, jump_z=None):
    return [
        q
        for q, (cx, _, cz) in enumerate(SPEEDS)
        if (jump_x is None or cx == jump_x) and (jump_z is None or cz == jump_z)
    ]


class Plan:
    def __init__(self, count_x, count_y, density, populations):
        self.gx, self.gy = count_x, count_y
        self.x, self.y, self.z = density.shape
        _, self.xc, self.zc, self.yc = populations.shape
        self.yb = self.y // 2
        self.zf = 2 * self.zc
        self.window = self.zf + 2 * WINDOW_HALO
        self.half = self.zc // 2
        self.rows = WINDOW_ROWS
        self.pair = count_x == 2
        self.blocks = 2 if self.pair else 3
        self.planes = self.yc // LANES
        self.layers = self.blocks * self.x
        self.frame = self.y + ROWS
        self.coarse_layers = self.blocks * self.xc
        assert self.x * self.y == LANES and MOMENTS * self.xc * self.yb == LANES
        assert self.z == LANES and self.yc % LANES == 0 and self.zc % 2 == 0
        assert self.window + self.zc + self.half <= WINDOW_ROWS and self.zc + 2 <= ROWS
        wide = self.planes
        self.rows_x = self.x * self.y + 2 * 9 * self.zc * wide
        self.rows_y = self.x * ROWS + 9 * self.xc * wide
        self.rows_d = self.x * ROWS + 2 * 5 * wide

    def layer(self, x):
        return x % self.layers if self.pair else x + self.x

    def coarse_layer(self, x):
        return x % self.coarse_layers if self.pair else x + self.xc

    def span(self, low, high):
        seen = {}
        for x in range(low, high):
            seen.setdefault(self.layer(x), x)
        return list(seen.values())


def butterfly(arrays, granule):
    count = LANES // granule
    lane = lax.broadcasted_iota(jnp.int32, arrays[0].shape, 1) // granule
    bit = 1
    while bit < count:
        upper = (lane & bit) != 0
        turned = list(arrays)
        for a in range(count):
            if a & bit:
                continue
            low, high = arrays[a], arrays[a | bit]
            turned[a] = jnp.where(upper, pltpu.roll(high, bit * granule, 1), low)
            turned[a | bit] = jnp.where(upper, high, pltpu.roll(low, LANES - bit * granule, 1))
        arrays = turned
        bit *= 2
    return arrays


def roll(value, shift, dimension):
    size = value.shape[dimension]
    return pltpu.roll(value, shift % size, dimension)


def moments_of(members):
    total = functools.reduce(lambda a, b: a + b, members)
    out = [total]
    for axis in range(3):
        plus = [members[q] for q, c in enumerate(SPEEDS) if c[axis] == 1]
        minus = [members[q] for q, c in enumerate(SPEEDS) if c[axis] == -1]
        out.append(
            functools.reduce(lambda a, b: a + b, plus) - functools.reduce(lambda a, b: a + b, minus)
        )
    return out


def put(buffer, at, value):
    rows, width = value.shape
    for plane in range(width // LANES):
        buffer[at : at + rows, :] = value[:, plane * LANES : (plane + 1) * LANES]
        at += rows
    return at


def take(buffer, at, rows, planes):
    parts = [buffer[at + k * rows : at + (k + 1) * rows, :] for k in range(planes)]
    return parts[0] if planes == 1 else jnp.concatenate(parts, axis=1)


def pack_kernel(plan, density_in, populations_in, send, moments, density, populations, window, pieces, sems):
    fetch_density = pltpu.make_async_copy(density_in, density, sems.at[0])
    fetch_populations = pltpu.make_async_copy(populations_in, populations, sems.at[1])
    fetch_density.start()
    fetch_populations.start()
    copies = plan.gx if plan.pair else 1
    early = plan.window // ROWS * ROWS

    def deliver(low, high, first):
        out = []
        for copy in range(copies):
            out.append(
                pltpu.make_async_copy(
                    pieces.at[:, low:high, :], send.at[copy, :, low:high, :], sems.at[first + copy]
                )
            )
            out[-1].start()
        return out

    fetch_density.wait()
    rows = []
    for x in range(plan.x):
        for parity in range(2):
            rows.append(density[x, pl.ds(parity, plan.yb, stride=2), :])
    turned = jnp.concatenate(rows, axis=0).T
    halo = WINDOW_HALO
    window[halo : halo + plan.z, :] = turned
    window[0:halo, :] = turned[plan.z - halo :, :]
    window[halo + plan.z : 2 * halo + plan.z, :] = turned[:halo, :]
    for target in range(plan.gy):
        first = plan.zf * target
        pieces[target, 0 : plan.window, :] = window[first : first + plan.window, :]
    going = deliver(0, early, 2)
    fetch_populations.wait()
    fields = [[None] * plan.xc for _ in range(MOMENTS)]
    for x in range(plan.xc):
        for f, value in enumerate(moments_of([populations[q, x] for q in range(len(SPEEDS))])):
            fields[f][x] = value
            moments[f, x] = value
    turned = []
    for plane in range(plan.planes):
        span = slice(plane * LANES, (plane + 1) * LANES)
        turned += butterfly([value[:, span] for row in fields for value in row], plan.yb)
    y = lax.broadcasted_iota(jnp.int32, (plan.half, LANES), 1) % plan.yb
    y_all = lax.broadcasted_iota(jnp.int32, (plan.zc, LANES), 1) % plan.yb
    for target in range(plan.gy):
        before, after = turned[(target - 1) % plan.gy], turned[(target + 1) % plan.gy]
        beside = jnp.where(y_all >= plan.yb // 2, before, after)
        first, second = beside[: plan.half], beside[plan.half :]
        packed = jnp.where(
            (y < 2) | (y >= plan.yb - 2),
            first,
            jnp.where(y < 4, roll(second, 2, 1), roll(second, -2, 1)),
        )
        at = plan.window
        pieces[target, at : at + plan.zc, :] = turned[target]
        pieces[target, at + plan.zc : at + plan.zc + plan.half, :] = packed
        left = plan.rows - (at + plan.zc + plan.half)
        if left:
            pieces[target, plan.rows - left :, :] = jnp.zeros((left, LANES), jnp.float32)
    going += deliver(early, plan.rows, 2 + copies)
    for copy in going:
        copy.wait()


def edge_kernel(plan, index, density, populations, moments, to_x, near, far, near_x, far_x):
    even = index[1] == 0

    def both(first, second, at, up, down):
        put(first, at, jnp.where(even, up, down))
        return put(second, at, jnp.where(even, down, up))

    at = plan.x * plan.y
    for x in range(plan.x):
        to_x[x * plan.y : (x + 1) * plan.y, :] = density[x]
        up, down = density[x, plan.y - ROWS :, :], density[x, :ROWS, :]
        both(near, far, x * ROWS, up, down)
        both(near_x, far_x, x * ROWS, up, down)
    for x, jump in ((plan.xc - 1, 1), (0, -1)):
        for f in range(MOMENTS):
            at = put(to_x, at, moments[f, x])
        for q in moving(jump_x=jump):
            at = put(to_x, at, populations[q, x])
    last = slice(plan.zc - 1, plan.zc)
    first = slice(0, 1)
    at = plan.x * ROWS
    for x in range(plan.xc):
        for f in range(MOMENTS):
            at = both(near, far, at, moments[f, x, last], moments[f, x, first])
        for up, down in zip(moving(jump_z=1), moving(jump_z=-1), strict=True):
            at = both(near, far, at, populations[up, x, last], populations[down, x, first])
    at = plan.x * ROWS
    for x, jump_x in ((plan.xc - 1, 1), (0, -1)):
        for f in range(MOMENTS):
            at = both(near_x, far_x, at, moments[f, x, last], moments[f, x, first])
        for up, down in zip(moving(jump_x, 1), moving(jump_x, -1), strict=True):
            at = both(near_x, far_x, at, populations[up, x, last], populations[down, x, first])


def gather_solvent(plan, populations, moments, halo, field, member):
    from_low, from_high, from_below, from_above, below_low, below_high, above_low, above_high = halo
    width = plan.planes

    def store(target, lead, value_own, value_below, value_above):
        target[lead + (slice(0, plan.zc),)] = value_own
        if value_below is not None:
            target[lead + (slice(ROWS - 1, ROWS),)] = value_below
        if value_above is not None:
            target[lead + (slice(plan.zc, plan.zc + 1),)] = value_above

    for x in range(plan.xc):
        at = plan.x * ROWS + x * 9 * width
        for f in range(MOMENTS):
            store(
                field,
                (f, x + 1),
                moments[f, x],
                from_below(at, 1, width),
                from_above(at, 1, width),
            )
            at += width
        at_plus = at_minus = at
        for q, (_, _, jump_z) in enumerate(SPEEDS):
            below = above = None
            if jump_z == 1:
                below = from_below(at_plus, 1, width)
                at_plus += width
            if jump_z == -1:
                above = from_above(at_minus, 1, width)
                at_minus += width
            store(member, (q, x + 1), populations[q, x], below, above)
    for slot, block, first, low, high, jump in (
        (0, from_low, True, below_low, above_low, 1),
        (plan.xc + 1, from_high, False, below_high, above_high, -1),
    ):
        at = plan.x * plan.y + (0 if first else 9 * plan.zc * width)
        corner = plan.x * ROWS + (0 if first else 5 * width)
        for f in range(MOMENTS):
            store(
                field,
                (f, slot),
                block(at, plan.zc, width),
                low(corner, 1, width),
                high(corner, 1, width),
            )
            at += plan.zc * width
            corner += width
        for q in moving(jump_x=jump):
            jump_z = SPEEDS[q][2]
            store(
                member,
                (q, slot),
                block(at, plan.zc, width),
                low(corner, 1, width) if jump_z == 1 else None,
                high(corner, 1, width) if jump_z == -1 else None,
            )
            at += plan.zc * width


def laplace_at(plan, source, x):
    value = source[plan.layer(x)]
    running = -6.0 * value + source[plan.layer(x - 1)] + source[plan.layer(x + 1)]
    running = running + roll(value, 1, 0) + roll(value, -1, 0)
    return running + roll(value, 1, 1) + roll(value, -1, 1)


def potential_at(plan, grid, lap, pot, reach):
    for x in plan.span(-reach, plan.x + reach):
        lap[plan.layer(x)] = laplace_at(plan, grid, x)
    for x in plan.span(1 - reach, plan.x + reach - 1):
        here = plan.layer(x)
        value = grid[here]
        pot[here] = (
            (quench_depth + 1.0) * value
            + 2.0 * lap[here]
            + laplace_at(plan, lap, x)
            + value * value * value
        )


def central_at(plan, source, x, c):
    if c == 0:
        return source[plan.layer(x + 1)] - source[plan.layer(x - 1)]
    value = source[plan.layer(x)]
    return roll(value, -1, c - 1) - roll(value, 1, c - 1)


def first_substep(plan, density, halo, base, slope, drift, push, grid, lap, pot):
    from_low, from_high, from_below, from_above, below_low, below_high, above_low, above_high = halo
    sets = [(0, None, from_below, from_above)]
    if plan.pair:
        sets.append((plan.x, from_low, below_low, above_low))
    else:
        sets.append((-plan.x, from_low, below_low, above_low))
        sets.append((plan.x, from_high, below_high, above_high))
    for first, block, below, above in sets:
        for x in range(plan.x):
            here = plan.layer(first + x)
            grid[here, ROWS : ROWS + plan.y] = (
                density[x] if block is None else block(x * plan.y, plan.y, 1)
            )
            grid[here, :ROWS] = below(x * ROWS, ROWS, 1)
            grid[here, ROWS + plan.y :] = above(x * ROWS, ROWS, 1)
    potential_at(plan, grid, lap, pot, 6)
    shape = grid.shape[1:]
    odd = [(lax.broadcasted_iota(jnp.int32, shape, c) & 1) != 0 for c in range(2)]
    rows = slice(ROWS // 2, ROWS // 2 + plan.frame)
    reach = 3 * (DENSITY_SUBSTEPS - 1)
    wanted = {plan.layer(x): x for x in plan.span(-reach, plan.x + reach)}
    done = set()
    for coarse in range(-2, plan.xc + 2):
        force = []
        for c in range(3):
            total = None
            for x in (2 * coarse, 2 * coarse + 1):
                now = grid[plan.layer(x)] * central_at(plan, pot, x, c)
                total = now if total is None else total + now
            for dimension in range(2):
                total = total + jnp.where(
                    odd[dimension], roll(total, 1, dimension), roll(total, -1, dimension)
                )
            force.append(total * (-0.25 * force_unit / 8.0))
            if 0 <= coarse < plan.xc:
                push[c, coarse] = force[c][rows]
        for x in (2 * coarse, 2 * coarse + 1):
            here = plan.layer(x)
            if here not in wanted or here in done:
                continue
            done.add(here)
            base[here] = (grid[here] + coupled_time_step * laplace_at(plan, pot, x))[rows]
            total = None
            for c in range(3):
                scaled = central_at(plan, grid, x, c) * (0.5 * speed_unit * coupled_time_step)
                slope[c, here] = scaled[rows]
                now = force[c] * scaled
                total = now if total is None else total + now
            drift[here] = total[rows]


def prepare_kernel(plan, index, density, populations, moments, *rest):
    neighbours = 5 if plan.pair else 8
    buffers, rest = rest[:neighbours], rest[neighbours:]
    base, slope, drift, push, field, member, grid, lap, pot = rest
    even = index[1] == 0

    def plain(ref):
        return lambda at, rows, planes: take(ref, at, rows, planes)

    def either(first, second):
        return lambda at, rows, planes: jnp.where(
            even, take(first, at, rows, planes), take(second, at, rows, planes)
        )

    if plan.pair:
        other, near, far, near_x, far_x = buffers
        low = high = other
        near_low = near_high = near_x
        far_low = far_high = far_x
    else:
        low, high, near, far, near_low, near_high, far_low, far_high = buffers
    halo = (
        plain(low),
        plain(high),
        either(far, near),
        either(near, far),
        either(far_low, near_low),
        either(far_high, near_high),
        either(near_low, far_low),
        either(near_high, far_high),
    )
    gather_solvent(plan, populations, moments, halo, field, member)
    first_substep(plan, density, halo, base, slope, drift, push, grid, lap, pot)


def solvent_part(plan, place, received, field, member, out, grid, lap, pot, pooled, forces):
    width, layers = plan.planes, plan.layers
    senders = LANES // plan.yb

    def load(source, parity, z):
        parts = [source[parity, k, z * layers : (z + 1) * layers, :] for k in range(width)]
        return parts[0] if width == 1 else jnp.concatenate(parts, axis=1)

    def save(target, parity, z, value):
        for k in range(width):
            target[parity, k, z * layers : (z + 1) * layers, :] = value[:, k * LANES : (k + 1) * LANES]

    for tile in range(pl.cdiv(plan.window, ROWS)):
        count = min(ROWS, plan.window - tile * ROWS)
        for block in range(plan.blocks):
            for plane in range(width):
                arrays = [
                    received[place(block), plane * senders + t, tile * ROWS : (tile + 1) * ROWS, :]
                    for t in range(senders)
                ]
                for g, value in enumerate(butterfly(arrays, plan.yb)):
                    first = tile * ROWS * layers + block * plan.x + g // 2
                    grid[g % 2, plane, pl.ds(first, count, stride=layers), :] = value[:count]

    def laplace(source, z):
        even, odd = load(source, 0, z), load(source, 1, z)
        sides = (odd + roll(odd, 1, 1), even + roll(even, -1, 1))
        out = []
        for parity, value in enumerate((even, odd)):
            running = -6.0 * value + load(source, parity, z - 1) + load(source, parity, z + 1)
            running = running + sides[parity]
            out.append(running + roll(value, 1, 0) + roll(value, -1, 0))
        return out

    for z in range(1, plan.window - 1):
        for parity, value in enumerate(laplace(grid, z)):
            save(lap, parity, z, value)
    for z in range(2, plan.window - 2):
        for parity, second in enumerate(laplace(lap, z)):
            value = load(grid, parity, z)
            save(
                pot,
                parity,
                z,
                (quench_depth + 1.0) * value
                + 2.0 * load(lap, parity, z)
                + second
                + value * value * value,
            )
    scale = -0.5 * force_unit / 8.0
    coarse_layers = plan.coarse_layers
    for coarse in range(-1, plan.zc + 1):
        total = None
        for z in (2 * coarse + WINDOW_HALO, 2 * coarse + 1 + WINDOW_HALO):
            even, odd = load(grid, 0, z), load(grid, 1, z)
            pot_even, pot_odd = load(pot, 0, z), load(pot, 1, z)
            along_x = even * (roll(pot_even, -1, 0) - roll(pot_even, 1, 0)) + odd * (
                roll(pot_odd, -1, 0) - roll(pot_odd, 1, 0)
            )
            along_y = even * (pot_odd - roll(pot_odd, 1, 1)) + odd * (roll(pot_even, -1, 1) - pot_even)
            along_z = even * (load(pot, 0, z + 1) - load(pot, 0, z - 1)) + odd * (
                load(pot, 1, z + 1) - load(pot, 1, z - 1)
            )
            now = (along_x, along_y, along_z)
            total = now if total is None else tuple(a + b for a, b in zip(total, now))
        for c in range(3):
            for k in range(width):
                at = (c * width + k) * layers
                pooled[coarse % ROWS, at : at + layers, :] = total[c][:, k * LANES : (k + 1) * LANES]
                value = (
                    pooled[coarse % ROWS, pl.ds(at, coarse_layers, stride=2), :]
                    + pooled[coarse % ROWS, pl.ds(at + 1, coarse_layers, stride=2), :]
                )
                forces[c, k, pl.ds(coarse % ROWS, coarse_layers, stride=ROWS), :] = value * scale

    rate = 1.0 / relax_time
    gain = 1.0 - 0.5 / relax_time
    for slot in range(plan.xc + 2):
        x = slot - 1
        at = plan.coarse_layer(x) * ROWS
        force = []
        for c in range(3):
            parts = [forces[c, k, at : at + ROWS, :] for k in range(width)]
            force.append(parts[0] if width == 1 else jnp.concatenate(parts, axis=1))
        mass = field[0, slot]
        inverse = 1.0 / mass
        speed = [(field[c + 1, slot] + 0.5 * force[c]) * inverse for c in range(3)]
        square = speed[0] * speed[0] + speed[1] * speed[1] + speed[2] * speed[2]
        work_rate = speed[0] * force[0] + speed[1] * force[1] + speed[2] * force[2]
        rest = mass * (rate - 1.5 * rate * square) - (3.0 * gain) * work_rate

        def emit(q, even, odd):
            jump_x, jump_y, jump_z = SPEEDS[q]
            target = x + jump_x
            if not 0 <= target < plan.xc:
                return
            value = member[q, slot] * (1.0 - rate) + WEIGHTS[q] * (even if odd is None else even + odd)
            if jump_z:
                value = roll(value, jump_z, 0)
            value = value[: plan.zc]
            if jump_y:
                value = roll(value, jump_y, 1)
            out[q, target] = value

        emit(0, rest, None)
        for q in range(1, len(SPEEDS), 2):
            projected = along = None
            for c in range(3):
                if SPEEDS[q][c]:
                    s, g = SPEEDS[q][c] * speed[c], SPEEDS[q][c] * force[c]
                    projected = s if projected is None else projected + s
                    along = g if along is None else along + g
            even = rest + (4.5 * rate) * mass * projected * projected + (9.0 * gain) * projected * along
            odd = (3.0 * rate) * mass * projected + (3.0 * gain) * along
            emit(q, even, odd)
            emit(q + 1, even, -odd)


def density_part(plan, place, received, base, slope, drift, push, out, flow, column, beside, grid, lap, pot):
    def spread(source, period, offset):
        count = source.shape[0]
        row = lax.broadcasted_iota(jnp.int32, (count, plan.z), 0)
        cell = lax.broadcasted_iota(jnp.int32, (count, plan.z), 1) // 2
        chosen = (row // period) * plan.zc + row % period + offset == cell
        return lax.dot_general(
            source.T,
            chosen.astype(jnp.float32),
            (((1,), (0,)), ((), ())),
            precision=lax.Precision.HIGHEST,
            preferred_element_type=jnp.float32,
        )

    own_row = ROWS // 2
    yb = plan.yb
    for block in range(plan.blocks):
        at = plan.window
        for j in range(plan.gy):
            column[j * plan.zc : (j + 1) * plan.zc, :] = received[place(block), j, at : at + plan.zc, :]
            beside[j * plan.half : (j + 1) * plan.half, :] = received[
                place(block), j, at + plan.zc : at + plan.zc + plan.half, :
            ]
        own = spread(column[...], plan.zc, 0)
        first = spread(beside[...], plan.half, 0)
        second = spread(beside[...], plan.half, plan.half)
        for f in range(MOMENTS):
            for x in range(plan.xc):
                at = (f * plan.xc + x) * yb
                lead = (f, block * plan.xc + x)
                after = first[at : at + 2] + second[at + 2 : at + 4]
                before = first[at + yb - 2 : at + yb] + second[at + yb - 4 : at + yb - 2]
                for parity in range(2):
                    flow[lead + (pl.ds(own_row + parity, yb, stride=2),)] = own[at : at + yb]
                    flow[lead + (pl.ds(own_row + plan.y + parity, 2, stride=2),)] = after
                    flow[lead + (pl.ds(own_row - 4 + parity, 2, stride=2),)] = before

    reach = 3 * (DENSITY_SUBSTEPS - 1)
    inverses = {}
    for x in plan.span(-reach, plan.x + reach):
        here, slot = plan.layer(x), plan.coarse_layer(x // 2)
        if slot not in inverses:
            inverses[slot] = 1.0 / flow[0, slot]
        advection = drift[here]
        for c in range(3):
            advection = advection + flow[c + 1, slot] * slope[c, here]
        grid[here] = base[here] - advection * inverses[slot]
    potential_at(plan, grid, lap, pot, 2)
    for coarse in range(plan.xc):
        slot = plan.coarse_layer(coarse)
        scaled = (0.5 * speed_unit) / flow[0, slot]
        speed = [(flow[c + 1, slot] + push[c, coarse]) * scaled for c in range(3)]
        for x in (2 * coarse, 2 * coarse + 1):
            change = laplace_at(plan, pot, x)
            for c in range(3):
                change = change - speed[c] * central_at(plan, grid, x, c)
            value = grid[plan.layer(x)] + coupled_time_step * change
            out[x] = value[own_row : own_row + plan.y]


def update_kernel(plan, index, received, base, slope, drift, push, field, member, *rest):
    density_next, populations_next = rest[:2]
    side_grid, side_lap, side_pot, pooled, forces, flow, column, beside, grid, lap, pot = rest[2:13]
    density_out, populations_out, sems = rest[13:]
    mine = index[0]

    def place(block):
        if not plan.pair:
            return block
        return mine if block == 0 else 1 - mine

    solvent_part(
        plan, place, received, field, member, populations_out, side_grid, side_lap, side_pot, pooled, forces
    )
    give_populations = pltpu.make_async_copy(populations_out, populations_next, sems.at[0])
    give_populations.start()
    density_part(
        plan, place, received, base, slope, drift, push, density_out, flow, column, beside, grid, lap, pot
    )
    give_density = pltpu.make_async_copy(density_out, density_next, sems.at[1])
    give_density.start()
    give_populations.wait()
    give_density.wait()


VMEM, SMEM, HBM = pltpu.VMEM, pltpu.SMEM, pltpu.HBM


def call(kernel, arguments, outputs, scratch, sems=0, cost=None):
    return pl.pallas_call(
        kernel,
        out_shape=[jax.ShapeDtypeStruct(shape, jnp.float32) for shape, _ in outputs],
        in_specs=[pl.BlockSpec(memory_space=space) for _, space in arguments],
        out_specs=[pl.BlockSpec(memory_space=space) for _, space in outputs],
        scratch_shapes=[pltpu.VMEM(shape, jnp.float32) for shape in scratch]
        + ([pltpu.SemaphoreType.DMA((sems,))] if sems else []),
        compiler_params=pltpu.CompilerParams(vmem_limit_bytes=16 * 1024 * 1024),
        cost_estimate=cost,
    )(*[value for value, _ in arguments])


def exchange(plan, send, to_x, near, far, near_x, far_x):
    everywhere = ("gx", "gy")

    def shifted(value, step_x, partner):
        pairs = [
            (a * plan.gy + b, ((a + step_x) % plan.gx) * plan.gy + partner(b))
            for a in range(plan.gx)
            for b in range(plan.gy)
        ]
        return lax.ppermute(value, everywhere, pairs)

    def same(b):
        return b

    def nearer(b):
        return b + 1 if b % 2 == 0 else b - 1

    def farther(b):
        return (b - 1 if b % 2 == 0 else b + 1) % plan.gy

    if plan.pair:
        whole = lax.all_to_all(
            send.reshape(plan.gx * plan.gy, plan.rows, LANES), everywhere, 0, 0, tiled=True
        )
        received = whole.reshape(plan.gx, plan.gy, plan.rows, LANES)
        halo = (
            shifted(to_x, 1, same),
            shifted(near, 0, nearer),
            shifted(far, 0, farther),
            shifted(near_x, 1, nearer),
            shifted(far_x, 1, farther),
        )
        return received, halo
    send = send[0]
    three = jnp.stack([shifted(send, 1, same), send, shifted(send, -1, same)], axis=1)
    three = lax.all_to_all(three, "gy", 0, 0, tiled=True)
    halo = (
        shifted(to_x, 1, same),
        shifted(to_x, -1, same),
        shifted(near, 0, nearer),
        shifted(far, 0, farther),
        shifted(near_x, 1, nearer),
        shifted(near_x, -1, nearer),
        shifted(far_x, 1, farther),
        shifted(far_x, -1, farther),
    )
    return three.transpose(1, 0, 2, 3), halo


def local(density, populations):
    plan = Plan(lax.axis_size("gx"), lax.axis_size("gy"), density, populations)
    copies = plan.gx if plan.pair else 1
    index = jnp.stack([lax.axis_index("gx"), lax.axis_index("gy") % 2]).astype(jnp.int32)
    send, moments = call(
        functools.partial(pack_kernel, plan),
        [(density, HBM), (populations, HBM)],
        [
            ((copies, plan.gy, plan.rows, LANES), HBM),
            ((MOMENTS, plan.xc, plan.zc, plan.yc), VMEM),
        ],
        [
            density.shape,
            populations.shape,
            (plan.z + 2 * ROWS, LANES),
            (plan.gy, plan.rows, LANES),
        ],
        sems=2 + 2 * copies,
    )
    own = [(index, SMEM), (density, VMEM), (populations, VMEM), (moments, VMEM)]
    edges = call(
        functools.partial(edge_kernel, plan),
        own,
        [((rows, LANES), VMEM) for rows in (plan.rows_x,) + (plan.rows_y,) * 2 + (plan.rows_d,) * 2],
        [],
    )
    received, halo = exchange(plan, send, *edges)
    tall = (plan.layers, plan.y + 2 * ROWS, plan.z)
    short = (plan.layers, plan.frame, plan.z)
    prepared = call(
        functools.partial(prepare_kernel, plan),
        own + [(value, VMEM) for value in halo],
        [
            (short, VMEM),
            ((3,) + short, VMEM),
            (short, VMEM),
            ((3, plan.xc, plan.frame, plan.z), VMEM),
            ((MOMENTS, plan.xc + 2, ROWS, plan.yc), VMEM),
            ((len(SPEEDS), plan.xc + 2, ROWS, plan.yc), VMEM),
        ],
        [tall, tall, tall],
    )
    side = (2, plan.planes, plan.window * plan.layers, LANES)
    return call(
        functools.partial(update_kernel, plan),
        [(index, SMEM), (received, VMEM)] + [(value, VMEM) for value in prepared],
        [(density.shape, HBM), (populations.shape, HBM)],
        [
            side,
            side,
            side,
            (ROWS, 3 * plan.planes * plan.layers, LANES),
            (3, plan.planes, plan.coarse_layers * ROWS, LANES),
            (MOMENTS, plan.coarse_layers, plan.frame, plan.z),
            (plan.zc * plan.gy, LANES),
            (plan.half * plan.gy, LANES),
            short,
            short,
            short,
            density.shape,
            populations.shape,
        ],
        sems=2,
    )


def solution(mesh):
    return jax.shard_map(
        lambda density, populations: tuple(local(density, populations)),
        mesh=mesh,
        in_specs=(P("gx", "gy", None), P(None, "gx", "gy", None)),
        out_specs=(P("gx", "gy", None), P(None, "gx", "gy", None)),
        check_vma=False,
    )
```

time: 29.4 us -> 30.8 us (1.048)
  starting transfers between devices: 18.9 us -> 15.3 us
  waiting for transfers between devices: 2.19 us -> 5.31 us
  Pallas kernels: 5.56 us -> 7.45 us
    ppermute x5, starting transfers between devices: 11.6 us -> 7.94 us  [shifted(): return lax.ppermute(value, everywhere, pairs)]
    ppermute x5, waiting for transfers between devices: 2.19 us -> 5.31 us  [shifted(): return lax.ppermute(value, everywhere, pairs)]
    pallas_call x3 -> x4, Pallas kernels: 5.56 us -> 7.45 us  [call(): pl.pallas_call(kernel, out_shape=[jax.ShapeDtypeStruct(shape, jnp.float32...]
  transfers between devices with their start and end apart: 6 -> 6, of which waited for: 1 -> 2; matrix products, arithmetic and copies ran while one was open for 0% -> 0% of each run, Pallas kernels for 0% -> 8%
where the time goes in v2:
time: 30.8 us; the launch traced here: 30.6 us
  starting transfers between devices  15.3 us (50%)
  Pallas kernels  7.45 us (24%)
  waiting for transfers between devices  5.31 us (17%)
  local copies, waits for them, and re-layouts  1.76 us (6%)
  between operations  0.71 us (2%)
    ppermute x5, starting transfers between devices, shifted(): return lax.ppermute(value, everywhere, pairs)  7.94 us
    pallas_call x4, Pallas kernels, call(): pl.pallas_call(kernel, out_shape=[jax.ShapeDtypeStruct(shape, jnp.float32...  7.45 us
    all_to_all x1, starting transfers between devices, exchange(): lax.all_to_all(send.reshape(plan.gx * plan.gy, plan.rows, LANES), everywh...  7.33 us
    ppermute x5, waiting for transfers between devices, shifted(): return lax.ppermute(value, everywhere, pairs)  5.31 us
    unnamed x8, local copies, waits for them, and re-layouts  1.76 us
  transfers between devices with their start and end apart: 6, of which 2 were waited for; matrix products, arithmetic and copies ran while one was open for 0% of the time, Pallas kernels for 8%

profile of v2, /device:TPU:0, one launch (start us, length us, event | category | flops | bytes accessed | tf_op | source)
XLA Modules:
  0.0 30.6 jit_solution(8790696804456805548)
XLA Ops:
  0.6 0.0 copy-start
  0.6 0.9 %copy-done = f32[19,4,4,128]{3,2,1,0:T(4,128)S(1)} copy-done((f32[19,4,4,128]{3,2,1,0:T(4,128)S(1)}, f32[19,4,4,128]{3,2,1,0:T(4,128)}, u32[]{:S(2)}) %copy-start) | copy-done | bytes 155672
  1.5 0.0 copy-start.2
  1.5 0.8 %copy-done.2 = f32[8,16,128]{2,1,0:T(8,128)S(1)} copy-done((f32[8,16,128]{2,1,0:T(8,128)S(1)}, f32[8,16,128]{2,1,0:T(8,128)}, u32[]{:S(2)}) %copy-start.2) | copy-done | bytes 65560
  2.4 1.5 %shard_map.41 = (f32[2,16,24,128]{3,2,1,0:T(8,128)}, f32[4,4,4,128]{3,2,1,0:T(4,128)S(1)}) custom-call(f32[8,16,128]{2,1,0:T(8,128)S(1)} %copy-done.2, f32[19,4,4,128]{3,2,1,0:T(4,128)S(1)} %copy-done), custom_call_target="tpu_custom_call" | custom-call | tf_op jit(solution)/shard_map/pallas_call | solution.py:622
  3.9 0.0 copy-start.1
  3.9 0.0 copy-start.3
  3.9 7.3 %all-to-all-start = ((f32[32,24,128]{2,1,0:T(8,128)}), f32[32,24,128]{2,1,0:T(8,128)S(1)}, u32[]{:S(2)}, u32[]{:S(2)}) async-start(f32[32,24,128]{2,1,0:T(8,128)} %bitcast.2), calls=%async_computation | async-start | bytes 786432 | tf_op jit(solution)/shard_map/all_to_all | solution.py:655
  11.3 0.1 pad_add_fusion.index
  11.3 0.0 copy-done.1
  11.3 0.0 copy-done.3
  11.3 0.6 %shard_map.42 = (f32[200,128]{1,0:T(8,128)S(1)}, f32[100,128]{1,0:T(8,128)S(1)}, f32[100,128]{1,0:T(8,128)S(1)}, f32[74,128]{1,0:T(8,128)S(1)}, f32[74,128]{1,0:T(8,128)S(1)}) custom-call(s32[2]{0:T(128)S(1)} %pad_add_fusion.index, f32[8,16,128]{2,1,0:T(8,128)S(1)} %copy-done.3, f32[19,4,4,128]{3,2,1,0:T(4,128)S(1)} %copy-done.1, ...), custom_call_target="tpu_custom_call" | custom-call | tf_op jit(solution)/shard_map/pallas_call | solution.py:622
  11.9 1.8 %collective-permute-start = (f32[200,128]{1,0:T(8,128)S(1)}, f32[200,128]{1,0:T(8,128)S(1)}, u32[]{:S(2)}, u32[]{:S(2)}) collective-permute-start(f32[200,128]{1,0:T(8,128)S(1)} %get-tuple-element.17), channel_id=1, source_target_pairs={{0,16},{1,17},{2,18},{3,19},{4,20},{5,21},{6,22},{7,23},{8,24},{9,... | collective-permute-start | bytes 307208 | tf_op jit(solution)/shard_map/ppermute | solution.py:643
  13.8 0.0 collective-permute-start.1
  13.8 4.4 %collective-permute-start.2 = (f32[100,128]{1,0:T(8,128)S(1)}, f32[100,128]{1,0:T(8,128)S(1)}, u32[]{:S(2)}, u32[]{:S(2)}) collective-permute-start(f32[100,128]{1,0:T(8,128)S(1)} %get-tuple-element.19), channel_id=1, source_target_pairs={{0,15},{1,2},{2,1},{3,4},{4,3},{5,6},{6,5},{7,8},{8,7},{9,10},{10,... | collective-permute-start | bytes 153608 | tf_op jit(solution)/shard_map/ppermute | solution.py:643
  18.2 0.0 collective-permute-start.3
  18.2 1.7 %collective-permute-start.4 = (f32[74,128]{1,0:T(8,128)S(1)}, f32[74,128]{1,0:T(8,128)S(1)}, u32[]{:S(2)}, u32[]{:S(2)}) collective-permute-start(f32[74,128]{1,0:T(8,128)S(1)} %get-tuple-element.21), channel_id=1, source_target_pairs={{0,31},{1,18},{2,17},{3,20},{4,19},{5,22},{6,21},{7,24},{8,23},{9,... | collective-permute-start | bytes 113672 | tf_op jit(solution)/shard_map/ppermute | solution.py:643
  19.9 1.7 %collective-permute-done.3.rest_3_ = f32[74,128]{1,0:T(8,128)S(1)} collective-permute-done((f32[74,128]{1,0:T(8,128)S(1)}, f32[74,128]{1,0:T(8,128)S(1)}, u32[]{:S(2)}, u32[]{:S(2)}) %collective-permute-start.3) | collective-permute-done | bytes 37920 | tf_op jit(solution)/shard_map/ppermute | solution.py:643
  21.6 3.6 %collective-permute-done.4.rest_4_ = f32[74,128]{1,0:T(8,128)S(1)} collective-permute-done((f32[74,128]{1,0:T(8,128)S(1)}, f32[74,128]{1,0:T(8,128)S(1)}, u32[]{:S(2)}, u32[]{:S(2)}) %collective-permute-start.4) | collective-permute-done | bytes 37920 | tf_op jit(solution)/shard_map/ppermute | solution.py:643
  25.2 0.0 collective-permute-done.1.rest_1_
  25.2 0.0 collective-permute-done.2.rest_2_
  25.2 0.0 collective-permute-done.rest_0_
  25.2 2.0 %shard_map.43 = (f32[16,24,128]{2,1,0:T(8,128)S(1)}, f32[3,16,24,128]{3,2,1,0:T(8,128)S(1)}, f32[16,24,128]{2,1,0:T(8,128)S(1)}, f32[3,4,24,128]{3,2,1,0:T(8,128...) custom-call(s32[2]{0:T(128)S(1)} %pad_add_fusion.index, f32[8,16,128]{2,1,0:T(8,128)S(1)} %copy-done.3, ...), custom_call_target="tpu_custom_call" | custom-call | tf_op jit(solution)/shard_map/pallas_call | solution.py:622
  27.2 0.0 all-to-all-done
  27.2 3.4 %shard_map.44 = (f32[8,16,128]{2,1,0:T(8,128)}, f32[19,4,4,128]{3,2,1,0:T(4,128)}) custom-call(s32[2]{0:T(128)S(1)} %pad_add_fusion.index, f32[2,16,24,128]{3,2,1,0:T(8,128)S(1)} %bitcast.4, f32[16,24,128]{2,1,0:T(8,128)S(1)} %get-tuple-element.22.base, f32[3,16,24,128]{3,2,1,0:T(8,128)S(1)} %get-tuple-element.23.slope, ...), custom_call_target="tpu_custom_call" | custom-call | tf_op jit(solution)/shard_map/pallas_call | solution.py:622
Async XLA Ops:
  0.6 0.9 %copy-start = (f32[19,4,4,128]{3,2,1,0:T(4,128)S(1)}, f32[19,4,4,128]{3,2,1,0:T(4,128)}, u32[]{:S(2)}) copy-start(f32[19,4,4,128]{3,2,1,0:T(4,128)} %populations.3) | copy-start | bytes 466948
  1.5 0.8 %copy-start.2 = (f32[8,16,128]{2,1,0:T(8,128)S(1)}, f32[8,16,128]{2,1,0:T(8,128)}, u32[]{:S(2)}) copy-start(f32[8,16,128]{2,1,0:T(8,128)} %density.3) | copy-start | bytes 196612
  3.9 7.5 %copy-start.1 = (f32[19,4,4,128]{3,2,1,0:T(4,128)S(1)}, f32[19,4,4,128]{3,2,1,0:T(4,128)}, u32[]{:S(2)}) copy-start(f32[19,4,4,128]{3,2,1,0:T(4,128)} %populations.3) | copy-start | bytes 466948
  3.9 7.4 %copy-start.3 = (f32[8,16,128]{2,1,0:T(8,128)S(1)}, f32[8,16,128]{2,1,0:T(8,128)}, u32[]{:S(2)}) copy-start(f32[8,16,128]{2,1,0:T(8,128)} %density.3) | copy-start | bytes 196612
  3.9 23.3 %all-to-all-start = ((f32[32,24,128]{2,1,0:T(8,128)}), f32[32,24,128]{2,1,0:T(8,128)S(1)}, u32[]{:S(2)}, u32[]{:S(2)}) async-start(f32[32,24,128]{2,1,0:T(8,128)} %bitcast.2), calls=%async_computation | async-start | bytes 786432 | tf_op jit(solution)/shard_map/all_to_all | solution.py:655
  11.9 13.3 %collective-permute-start = (f32[200,128]{1,0:T(8,128)S(1)}, f32[200,128]{1,0:T(8,128)S(1)}, u32[]{:S(2)}, u32[]{:S(2)}) collective-permute-start(f32[200,128]{1,0:T(8,128)S(1)} %get-tuple-element.17), channel_id=1, source_target_pairs={{0,16},{1,17},{2,18},{3,19},{4,20},{5,21},{6,22},{7,23},{8,24},{9,... | collective-permute-start | bytes 307208 | tf_op jit(solution)/shard_map/ppermute | solution.py:643
  13.8 11.4 %collective-permute-start.1 = (f32[100,128]{1,0:T(8,128)S(1)}, f32[100,128]{1,0:T(8,128)S(1)}, u32[]{:S(2)}, u32[]{:S(2)}) collective-permute-start(f32[100,128]{1,0:T(8,128)S(1)} %get-tuple-element.18), channel_id=1, source_target_pairs={{0,1},{1,0},{2,3},{3,2},{4,5},{5,4},{6,7},{7,6},{8,9},{9,8},{10,11... | collective-permute-start | bytes 153608 | tf_op jit(solution)/shard_map/ppermute | solution.py:643
  13.8 11.4 %collective-permute-start.2 = (f32[100,128]{1,0:T(8,128)S(1)}, f32[100,128]{1,0:T(8,128)S(1)}, u32[]{:S(2)}, u32[]{:S(2)}) collective-permute-start(f32[100,128]{1,0:T(8,128)S(1)} %get-tuple-element.19), channel_id=1, source_target_pairs={{0,15},{1,2},{2,1},{3,4},{4,3},{5,6},{6,5},{7,8},{8,7},{9,10},{10,... | collective-permute-start | bytes 153608 | tf_op jit(solution)/shard_map/ppermute | solution.py:643
  18.2 3.4 %collective-permute-start.3 = (f32[74,128]{1,0:T(8,128)S(1)}, f32[74,128]{1,0:T(8,128)S(1)}, u32[]{:S(2)}, u32[]{:S(2)}) collective-permute-start(f32[74,128]{1,0:T(8,128)S(1)} %get-tuple-element.20), channel_id=1, source_target_pairs={{0,17},{1,16},{2,19},{3,18},{4,21},{5,20},{6,23},{7,22},{8,25},{9,... | collective-permute-start | bytes 113672 | tf_op jit(solution)/shard_map/ppermute | solution.py:643
  18.2 7.0 %collective-permute-start.4 = (f32[74,128]{1,0:T(8,128)S(1)}, f32[74,128]{1,0:T(8,128)S(1)}, u32[]{:S(2)}, u32[]{:S(2)}) collective-permute-start(f32[74,128]{1,0:T(8,128)S(1)} %get-tuple-element.21), channel_id=1, source_target_pairs={{0,31},{1,18},{2,17},{3,20},{4,19},{5,22},{6,21},{7,24},{8,23},{9,... | collective-permute-start | bytes 113672 | tf_op jit(solution)/shard_map/ppermute | solution.py:643

commit v3 on v2

--- a/solution.py
+++ b/solution.py
@@ -6,6 +6,7 @@
 from jax.experimental import pallas as pl
 from jax.experimental.pallas import tpu as pltpu
 from jax.sharding import PartitionSpec as P
+
 
 DENSITY_SUBSTEPS = 2
 
@@ -138,7 +139,42 @@
     return parts[0] if planes == 1 else jnp.concatenate(parts, axis=1)
 
 
-def pack_kernel(plan, density_in, populations_in, send, moments, density, populations, window, pieces, sems):
+def fill_edges(plan, density, populations, moments, to_x, near, far, near_x, far_x):
+    even = lax.axis_index("gy") % 2 == 0
+
+    def both(first, second, at, up, down):
+        put(first, at, jnp.where(even, up, down))
+        return put(second, at, jnp.where(even, down, up))
+
+    at = plan.x * plan.y
+    for x in range(plan.x):
+        to_x[x * plan.y : (x + 1) * plan.y, :] = density[x]
+        up, down = density[x, plan.y - ROWS :, :], density[x, :ROWS, :]
+        both(near, far, x * ROWS, up, down)
+        both(near_x, far_x, x * ROWS, up, down)
+    for x, jump in ((plan.xc - 1, 1), (0, -1)):
+        for f in range(MOMENTS):
+            at = put(to_x, at, moments[f, x])
+        for q in moving(jump_x=jump):
+            at = put(to_x, at, populations[q, x])
+    last = slice(plan.zc - 1, plan.zc)
+    first = slice(0, 1)
+    at = plan.x * ROWS
+    for x in range(plan.xc):
+        for f in range(MOMENTS):
+            at = both(near, far, at, moments[f, x, last], moments[f, x, first])
+        for up, down in zip(moving(jump_z=1), moving(jump_z=-1), strict=True):
+            at = both(near, far, at, populations[up, x, last], populations[down, x, first])
+    at = plan.x * ROWS
+    for x, jump_x in ((plan.xc - 1, 1), (0, -1)):
+        for f in range(MOMENTS):
+            at = both(near_x, far_x, at, moments[f, x, last], moments[f, x, first])
+        for up, down in zip(moving(jump_x, 1), moving(jump_x, -1), strict=True):
+            at = both(near_x, far_x, at, populations[up, x, last], populations[down, x, first])
+
+
+def pack_kernel(plan, density_in, populations_in, send, moments, *rest):
+    edges, (density, populations, window, pieces, sems) = rest[:5], rest[5:]
     fetch_density = pltpu.make_async_copy(density_in, density, sems.at[0])
     fetch_populations = pltpu.make_async_copy(populations_in, populations, sems.at[1])
     fetch_density.start()
@@ -199,42 +235,9 @@
         if left:
             pieces[target, plan.rows - left :, :] = jnp.zeros((left, LANES), jnp.float32)
     going += deliver(early, plan.rows, 2 + copies)
+    fill_edges(plan, density, populations, moments, *edges)
     for copy in going:
         copy.wait()
-
-
-def edge_kernel(plan, index, density, populations, moments, to_x, near, far, near_x, far_x):
-    even = index[1] == 0
-
-    def both(first, second, at, up, down):
-        put(first, at, jnp.where(even, up, down))
-        return put(second, at, jnp.where(even, down, up))
-
-    at = plan.x * plan.y
-    for x in range(plan.x):
-        to_x[x * plan.y : (x + 1) * plan.y, :] = density[x]
-        up, down = density[x, plan.y - ROWS :, :], density[x, :ROWS, :]
-        both(near, far, x * ROWS, up, down)
-        both(near_x, far_x, x * ROWS, up, down)
-    for x, jump in ((plan.xc - 1, 1), (0, -1)):
-        for f in range(MOMENTS):
-            at = put(to_x, at, moments[f, x])
-        for q in moving(jump_x=jump):
-            at = put(to_x, at, populations[q, x])
-    last = slice(plan.zc - 1, plan.zc)
-    first = slice(0, 1)
-    at = plan.x * ROWS
-    for x in range(plan.xc):
-        for f in range(MOMENTS):
-            at = both(near, far, at, moments[f, x, last], moments[f, x, first])
-        for up, down in zip(moving(jump_z=1), moving(jump_z=-1), strict=True):
-            at = both(near, far, at, populations[up, x, last], populations[down, x, first])
-    at = plan.x * ROWS
-    for x, jump_x in ((plan.xc - 1, 1), (0, -1)):
-        for f in range(MOMENTS):
-            at = both(near_x, far_x, at, moments[f, x, last], moments[f, x, first])
-        for up, down in zip(moving(jump_x, 1), moving(jump_x, -1), strict=True):
-            at = both(near_x, far_x, at, populations[up, x, last], populations[down, x, first])
 
 
 def gather_solvent(plan, populations, moments, halo, field, member):
@@ -377,11 +380,11 @@
             drift[here] = total[rows]
 
 
-def prepare_kernel(plan, index, density, populations, moments, *rest):
+def prepare_kernel(plan, density, populations, moments, *rest):
     neighbours = 5 if plan.pair else 8
     buffers, rest = rest[:neighbours], rest[neighbours:]
     base, slope, drift, push, field, member, grid, lap, pot = rest
-    even = index[1] == 0
+    even = lax.axis_index("gy") % 2 == 0
 
     def plain(ref):
         return lambda at, rows, planes: take(ref, at, rows, planes)
@@ -590,11 +593,11 @@
             out[x] = value[own_row : own_row + plan.y]
 
 
-def update_kernel(plan, index, received, base, slope, drift, push, field, member, *rest):
+def update_kernel(plan, received, base, slope, drift, push, field, member, *rest):
     density_next, populations_next = rest[:2]
     side_grid, side_lap, side_pot, pooled, forces, flow, column, beside, grid, lap, pot = rest[2:13]
     density_out, populations_out, sems = rest[13:]
-    mine = index[0]
+    mine = lax.axis_index("gx")
 
     def place(block):
         if not plan.pair:
@@ -615,10 +618,10 @@
     give_density.wait()
 
 
-VMEM, SMEM, HBM = pltpu.VMEM, pltpu.SMEM, pltpu.HBM
-
-
-def call(kernel, arguments, outputs, scratch, sems=0, cost=None):
+VMEM, HBM = pltpu.VMEM, pltpu.HBM
+
+
+def call(kernel, arguments, outputs, scratch, sems=0, limit=16 * 1024 * 1024):
     return pl.pallas_call(
         kernel,
         out_shape=[jax.ShapeDtypeStruct(shape, jnp.float32) for shape, _ in outputs],
@@ -626,8 +629,7 @@
         out_specs=[pl.BlockSpec(memory_space=space) for _, space in outputs],
         scratch_shapes=[pltpu.VMEM(shape, jnp.float32) for shape in scratch]
         + ([pltpu.SemaphoreType.DMA((sems,))] if sems else []),
-        compiler_params=pltpu.CompilerParams(vmem_limit_bytes=16 * 1024 * 1024),
-        cost_estimate=cost,
+        compiler_params=pltpu.CompilerParams(vmem_limit_bytes=limit),
     )(*[value for value, _ in arguments])
 
 
@@ -683,14 +685,14 @@
 def local(density, populations):
     plan = Plan(lax.axis_size("gx"), lax.axis_size("gy"), density, populations)
     copies = plan.gx if plan.pair else 1
-    index = jnp.stack([lax.axis_index("gx"), lax.axis_index("gy") % 2]).astype(jnp.int32)
-    send, moments = call(
+    send, moments, *edges = call(
         functools.partial(pack_kernel, plan),
         [(density, HBM), (populations, HBM)],
         [
             ((copies, plan.gy, plan.rows, LANES), HBM),
             ((MOMENTS, plan.xc, plan.zc, plan.yc), VMEM),
-        ],
+        ]
+        + [((rows, LANES), VMEM) for rows in (plan.rows_x,) + (plan.rows_y,) * 2 + (plan.rows_d,) * 2],
         [
             density.shape,
             populations.shape,
@@ -698,14 +700,9 @@
             (plan.gy, plan.rows, LANES),
         ],
         sems=2 + 2 * copies,
+        limit=None,
     )
-    own = [(index, SMEM), (density, VMEM), (populations, VMEM), (moments, VMEM)]
-    edges = call(
-        functools.partial(edge_kernel, plan),
-        own,
-        [((rows, LANES), VMEM) for rows in (plan.rows_x,) + (plan.rows_y,) * 2 + (plan.rows_d,) * 2],
-        [],
-    )
+    own = [(density, VMEM), (populations, VMEM), (moments, VMEM)]
     received, halo = exchange(plan, send, *edges)
     tall = (plan.layers, plan.y + 2 * ROWS, plan.z)
     short = (plan.layers, plan.frame, plan.z)
@@ -725,7 +722,7 @@
     side = (2, plan.planes, plan.window * plan.layers, LANES)
     return call(
         functools.partial(update_kernel, plan),
-        [(index, SMEM), (received, VMEM)] + [(value, VMEM) for value in prepared],
+        [(received, VMEM)] + [(value, VMEM) for value in prepared],
         [(density.shape, HBM), (populations.shape, HBM)],
         [
             side,

time: 30.8 us -> 29.4 us (0.955)
  local copies, waits for them, and re-layouts: 1.76 us -> 0.04 us
  waiting for transfers between devices: 5.31 us -> 5.92 us
  Pallas kernels: 7.45 us -> 7.12 us
    unnamed x8 -> x16, local copies, waits for them, and re-layouts: 1.76 us -> 0.04 us
    ppermute x5, waiting for transfers between devices: 5.31 us -> 5.91 us  [shifted(): return lax.ppermute(value, everywhere, pairs)]
    pallas_call x4 -> x3, Pallas kernels: 7.45 us -> 7.12 us  [call(): pl.pallas_call(kernel, out_shape=[jax.ShapeDtypeStruct(shape, jnp.float32...]
  transfers between devices with their start and end apart: 6 -> 6, of which waited for: 2 -> 2; matrix products, arithmetic and copies ran while one was open for 0% -> 0% of each run, Pallas kernels for 8% -> 5%
where the time goes in v3:
time: 29.4 us; the launch traced here: 29.1 us
  starting transfers between devices  15.3 us (52%)
  Pallas kernels  7.12 us (24%)
  waiting for transfers between devices  5.92 us (20%)
  between operations  0.77 us (3%)
    ppermute x5, starting transfers between devices, shifted(): return lax.ppermute(value, everywhere, pairs)  7.93 us
    all_to_all x1, starting transfers between devices, exchange(): lax.all_to_all(send.reshape(plan.gx * plan.gy, plan.rows, LANES), everywh...  7.33 us
    pallas_call x3, Pallas kernels, call(): pl.pallas_call(kernel, out_shape=[jax.ShapeDtypeStruct(shape, jnp.float32...  7.12 us
    ppermute x5, waiting for transfers between devices, shifted(): return lax.ppermute(value, everywhere, pairs)  5.91 us
  transfers between devices with their start and end apart: 6, of which 2 were waited for; matrix products, arithmetic and copies ran while one was open for 0% of the time, Pallas kernels for 5%

profile of v3, /device:TPU:0, one launch (start us, length us, event | category | flops | bytes accessed | tf_op | source)
XLA Modules:
  0.0 29.1 jit_solution(13509704041561083222)
XLA Ops:
  0.6 2.8 %shard_map.41 = (f32[2,16,24,128]{3,2,1,0:T(8,128)}, f32[4,4,4,128]{3,2,1,0:T(4,128)}, f32[200,128]{1,0:T(8,128)}, f32[100,128]{1,0:T(8,128)}, f32[100,128]{1,0:...) custom-call(f32[8,16,128]{2,1,0:T(8,128)} %density.1, f32[19,4,4,128]{3,2,1,0:T(4,128)} %populations.1), custom_call_target="tpu_custom_call" | custom-call | tf_op jit(solution)/shard_map/pallas_call | solution.py:625
  3.5 0.0 copy-start.3
  3.5 0.0 copy-start.5
  3.5 0.0 copy-start.4
  3.5 0.0 copy-start.7
  3.5 0.0 copy-start.6
  3.5 0.0 copy-start
  3.5 0.0 copy-start.1
  3.6 0.0 copy-start.2
  3.6 7.3 %all-to-all-start = ((f32[32,24,128]{2,1,0:T(8,128)}), f32[32,24,128]{2,1,0:T(8,128)S(1)}, u32[]{:S(2)}, u32[]{:S(2)}) async-start(f32[32,24,128]{2,1,0:T(8,128)} %bitcast.3), calls=%async_computation | async-start | bytes 786432 | tf_op jit(solution)/shard_map/all_to_all | solution.py:657
  10.9 0.0 copy-done.3
  10.9 1.8 %collective-permute-start = (f32[200,128]{1,0:T(8,128)S(1)}, f32[200,128]{1,0:T(8,128)S(1)}, u32[]{:S(2)}, u32[]{:S(2)}) collective-permute-start(f32[200,128]{1,0:T(8,128)S(1)} %copy-done.3), channel_id=1, source_target_pairs={{0,16},{1,17},{2,18},{3,19},{4,20},{5,21},{6,22},{7,23},{8,24},{9,... | collective-permute-start | bytes 307208 | tf_op jit(solution)/shard_map/ppermute | solution.py:645
  12.8 0.0 copy-done.5
  12.8 0.0 collective-permute-start.1
  12.8 0.0 copy-done.4
  12.8 4.4 %collective-permute-start.2 = (f32[100,128]{1,0:T(8,128)S(1)}, f32[100,128]{1,0:T(8,128)S(1)}, u32[]{:S(2)}, u32[]{:S(2)}) collective-permute-start(f32[100,128]{1,0:T(8,128)S(1)} %copy-done.4), channel_id=1, source_target_pairs={{0,15},{1,2},{2,1},{3,4},{4,3},{5,6},{6,5},{7,8},{8,7},{9,10},{10,... | collective-permute-start | bytes 153608 | tf_op jit(solution)/shard_map/ppermute | solution.py:645
  17.1 0.0 copy-done.7
  17.1 0.0 collective-permute-start.3
  17.1 0.0 copy-done.6
  17.1 1.7 %collective-permute-start.4 = (f32[74,128]{1,0:T(8,128)S(1)}, f32[74,128]{1,0:T(8,128)S(1)}, u32[]{:S(2)}, u32[]{:S(2)}) collective-permute-start(f32[74,128]{1,0:T(8,128)S(1)} %copy-done.6), channel_id=1, source_target_pairs={{0,31},{1,18},{2,17},{3,20},{4,19},{5,22},{6,21},{7,24},{8,23},{9,... | collective-permute-start | bytes 113672 | tf_op jit(solution)/shard_map/ppermute | solution.py:645
  18.9 1.7 %collective-permute-done.3.rest_3_ = f32[74,128]{1,0:T(8,128)S(1)} collective-permute-done((f32[74,128]{1,0:T(8,128)S(1)}, f32[74,128]{1,0:T(8,128)S(1)}, u32[]{:S(2)}, u32[]{:S(2)}) %collective-permute-start.3) | collective-permute-done | bytes 37920 | tf_op jit(solution)/shard_map/ppermute | solution.py:645
  20.6 4.2 %collective-permute-done.4.rest_4_ = f32[74,128]{1,0:T(8,128)S(1)} collective-permute-done((f32[74,128]{1,0:T(8,128)S(1)}, f32[74,128]{1,0:T(8,128)S(1)}, u32[]{:S(2)}, u32[]{:S(2)}) %collective-permute-start.4) | collective-permute-done | bytes 37920 | tf_op jit(solution)/shard_map/ppermute | solution.py:645
  24.8 0.0 collective-permute-done.1.rest_1_
  24.8 0.0 collective-permute-done.2.rest_2_
  24.8 0.0 collective-permute-done.rest_0_
  24.8 0.0 copy-done
  24.8 0.0 copy-done.1
  24.8 0.0 copy-done.2
  24.8 1.5 %shard_map.42 = (f32[16,24,128]{2,1,0:T(8,128)S(1)}, f32[3,16,24,128]{3,2,1,0:T(8,128)S(1)}, f32[16,24,128]{2,1,0:T(8,128)S(1)}, f32[3,4,24,128]{3,2,1,0:T(8,128...) custom-call(f32[8,16,128]{2,1,0:T(8,128)S(1)} %copy-done.1, f32[19,4,4,128]{3,2,1,0:T(4,128)S(1)} %copy-done, ...), custom_call_target="tpu_custom_call" | custom-call | tf_op jit(solution)/shard_map/pallas_call | solution.py:625
  26.3 0.0 all-to-all-done
  26.3 2.8 %shard_map.43 = (f32[8,16,128]{2,1,0:T(8,128)}, f32[19,4,4,128]{3,2,1,0:T(4,128)}) custom-call(f32[2,16,24,128]{3,2,1,0:T(8,128)S(1)} %bitcast.2, f32[16,24,128]{2,1,0:T(8,128)S(1)} %get-tuple-element.22.base, f32[3,16,24,128]{3,2,1,0:T(8,128)S(1)} %get-tuple-element.23.slope, f32[16,24,128]{2,1,0:T(8,128)S(1)} %get-tuple-element.24.drift, ...), custom_call_target="tpu_custom_call" | custom-call | tf_op jit(solution)/shard_map/pallas_call | solution.py:625
Async XLA Ops:
  3.5 7.4 %copy-start.3 = (f32[200,128]{1,0:T(8,128)S(1)}, f32[200,128]{1,0:T(8,128)}, u32[]{:S(2)}) copy-start(f32[200,128]{1,0:T(8,128)} %get-tuple-element.17) | copy-start | bytes 307204
  3.5 9.3 %copy-start.5 = (f32[100,128]{1,0:T(8,128)S(1)}, f32[100,128]{1,0:T(8,128)}, u32[]{:S(2)}) copy-start(f32[100,128]{1,0:T(8,128)} %get-tuple-element.18) | copy-start | bytes 153604
  3.5 9.3 %copy-start.4 = (f32[100,128]{1,0:T(8,128)S(1)}, f32[100,128]{1,0:T(8,128)}, u32[]{:S(2)}) copy-start(f32[100,128]{1,0:T(8,128)} %get-tuple-element.19) | copy-start | bytes 153604
  3.5 13.6 %copy-start.7 = (f32[74,128]{1,0:T(8,128)S(1)}, f32[74,128]{1,0:T(8,128)}, u32[]{:S(2)}) copy-start(f32[74,128]{1,0:T(8,128)} %get-tuple-element.20) | copy-start | bytes 113668
  3.5 13.6 %copy-start.6 = (f32[74,128]{1,0:T(8,128)S(1)}, f32[74,128]{1,0:T(8,128)}, u32[]{:S(2)}) copy-start(f32[74,128]{1,0:T(8,128)} %get-tuple-element.21) | copy-start | bytes 113668
  3.5 21.3 %copy-start = (f32[19,4,4,128]{3,2,1,0:T(4,128)S(1)}, f32[19,4,4,128]{3,2,1,0:T(4,128)}, u32[]{:S(2)}) copy-start(f32[19,4,4,128]{3,2,1,0:T(4,128)} %populations.1) | copy-start | bytes 466948
  3.5 21.3 %copy-start.1 = (f32[8,16,128]{2,1,0:T(8,128)S(1)}, f32[8,16,128]{2,1,0:T(8,128)}, u32[]{:S(2)}) copy-start(f32[8,16,128]{2,1,0:T(8,128)} %density.1) | copy-start | bytes 196612
  3.6 21.3 %copy-start.2 = (f32[4,4,4,128]{3,2,1,0:T(4,128)S(1)}, f32[4,4,4,128]{3,2,1,0:T(4,128)}, u32[]{:S(2)}) copy-start(f32[4,4,4,128]{3,2,1,0:T(4,128)} %get-tuple-element.16.moments) | copy-start | bytes 98308
  3.6 22.7 %all-to-all-start = ((f32[32,24,128]{2,1,0:T(8,128)}), f32[32,24,128]{2,1,0:T(8,128)S(1)}, u32[]{:S(2)}, u32[]{:S(2)}) async-start(f32[32,24,128]{2,1,0:T(8,128)} %bitcast.3), calls=%async_computation | async-start | bytes 786432 | tf_op jit(solution)/shard_map/all_to_all | solution.py:657
  10.9 13.9 %collective-permute-start = (f32[200,128]{1,0:T(8,128)S(1)}, f32[200,128]{1,0:T(8,128)S(1)}, u32[]{:S(2)}, u32[]{:S(2)}) collective-permute-start(f32[200,128]{1,0:T(8,128)S(1)} %copy-done.3), channel_id=1, source_target_pairs={{0,16},{1,17},{2,18},{3,19},{4,20},{5,21},{6,22},{7,23},{8,24},{9,... | collective-permute-start | bytes 307208 | tf_op jit(solution)/shard_map/ppermute | solution.py:645
  12.8 12.0 %collective-permute-start.1 = (f32[100,128]{1,0:T(8,128)S(1)}, f32[100,128]{1,0:T(8,128)S(1)}, u32[]{:S(2)}, u32[]{:S(2)}) collective-permute-start(f32[100,128]{1,0:T(8,128)S(1)} %copy-done.5), channel_id=1, source_target_pairs={{0,1},{1,0},{2,3},{3,2},{4,5},{5,4},{6,7},{7,6},{8,9},{9,8},{10,11... | collective-permute-start | bytes 153608 | tf_op jit(solution)/shard_map/ppermute | solution.py:645
  12.8 12.0 %collective-permute-start.2 = (f32[100,128]{1,0:T(8,128)S(1)}, f32[100,128]{1,0:T(8,128)S(1)}, u32[]{:S(2)}, u32[]{:S(2)}) collective-permute-start(f32[100,128]{1,0:T(8,128)S(1)} %copy-done.4), channel_id=1, source_target_pairs={{0,15},{1,2},{2,1},{3,4},{4,3},{5,6},{6,5},{7,8},{8,7},{9,10},{10,... | collective-permute-start | bytes 153608 | tf_op jit(solution)/shard_map/ppermute | solution.py:645
  17.1 3.4 %collective-permute-start.3 = (f32[74,128]{1,0:T(8,128)S(1)}, f32[74,128]{1,0:T(8,128)S(1)}, u32[]{:S(2)}, u32[]{:S(2)}) collective-permute-start(f32[74,128]{1,0:T(8,128)S(1)} %copy-done.7), channel_id=1, source_target_pairs={{0,17},{1,16},{2,19},{3,18},{4,21},{5,20},{6,23},{7,22},{8,25},{9,... | collective-permute-start | bytes 113672 | tf_op jit(solution)/shard_map/ppermute | solution.py:645
  17.1 7.6 %collective-permute-start.4 = (f32[74,128]{1,0:T(8,128)S(1)}, f32[74,128]{1,0:T(8,128)S(1)}, u32[]{:S(2)}, u32[]{:S(2)}) collective-permute-start(f32[74,128]{1,0:T(8,128)S(1)} %copy-done.6), channel_id=1, source_target_pairs={{0,31},{1,18},{2,17},{3,20},{4,19},{5,22},{6,21},{7,24},{8,23},{9,... | collective-permute-start | bytes 113672 | tf_op jit(solution)/shard_map/ppermute | solution.py:645

commit v4 on v3

--- a/solution.py
+++ b/solution.py
@@ -139,7 +139,7 @@
     return parts[0] if planes == 1 else jnp.concatenate(parts, axis=1)
 
 
-def fill_edges(plan, density, populations, moments, to_x, near, far, near_x, far_x):
+def edge_kernel(plan, density, populations, moments, to_x, near, far, near_x, far_x):
     even = lax.axis_index("gy") % 2 == 0
 
     def both(first, second, at, up, down):
@@ -173,8 +173,7 @@
             at = both(near_x, far_x, at, populations[up, x, last], populations[down, x, first])
 
 
-def pack_kernel(plan, density_in, populations_in, send, moments, *rest):
-    edges, (density, populations, window, pieces, sems) = rest[:5], rest[5:]
+def pack_kernel(plan, density_in, populations_in, send, moments, density, populations, window, pieces, sems):
     fetch_density = pltpu.make_async_copy(density_in, density, sems.at[0])
     fetch_populations = pltpu.make_async_copy(populations_in, populations, sems.at[1])
     fetch_density.start()
@@ -235,7 +234,6 @@
         if left:
             pieces[target, plan.rows - left :, :] = jnp.zeros((left, LANES), jnp.float32)
     going += deliver(early, plan.rows, 2 + copies)
-    fill_edges(plan, density, populations, moments, *edges)
     for copy in going:
         copy.wait()
 
@@ -685,14 +683,13 @@
 def local(density, populations):
     plan = Plan(lax.axis_size("gx"), lax.axis_size("gy"), density, populations)
     copies = plan.gx if plan.pair else 1
-    send, moments, *edges = call(
+    send, moments = call(
         functools.partial(pack_kernel, plan),
         [(density, HBM), (populations, HBM)],
         [
             ((copies, plan.gy, plan.rows, LANES), HBM),
             ((MOMENTS, plan.xc, plan.zc, plan.yc), VMEM),
-        ]
-        + [((rows, LANES), VMEM) for rows in (plan.rows_x,) + (plan.rows_y,) * 2 + (plan.rows_d,) * 2],
+        ],
         [
             density.shape,
             populations.shape,
@@ -703,6 +700,12 @@
         limit=None,
     )
     own = [(density, VMEM), (populations, VMEM), (moments, VMEM)]
+    edges = call(
+        functools.partial(edge_kernel, plan),
+        own,
+        [((rows, LANES), VMEM) for rows in (plan.rows_x,) + (plan.rows_y,) * 2 + (plan.rows_d,) * 2],
+        [],
+    )
     received, halo = exchange(plan, send, *edges)
     tall = (plan.layers, plan.y + 2 * ROWS, plan.z)
     short = (plan.layers, plan.frame, plan.z)

time: 29.4 us -> 29.1 us (0.990)
    pallas_call x3 -> x4, Pallas kernels: 7.12 us -> 7.03 us  [call(): pl.pallas_call(kernel, out_shape=[jax.ShapeDtypeStruct(shape, jnp.float32...]
where the time goes in v4:
time: 29.1 us; the launch traced here: 28.9 us
  starting transfers between devices  15.3 us (53%)
  Pallas kernels  7.03 us (24%)
  waiting for transfers between devices  5.85 us (20%)
  between operations  0.72 us (2%)
    ppermute x5, starting transfers between devices, shifted(): return lax.ppermute(value, everywhere, pairs)  7.94 us
    all_to_all x1, starting transfers between devices, exchange(): lax.all_to_all(send.reshape(plan.gx * plan.gy, plan.rows, LANES), everywh...  7.33 us
    pallas_call x4, Pallas kernels, call(): pl.pallas_call(kernel, out_shape=[jax.ShapeDtypeStruct(shape, jnp.float32...  7.03 us
    ppermute x5, waiting for transfers between devices, shifted(): return lax.ppermute(value, everywhere, pairs)  5.84 us
  transfers between devices with their start and end apart: 6, of which 2 were waited for; matrix products, arithmetic and copies ran while one was open for 0% of the time, Pallas kernels for 5%

profile of v4, /device:TPU:0, one launch (start us, length us, event | category | flops | bytes accessed | tf_op | source)
XLA Modules:
  0.0 28.9 jit_solution(9769203185512561930)
XLA Ops:
  0.6 2.7 %shard_map.41 = (f32[2,16,24,128]{3,2,1,0:T(8,128)}, f32[4,4,4,128]{3,2,1,0:T(4,128)}) custom-call(f32[8,16,128]{2,1,0:T(8,128)} %density.3, f32[19,4,4,128]{3,2,1,0:T(4,128)} %populations.3), custom_call_target="tpu_custom_call" | custom-call | tf_op jit(solution)/shard_map/pallas_call | solution.py:623
  3.3 0.0 copy-start
  3.3 0.0 copy-start.1
  3.4 0.0 copy-start.2
  3.4 7.3 %all-to-all-start = ((f32[32,24,128]{2,1,0:T(8,128)}), f32[32,24,128]{2,1,0:T(8,128)S(1)}, u32[]{:S(2)}, u32[]{:S(2)}) async-start(f32[32,24,128]{2,1,0:T(8,128)} %bitcast.3), calls=%async_computation | async-start | bytes 786432 | tf_op jit(solution)/shard_map/all_to_all | solution.py:655
  10.7 0.0 copy-done
  10.7 0.0 copy-done.1
  10.7 0.0 copy-done.2
  10.7 0.1 shard_map.42
  10.8 1.8 %collective-permute-start = (f32[200,128]{1,0:T(8,128)S(1)}, f32[200,128]{1,0:T(8,128)S(1)}, u32[]{:S(2)}, u32[]{:S(2)}) collective-permute-start(f32[200,128]{1,0:T(8,128)S(1)} %get-tuple-element.17), channel_id=1, source_target_pairs={{0,16},{1,17},{2,18},{3,19},{4,20},{5,21},{6,22},{7,23},{8,24},{9,... | collective-permute-start | bytes 307208 | tf_op jit(solution)/shard_map/ppermute | solution.py:643
  12.6 0.0 collective-permute-start.1
  12.6 4.4 %collective-permute-start.2 = (f32[100,128]{1,0:T(8,128)S(1)}, f32[100,128]{1,0:T(8,128)S(1)}, u32[]{:S(2)}, u32[]{:S(2)}) collective-permute-start(f32[100,128]{1,0:T(8,128)S(1)} %get-tuple-element.19), channel_id=1, source_target_pairs={{0,15},{1,2},{2,1},{3,4},{4,3},{5,6},{6,5},{7,8},{8,7},{9,10},{10,... | collective-permute-start | bytes 153608 | tf_op jit(solution)/shard_map/ppermute | solution.py:643
  17.0 0.0 collective-permute-start.3
  17.0 1.7 %collective-permute-start.4 = (f32[74,128]{1,0:T(8,128)S(1)}, f32[74,128]{1,0:T(8,128)S(1)}, u32[]{:S(2)}, u32[]{:S(2)}) collective-permute-start(f32[74,128]{1,0:T(8,128)S(1)} %get-tuple-element.21), channel_id=1, source_target_pairs={{0,31},{1,18},{2,17},{3,20},{4,19},{5,22},{6,21},{7,24},{8,23},{9,... | collective-permute-start | bytes 113672 | tf_op jit(solution)/shard_map/ppermute | solution.py:643
  18.7 1.8 %collective-permute-done.3.rest_3_ = f32[74,128]{1,0:T(8,128)S(1)} collective-permute-done((f32[74,128]{1,0:T(8,128)S(1)}, f32[74,128]{1,0:T(8,128)S(1)}, u32[]{:S(2)}, u32[]{:S(2)}) %collective-permute-start.3) | collective-permute-done | bytes 37920 | tf_op jit(solution)/shard_map/ppermute | solution.py:643
  20.5 4.1 %collective-permute-done.4.rest_4_ = f32[74,128]{1,0:T(8,128)S(1)} collective-permute-done((f32[74,128]{1,0:T(8,128)S(1)}, f32[74,128]{1,0:T(8,128)S(1)}, u32[]{:S(2)}, u32[]{:S(2)}) %collective-permute-start.4) | collective-permute-done | bytes 37920 | tf_op jit(solution)/shard_map/ppermute | solution.py:643
  24.6 0.0 collective-permute-done.1.rest_1_
  24.6 0.0 collective-permute-done.2.rest_2_
  24.6 0.0 collective-permute-done.rest_0_
  24.6 1.5 %shard_map.43 = (f32[16,24,128]{2,1,0:T(8,128)S(1)}, f32[3,16,24,128]{3,2,1,0:T(8,128)S(1)}, f32[16,24,128]{2,1,0:T(8,128)S(1)}, f32[3,4,24,128]{3,2,1,0:T(8,128...) custom-call(f32[8,16,128]{2,1,0:T(8,128)S(1)} %copy-done.1, f32[19,4,4,128]{3,2,1,0:T(4,128)S(1)} %copy-done, ...), custom_call_target="tpu_custom_call" | custom-call | tf_op jit(solution)/shard_map/pallas_call | solution.py:623
  26.1 0.0 all-to-all-done
  26.1 2.8 %shard_map.44 = (f32[8,16,128]{2,1,0:T(8,128)}, f32[19,4,4,128]{3,2,1,0:T(4,128)}) custom-call(f32[2,16,24,128]{3,2,1,0:T(8,128)S(1)} %bitcast.2, f32[16,24,128]{2,1,0:T(8,128)S(1)} %get-tuple-element.22.base, f32[3,16,24,128]{3,2,1,0:T(8,128)S(1)} %get-tuple-element.23.slope, f32[16,24,128]{2,1,0:T(8,128)S(1)} %get-tuple-element.24.drift, ...), custom_call_target="tpu_custom_call" | custom-call | tf_op jit(solution)/shard_map/pallas_call | solution.py:623
Async XLA Ops:
  3.3 7.4 %copy-start = (f32[19,4,4,128]{3,2,1,0:T(4,128)S(1)}, f32[19,4,4,128]{3,2,1,0:T(4,128)}, u32[]{:S(2)}) copy-start(f32[19,4,4,128]{3,2,1,0:T(4,128)} %populations.3) | copy-start | bytes 466948
  3.3 7.4 %copy-start.1 = (f32[8,16,128]{2,1,0:T(8,128)S(1)}, f32[8,16,128]{2,1,0:T(8,128)}, u32[]{:S(2)}) copy-start(f32[8,16,128]{2,1,0:T(8,128)} %density.3) | copy-start | bytes 196612
  3.4 7.4 %copy-start.2 = (f32[4,4,4,128]{3,2,1,0:T(4,128)S(1)}, f32[4,4,4,128]{3,2,1,0:T(4,128)}, u32[]{:S(2)}) copy-start(f32[4,4,4,128]{3,2,1,0:T(4,128)} %get-tuple-element.16.moments) | copy-start | bytes 98308
  3.4 22.7 %all-to-all-start = ((f32[32,24,128]{2,1,0:T(8,128)}), f32[32,24,128]{2,1,0:T(8,128)S(1)}, u32[]{:S(2)}, u32[]{:S(2)}) async-start(f32[32,24,128]{2,1,0:T(8,128)} %bitcast.3), calls=%async_computation | async-start | bytes 786432 | tf_op jit(solution)/shard_map/all_to_all | solution.py:655
  10.8 13.8 %collective-permute-start = (f32[200,128]{1,0:T(8,128)S(1)}, f32[200,128]{1,0:T(8,128)S(1)}, u32[]{:S(2)}, u32[]{:S(2)}) collective-permute-start(f32[200,128]{1,0:T(8,128)S(1)} %get-tuple-element.17), channel_id=1, source_target_pairs={{0,16},{1,17},{2,18},{3,19},{4,20},{5,21},{6,22},{7,23},{8,24},{9,... | collective-permute-start | bytes 307208 | tf_op jit(solution)/shard_map/ppermute | solution.py:643
  12.6 11.9 %collective-permute-start.1 = (f32[100,128]{1,0:T(8,128)S(1)}, f32[100,128]{1,0:T(8,128)S(1)}, u32[]{:S(2)}, u32[]{:S(2)}) collective-permute-start(f32[100,128]{1,0:T(8,128)S(1)} %get-tuple-element.18), channel_id=1, source_target_pairs={{0,1},{1,0},{2,3},{3,2},{4,5},{5,4},{6,7},{7,6},{8,9},{9,8},{10,11... | collective-permute-start | bytes 153608 | tf_op jit(solution)/shard_map/ppermute | solution.py:643
  12.6 11.9 %collective-permute-start.2 = (f32[100,128]{1,0:T(8,128)S(1)}, f32[100,128]{1,0:T(8,128)S(1)}, u32[]{:S(2)}, u32[]{:S(2)}) collective-permute-start(f32[100,128]{1,0:T(8,128)S(1)} %get-tuple-element.19), channel_id=1, source_target_pairs={{0,15},{1,2},{2,1},{3,4},{4,3},{5,6},{6,5},{7,8},{8,7},{9,10},{10,... | collective-permute-start | bytes 153608 | tf_op jit(solution)/shard_map/ppermute | solution.py:643
  17.0 3.5 %collective-permute-start.3 = (f32[74,128]{1,0:T(8,128)S(1)}, f32[74,128]{1,0:T(8,128)S(1)}, u32[]{:S(2)}, u32[]{:S(2)}) collective-permute-start(f32[74,128]{1,0:T(8,128)S(1)} %get-tuple-element.20), channel_id=1, source_target_pairs={{0,17},{1,16},{2,19},{3,18},{4,21},{5,20},{6,23},{7,22},{8,25},{9,... | collective-permute-start | bytes 113672 | tf_op jit(solution)/shard_map/ppermute | solution.py:643
  17.0 7.6 %collective-permute-start.4 = (f32[74,128]{1,0:T(8,128)S(1)}, f32[74,128]{1,0:T(8,128)S(1)}, u32[]{:S(2)}, u32[]{:S(2)}) collective-permute-start(f32[74,128]{1,0:T(8,128)S(1)} %get-tuple-element.21), channel_id=1, source_target_pairs={{0,31},{1,18},{2,17},{3,20},{4,19},{5,22},{6,21},{7,24},{8,23},{9,... | collective-permute-start | bytes 113672 | tf_op jit(solution)/shard_map/ppermute | solution.py:643

commit v5 on v4

--- a/solution.py
+++ b/solution.py
@@ -68,15 +68,19 @@
         self.blocks = 2 if self.pair else 3
         self.planes = self.yc // LANES
         self.layers = self.blocks * self.x
+        self.pitch = self.layers + 2
         self.frame = self.y + ROWS
+        self.strip = ROWS - 1
+        self.corner = [self.strip - min(x + 1, self.x - x) for x in range(self.x)]
+        self.corner_rows = sum(self.corner)
         self.coarse_layers = self.blocks * self.xc
         assert self.x * self.y == LANES and MOMENTS * self.xc * self.yb == LANES
         assert self.z == LANES and self.yc % LANES == 0 and self.zc % 2 == 0
         assert self.window + self.zc + self.half <= WINDOW_ROWS and self.zc + 2 <= ROWS
         wide = self.planes
         self.rows_x = self.x * self.y + 2 * 9 * self.zc * wide
-        self.rows_y = self.x * ROWS + 9 * self.xc * wide
-        self.rows_d = self.x * ROWS + 2 * 5 * wide
+        self.rows_y = self.x * self.strip + 9 * self.xc * wide
+        self.rows_d = self.corner_rows + 2 * 5 * wide
 
     def layer(self, x):
         return x % self.layers if self.pair else x + self.x
@@ -149,9 +153,11 @@
     at = plan.x * plan.y
     for x in range(plan.x):
         to_x[x * plan.y : (x + 1) * plan.y, :] = density[x]
-        up, down = density[x, plan.y - ROWS :, :], density[x, :ROWS, :]
-        both(near, far, x * ROWS, up, down)
-        both(near_x, far_x, x * ROWS, up, down)
+        for first, second, start, rows in (
+            (near, far, x * plan.strip, plan.strip),
+            (near_x, far_x, sum(plan.corner[:x]), plan.corner[x]),
+        ):
+            both(first, second, start, density[x, plan.y - rows :, :], density[x, :rows, :])
     for x, jump in ((plan.xc - 1, 1), (0, -1)):
         for f in range(MOMENTS):
             at = put(to_x, at, moments[f, x])
@@ -159,13 +165,13 @@
             at = put(to_x, at, populations[q, x])
     last = slice(plan.zc - 1, plan.zc)
     first = slice(0, 1)
-    at = plan.x * ROWS
+    at = plan.x * plan.strip
     for x in range(plan.xc):
         for f in range(MOMENTS):
             at = both(near, far, at, moments[f, x, last], moments[f, x, first])
         for up, down in zip(moving(jump_z=1), moving(jump_z=-1), strict=True):
             at = both(near, far, at, populations[up, x, last], populations[down, x, first])
-    at = plan.x * ROWS
+    at = plan.corner_rows
     for x, jump_x in ((plan.xc - 1, 1), (0, -1)):
         for f in range(MOMENTS):
             at = both(near_x, far_x, at, moments[f, x, last], moments[f, x, first])
@@ -250,7 +256,7 @@
             target[lead + (slice(plan.zc, plan.zc + 1),)] = value_above
 
     for x in range(plan.xc):
-        at = plan.x * ROWS + x * 9 * width
+        at = plan.x * plan.strip + x * 9 * width
         for f in range(MOMENTS):
             store(
                 field,
@@ -275,7 +281,7 @@
         (plan.xc + 1, from_high, False, below_high, above_high, -1),
     ):
         at = plan.x * plan.y + (0 if first else 9 * plan.zc * width)
-        corner = plan.x * ROWS + (0 if first else 5 * width)
+        corner = plan.corner_rows + (0 if first else 5 * width)
         for f in range(MOMENTS):
             store(
                 field,
@@ -298,35 +304,42 @@
             at += plan.zc * width
 
 
-def laplace_at(plan, source, x):
-    value = source[plan.layer(x)]
-    running = -6.0 * value + source[plan.layer(x - 1)] + source[plan.layer(x + 1)]
-    running = running + roll(value, 1, 0) + roll(value, -1, 0)
+def shifted_rows(plan, source, x, part, shift=0):
+    return source[plan.layer(x), ROWS + part.start + shift : ROWS + part.stop + shift, :]
+
+
+def laplace_at(plan, source, x, part):
+    value = shifted_rows(plan, source, x, part)
+    running = -6.0 * value + shifted_rows(plan, source, x - 1, part) + shifted_rows(plan, source, x + 1, part)
+    running = running + shifted_rows(plan, source, x, part, 1) + shifted_rows(plan, source, x, part, -1)
     return running + roll(value, 1, 1) + roll(value, -1, 1)
 
 
-def potential_at(plan, grid, lap, pot, reach):
+def potential_at(plan, grid, lap, pot, reach, part):
+    rows = slice(ROWS + part.start, ROWS + part.stop)
     for x in plan.span(-reach, plan.x + reach):
-        lap[plan.layer(x)] = laplace_at(plan, grid, x)
+        lap[plan.layer(x), rows] = laplace_at(plan, grid, x, part)
     for x in plan.span(1 - reach, plan.x + reach - 1):
         here = plan.layer(x)
-        value = grid[here]
-        pot[here] = (
+        value = grid[here, rows]
+        pot[here, rows] = (
             (quench_depth + 1.0) * value
-            + 2.0 * lap[here]
-            + laplace_at(plan, lap, x)
+            + 2.0 * lap[here, rows]
+            + laplace_at(plan, lap, x, part)
             + value * value * value
         )
 
 
-def central_at(plan, source, x, c):
+def central_at(plan, source, x, c, part):
     if c == 0:
-        return source[plan.layer(x + 1)] - source[plan.layer(x - 1)]
-    value = source[plan.layer(x)]
-    return roll(value, -1, c - 1) - roll(value, 1, c - 1)
-
-
-def first_substep(plan, density, halo, base, slope, drift, push, grid, lap, pot):
+        return shifted_rows(plan, source, x + 1, part) - shifted_rows(plan, source, x - 1, part)
+    if c == 1:
+        return shifted_rows(plan, source, x, part, 1) - shifted_rows(plan, source, x, part, -1)
+    value = shifted_rows(plan, source, x, part)
+    return roll(value, -1, 1) - roll(value, 1, 1)
+
+
+def first_substep(plan, density, halo, base, slope, drift, push, grid, lap, pot, pooled):
     from_low, from_high, from_below, from_above, below_low, below_high, above_low, above_high = halo
     sets = [(0, None, from_below, from_above)]
     if plan.pair:
@@ -334,18 +347,23 @@
     else:
         sets.append((-plan.x, from_low, below_low, above_low))
         sets.append((plan.x, from_high, below_high, above_high))
+    own = 2 * ROWS
     for first, block, below, above in sets:
         for x in range(plan.x):
             here = plan.layer(first + x)
-            grid[here, ROWS : ROWS + plan.y] = (
-                density[x] if block is None else block(x * plan.y, plan.y, 1)
-            )
-            grid[here, :ROWS] = below(x * ROWS, ROWS, 1)
-            grid[here, ROWS + plan.y :] = above(x * ROWS, ROWS, 1)
-    potential_at(plan, grid, lap, pot, 6)
-    shape = grid.shape[1:]
-    odd = [(lax.broadcasted_iota(jnp.int32, shape, c) & 1) != 0 for c in range(2)]
-    rows = slice(ROWS // 2, ROWS // 2 + plan.frame)
+            if block is None:
+                start, rows = x * plan.strip, plan.strip
+                grid[here, own : own + plan.y] = density[x]
+            else:
+                start, rows = sum(plan.corner[:x]), plan.corner[x]
+                grid[here, own : own + plan.y] = block(x * plan.y, plan.y, 1)
+            grid[here, own - rows : own] = below(start, rows, 1)
+            grid[here, own + plan.y : own + plan.y + rows] = above(start, rows, 1)
+    whole = slice(0, plan.y + 2 * ROWS)
+    inner = slice(ROWS // 2, ROWS // 2 + plan.frame)
+    potential_at(plan, grid, lap, pot, 6, whole)
+    pairs = (plan.y + 2 * ROWS) // 2
+    odd = (lax.broadcasted_iota(jnp.int32, (pairs, plan.z), 1) & 1) != 0
     reach = 3 * (DENSITY_SUBSTEPS - 1)
     wanted = {plan.layer(x): x for x in plan.span(-reach, plan.x + reach)}
     done = set()
@@ -354,34 +372,38 @@
         for c in range(3):
             total = None
             for x in (2 * coarse, 2 * coarse + 1):
-                now = grid[plan.layer(x)] * central_at(plan, pot, x, c)
+                now = shifted_rows(plan, grid, x, whole) * central_at(plan, pot, x, c, whole)
                 total = now if total is None else total + now
-            for dimension in range(2):
-                total = total + jnp.where(
-                    odd[dimension], roll(total, 1, dimension), roll(total, -1, dimension)
-                )
-            force.append(total * (-0.25 * force_unit / 8.0))
+            at = c * (plan.xc + 4) + coarse + 2
+            pooled[at] = total
+            even_rows, odd_rows = pl.ds(0, pairs, stride=2), pl.ds(1, pairs, stride=2)
+            total = pooled[at, even_rows, :] + pooled[at, odd_rows, :]
+            total = total + jnp.where(odd, roll(total, 1, 1), roll(total, -1, 1))
+            total = total * (-0.25 * force_unit / 8.0)
+            pooled[at, even_rows, :] = total
+            pooled[at, odd_rows, :] = total
+            force.append(pooled[at, inner, :])
             if 0 <= coarse < plan.xc:
-                push[c, coarse] = force[c][rows]
+                push[c, coarse] = force[c]
         for x in (2 * coarse, 2 * coarse + 1):
             here = plan.layer(x)
             if here not in wanted or here in done:
                 continue
             done.add(here)
-            base[here] = (grid[here] + coupled_time_step * laplace_at(plan, pot, x))[rows]
+            base[here] = shifted_rows(plan, grid, x, inner) + coupled_time_step * laplace_at(plan, pot, x, inner)
             total = None
             for c in range(3):
-                scaled = central_at(plan, grid, x, c) * (0.5 * speed_unit * coupled_time_step)
-                slope[c, here] = scaled[rows]
+                scaled = central_at(plan, grid, x, c, inner) * (0.5 * speed_unit * coupled_time_step)
+                slope[c, here] = scaled
                 now = force[c] * scaled
                 total = now if total is None else total + now
-            drift[here] = total[rows]
+            drift[here] = total
 
 
 def prepare_kernel(plan, density, populations, moments, *rest):
     neighbours = 5 if plan.pair else 8
     buffers, rest = rest[:neighbours], rest[neighbours:]
-    base, slope, drift, push, field, member, grid, lap, pot = rest
+    base, slope, drift, push, field, member, grid, lap, pot, pooled = rest
     even = lax.axis_index("gy") % 2 == 0
 
     def plain(ref):
@@ -410,32 +432,47 @@
         either(near_high, far_high),
     )
     gather_solvent(plan, populations, moments, halo, field, member)
-    first_substep(plan, density, halo, base, slope, drift, push, grid, lap, pot)
+    first_substep(plan, density, halo, base, slope, drift, push, grid, lap, pot, pooled)
 
 
 def solvent_part(plan, place, received, field, member, out, grid, lap, pot, pooled, forces):
     width, layers = plan.planes, plan.layers
     senders = LANES // plan.yb
 
-    def load(source, parity, z):
-        parts = [source[parity, k, z * layers : (z + 1) * layers, :] for k in range(width)]
+    pitch = plan.pitch
+
+    def load(source, parity, z, shift=0):
+        first = z * pitch + 1 + shift
+        parts = [source[parity, k, first : first + layers, :] for k in range(width)]
         return parts[0] if width == 1 else jnp.concatenate(parts, axis=1)
 
     def save(target, parity, z, value):
+        first = z * pitch + 1
         for k in range(width):
-            target[parity, k, z * layers : (z + 1) * layers, :] = value[:, k * LANES : (k + 1) * LANES]
+            part = value[:, k * LANES : (k + 1) * LANES]
+            target[parity, k, first : first + layers, :] = part
+            if plan.pair:
+                target[parity, k, first - 1 : first, :] = part[layers - 1 :]
+                target[parity, k, first + layers : first + layers + 1, :] = part[:1]
 
     for tile in range(pl.cdiv(plan.window, ROWS)):
         count = min(ROWS, plan.window - tile * ROWS)
         for block in range(plan.blocks):
             for plane in range(width):
                 arrays = [
-                    received[place(block), plane * senders + t, tile * ROWS : (tile + 1) * ROWS, :]
+                    received[place(block), plane * senders + t, tile * ROWS : tile * ROWS + count, :]
                     for t in range(senders)
                 ]
                 for g, value in enumerate(butterfly(arrays, plan.yb)):
-                    first = tile * ROWS * layers + block * plan.x + g // 2
-                    grid[g % 2, plane, pl.ds(first, count, stride=layers), :] = value[:count]
+                    layer = block * plan.x + g // 2
+                    places = [layer + 1]
+                    if plan.pair and layer == 0:
+                        places.append(layers + 1)
+                    if plan.pair and layer == layers - 1:
+                        places.append(0)
+                    for row in places:
+                        first = tile * ROWS * pitch + row
+                        grid[g % 2, plane, pl.ds(first, count, stride=pitch), :] = value
 
     def laplace(source, z):
         even, odd = load(source, 0, z), load(source, 1, z)
@@ -444,7 +481,7 @@
         for parity, value in enumerate((even, odd)):
             running = -6.0 * value + load(source, parity, z - 1) + load(source, parity, z + 1)
             running = running + sides[parity]
-            out.append(running + roll(value, 1, 0) + roll(value, -1, 0))
+            out.append(running + load(source, parity, z, -1) + load(source, parity, z, 1))
         return out
 
     for z in range(1, plan.window - 1):
@@ -469,8 +506,8 @@
         for z in (2 * coarse + WINDOW_HALO, 2 * coarse + 1 + WINDOW_HALO):
             even, odd = load(grid, 0, z), load(grid, 1, z)
             pot_even, pot_odd = load(pot, 0, z), load(pot, 1, z)
-            along_x = even * (roll(pot_even, -1, 0) - roll(pot_even, 1, 0)) + odd * (
-                roll(pot_odd, -1, 0) - roll(pot_odd, 1, 0)
+            along_x = even * (load(pot, 0, z, 1) - load(pot, 0, z, -1)) + odd * (
+                load(pot, 1, z, 1) - load(pot, 1, z, -1)
             )
             along_y = even * (pot_odd - roll(pot_odd, 1, 1)) + odd * (roll(pot_even, -1, 1) - pot_even)
             along_z = even * (load(pot, 0, z + 1) - load(pot, 0, z - 1)) + odd * (
@@ -486,13 +523,13 @@
                     pooled[coarse % ROWS, pl.ds(at, coarse_layers, stride=2), :]
                     + pooled[coarse % ROWS, pl.ds(at + 1, coarse_layers, stride=2), :]
                 )
-                forces[c, k, pl.ds(coarse % ROWS, coarse_layers, stride=ROWS), :] = value * scale
+                forces[c, k, pl.ds(coarse % ROWS, coarse_layers, stride=ROWS + 1), :] = value * scale
 
     rate = 1.0 / relax_time
     gain = 1.0 - 0.5 / relax_time
     for slot in range(plan.xc + 2):
         x = slot - 1
-        at = plan.coarse_layer(x) * ROWS
+        at = plan.coarse_layer(x) * (ROWS + 1)
         force = []
         for c in range(3):
             parts = [forces[c, k, at : at + ROWS, :] for k in range(width)]
@@ -577,18 +614,19 @@
         advection = drift[here]
         for c in range(3):
             advection = advection + flow[c + 1, slot] * slope[c, here]
-        grid[here] = base[here] - advection * inverses[slot]
-    potential_at(plan, grid, lap, pot, 2)
+        grid[here, ROWS : ROWS + plan.frame] = base[here] - advection * inverses[slot]
+    whole = slice(0, plan.frame)
+    inner = slice(own_row, own_row + plan.y)
+    potential_at(plan, grid, lap, pot, 2, whole)
     for coarse in range(plan.xc):
         slot = plan.coarse_layer(coarse)
-        scaled = (0.5 * speed_unit) / flow[0, slot]
-        speed = [(flow[c + 1, slot] + push[c, coarse]) * scaled for c in range(3)]
+        scaled = (0.5 * speed_unit) / flow[0, slot, inner]
+        speed = [(flow[c + 1, slot, inner] + push[c, coarse, inner]) * scaled for c in range(3)]
         for x in (2 * coarse, 2 * coarse + 1):
-            change = laplace_at(plan, pot, x)
+            change = laplace_at(plan, pot, x, inner)
             for c in range(3):
-                change = change - speed[c] * central_at(plan, grid, x, c)
-            value = grid[plan.layer(x)] + coupled_time_step * change
-            out[x] = value[own_row : own_row + plan.y]
+                change = change - speed[c] * central_at(plan, grid, x, c, inner)
+            out[x] = shifted_rows(plan, grid, x, inner) + coupled_time_step * change
 
 
 def update_kernel(plan, received, base, slope, drift, push, field, member, *rest):
@@ -707,7 +745,8 @@
         [],
     )
     received, halo = exchange(plan, send, *edges)
-    tall = (plan.layers, plan.y + 2 * ROWS, plan.z)
+    tall = (plan.layers, plan.y + 4 * ROWS, plan.z)
+    spare = (plan.layers, plan.frame + 2 * ROWS, plan.z)
     short = (plan.layers, plan.frame, plan.z)
     prepared = call(
         functools.partial(prepare_kernel, plan),
@@ -720,9 +759,9 @@
             ((MOMENTS, plan.xc + 2, ROWS, plan.yc), VMEM),
             ((len(SPEEDS), plan.xc + 2, ROWS, plan.yc), VMEM),
         ],
-        [tall, tall, tall],
-    )
-    side = (2, plan.planes, plan.window * plan.layers, LANES)
+        [tall, tall, tall, (3 * (plan.xc + 4), plan.y + 2 * ROWS, plan.z)],
+    )
+    side = (2, plan.planes, plan.window * plan.pitch, LANES)
     return call(
         functools.partial(update_kernel, plan),
         [(received, VMEM)] + [(value, VMEM) for value in prepared],
@@ -732,13 +771,13 @@
             side,
             side,
             (ROWS, 3 * plan.planes * plan.layers, LANES),
-            (3, plan.planes, plan.coarse_layers * ROWS, LANES),
+            (3, plan.planes, plan.coarse_layers * (ROWS + 1), LANES),
             (MOMENTS, plan.coarse_layers, plan.frame, plan.z),
             (plan.zc * plan.gy, LANES),
             (plan.half * plan.gy, LANES),
-            short,
-            short,
-            short,
+            spare,
+            spare,
+            spare,
             density.shape,
             populations.shape,
         ],

time: 29.1 us -> 28.8 us (0.990)
  no operation moved by 1% of the time
where the time goes in v5:
time: 28.8 us; the launch traced here: 28.5 us
  starting transfers between devices  15.3 us (53%)
  Pallas kernels  6.91 us (24%)
  waiting for transfers between devices  5.62 us (20%)
  between operations  0.72 us (2%)
    ppermute x5, starting transfers between devices, shifted(): return lax.ppermute(value, everywhere, pairs)  7.94 us
    all_to_all x1, starting transfers between devices, exchange(): lax.all_to_all(send.reshape(plan.gx * plan.gy, plan.rows, LANES), everywh...  7.33 us
    pallas_call x4, Pallas kernels, call(): pl.pallas_call(kernel, out_shape=[jax.ShapeDtypeStruct(shape, jnp.float32...  6.91 us
    ppermute x5, waiting for transfers between devices, shifted(): return lax.ppermute(value, everywhere, pairs)  5.62 us
  transfers between devices with their start and end apart: 6, of which 2 were waited for; matrix products, arithmetic and copies ran while one was open for 0% of the time, Pallas kernels for 5%

profile of v5, /device:TPU:0, one launch (start us, length us, event | category | flops | bytes accessed | tf_op | source)
XLA Modules:
  0.0 28.5 jit_solution(6601276207553156862)
XLA Ops:
  0.6 2.7 %shard_map.41 = (f32[2,16,24,128]{3,2,1,0:T(8,128)}, f32[4,4,4,128]{3,2,1,0:T(4,128)}) custom-call(f32[8,16,128]{2,1,0:T(8,128)} %density.3, f32[19,4,4,128]{3,2,1,0:T(4,128)} %populations.3), custom_call_target="tpu_custom_call" | custom-call | tf_op jit(solution)/shard_map/pallas_call | solution.py:661
  3.3 0.0 copy-start
  3.3 0.0 copy-start.1
  3.4 0.0 copy-start.2
  3.4 7.3 %all-to-all-start = ((f32[32,24,128]{2,1,0:T(8,128)}), f32[32,24,128]{2,1,0:T(8,128)S(1)}, u32[]{:S(2)}, u32[]{:S(2)}) async-start(f32[32,24,128]{2,1,0:T(8,128)} %bitcast.3), calls=%async_computation | async-start | bytes 786432 | tf_op jit(solution)/shard_map/all_to_all | solution.py:693
  10.7 0.0 copy-done
  10.7 0.0 copy-done.1
  10.7 0.0 copy-done.2
  10.7 0.1 shard_map.42
  10.8 1.8 %collective-permute-start = (f32[200,128]{1,0:T(8,128)S(1)}, f32[200,128]{1,0:T(8,128)S(1)}, u32[]{:S(2)}, u32[]{:S(2)}) collective-permute-start(f32[200,128]{1,0:T(8,128)S(1)} %get-tuple-element.17), channel_id=1, source_target_pairs={{0,16},{1,17},{2,18},{3,19},{4,20},{5,21},{6,22},{7,23},{8,24},{9,... | collective-permute-start | bytes 307208 | tf_op jit(solution)/shard_map/ppermute | solution.py:681
  12.6 0.0 collective-permute-start.1
  12.6 4.4 %collective-permute-start.2 = (f32[92,128]{1,0:T(8,128)S(1)}, f32[92,128]{1,0:T(8,128)S(1)}, u32[]{:S(2)}, u32[]{:S(2)}) collective-permute-start(f32[92,128]{1,0:T(8,128)S(1)} %get-tuple-element.19), channel_id=1, source_target_pairs={{0,15},{1,2},{2,1},{3,4},{4,3},{5,6},{6,5},{7,8},{8,7},{9,10},{10,... | collective-permute-start | bytes 141320 | tf_op jit(solution)/shard_map/ppermute | solution.py:681
  17.0 0.0 collective-permute-start.3
  17.0 1.7 %collective-permute-start.4 = (f32[46,128]{1,0:T(8,128)S(1)}, f32[46,128]{1,0:T(8,128)S(1)}, u32[]{:S(2)}, u32[]{:S(2)}) collective-permute-start(f32[46,128]{1,0:T(8,128)S(1)} %get-tuple-element.21), channel_id=1, source_target_pairs={{0,31},{1,18},{2,17},{3,20},{4,19},{5,22},{6,21},{7,24},{8,23},{9,... | collective-permute-start | bytes 70664 | tf_op jit(solution)/shard_map/ppermute | solution.py:681
  18.8 1.5 %collective-permute-done.3.rest_3_ = f32[46,128]{1,0:T(8,128)S(1)} collective-permute-done((f32[46,128]{1,0:T(8,128)S(1)}, f32[46,128]{1,0:T(8,128)S(1)}, u32[]{:S(2)}, u32[]{:S(2)}) %collective-permute-start.3) | collective-permute-done | bytes 23584 | tf_op jit(solution)/shard_map/ppermute | solution.py:681
  20.3 4.1 %collective-permute-done.4.rest_4_ = f32[46,128]{1,0:T(8,128)S(1)} collective-permute-done((f32[46,128]{1,0:T(8,128)S(1)}, f32[46,128]{1,0:T(8,128)S(1)}, u32[]{:S(2)}, u32[]{:S(2)}) %collective-permute-start.4) | collective-permute-done | bytes 23584 | tf_op jit(solution)/shard_map/ppermute | solution.py:681
  24.4 0.0 collective-permute-done.1.rest_1_
  24.4 0.0 collective-permute-done.2.rest_2_
  24.4 0.0 collective-permute-done.rest_0_
  24.4 1.4 %shard_map.43 = (f32[16,24,128]{2,1,0:T(8,128)S(1)}, f32[3,16,24,128]{3,2,1,0:T(8,128)S(1)}, f32[16,24,128]{2,1,0:T(8,128)S(1)}, f32[3,4,24,128]{3,2,1,0:T(8,128...) custom-call(f32[8,16,128]{2,1,0:T(8,128)S(1)} %copy-done.1, f32[19,4,4,128]{3,2,1,0:T(4,128)S(1)} %copy-done, ...), custom_call_target="tpu_custom_call" | custom-call | tf_op jit(solution)/shard_map/pallas_call | solution.py:661
  25.7 0.0 all-to-all-done
  25.8 2.8 %shard_map.44 = (f32[8,16,128]{2,1,0:T(8,128)}, f32[19,4,4,128]{3,2,1,0:T(4,128)}) custom-call(f32[2,16,24,128]{3,2,1,0:T(8,128)S(1)} %bitcast.2, f32[16,24,128]{2,1,0:T(8,128)S(1)} %get-tuple-element.22.base, f32[3,16,24,128]{3,2,1,0:T(8,128)S(1)} %get-tuple-element.23.slope, f32[16,24,128]{2,1,0:T(8,128)S(1)} %get-tuple-element.24.drift, ...), custom_call_target="tpu_custom_call" | custom-call | tf_op jit(solution)/shard_map/pallas_call | solution.py:661
Async XLA Ops:
  3.3 7.4 %copy-start = (f32[19,4,4,128]{3,2,1,0:T(4,128)S(1)}, f32[19,4,4,128]{3,2,1,0:T(4,128)}, u32[]{:S(2)}) copy-start(f32[19,4,4,128]{3,2,1,0:T(4,128)} %populations.3) | copy-start | bytes 466948
  3.3 7.4 %copy-start.1 = (f32[8,16,128]{2,1,0:T(8,128)S(1)}, f32[8,16,128]{2,1,0:T(8,128)}, u32[]{:S(2)}) copy-start(f32[8,16,128]{2,1,0:T(8,128)} %density.3) | copy-start | bytes 196612
  3.4 7.4 %copy-start.2 = (f32[4,4,4,128]{3,2,1,0:T(4,128)S(1)}, f32[4,4,4,128]{3,2,1,0:T(4,128)}, u32[]{:S(2)}) copy-start(f32[4,4,4,128]{3,2,1,0:T(4,128)} %get-tuple-element.16.moments) | copy-start | bytes 98308
  3.4 22.4 %all-to-all-start = ((f32[32,24,128]{2,1,0:T(8,128)}), f32[32,24,128]{2,1,0:T(8,128)S(1)}, u32[]{:S(2)}, u32[]{:S(2)}) async-start(f32[32,24,128]{2,1,0:T(8,128)} %bitcast.3), calls=%async_computation | async-start | bytes 786432 | tf_op jit(solution)/shard_map/all_to_all | solution.py:693
  10.8 13.6 %collective-permute-start = (f32[200,128]{1,0:T(8,128)S(1)}, f32[200,128]{1,0:T(8,128)S(1)}, u32[]{:S(2)}, u32[]{:S(2)}) collective-permute-start(f32[200,128]{1,0:T(8,128)S(1)} %get-tuple-element.17), channel_id=1, source_target_pairs={{0,16},{1,17},{2,18},{3,19},{4,20},{5,21},{6,22},{7,23},{8,24},{9,... | collective-permute-start | bytes 307208 | tf_op jit(solution)/shard_map/ppermute | solution.py:681
  12.6 11.7 %collective-permute-start.1 = (f32[92,128]{1,0:T(8,128)S(1)}, f32[92,128]{1,0:T(8,128)S(1)}, u32[]{:S(2)}, u32[]{:S(2)}) collective-permute-start(f32[92,128]{1,0:T(8,128)S(1)} %get-tuple-element.18), channel_id=1, source_target_pairs={{0,1},{1,0},{2,3},{3,2},{4,5},{5,4},{6,7},{7,6},{8,9},{9,8},{10,11... | collective-permute-start | bytes 141320 | tf_op jit(solution)/shard_map/ppermute | solution.py:681
  12.6 11.7 %collective-permute-start.2 = (f32[92,128]{1,0:T(8,128)S(1)}, f32[92,128]{1,0:T(8,128)S(1)}, u32[]{:S(2)}, u32[]{:S(2)}) collective-permute-start(f32[92,128]{1,0:T(8,128)S(1)} %get-tuple-element.19), channel_id=1, source_target_pairs={{0,15},{1,2},{2,1},{3,4},{4,3},{5,6},{6,5},{7,8},{8,7},{9,10},{10,... | collective-permute-start | bytes 141320 | tf_op jit(solution)/shard_map/ppermute | solution.py:681
  17.0 3.3 %collective-permute-start.3 = (f32[46,128]{1,0:T(8,128)S(1)}, f32[46,128]{1,0:T(8,128)S(1)}, u32[]{:S(2)}, u32[]{:S(2)}) collective-permute-start(f32[46,128]{1,0:T(8,128)S(1)} %get-tuple-element.20), channel_id=1, source_target_pairs={{0,17},{1,16},{2,19},{3,18},{4,21},{5,20},{6,23},{7,22},{8,25},{9,... | collective-permute-start | bytes 70664 | tf_op jit(solution)/shard_map/ppermute | solution.py:681
  17.0 7.3 %collective-permute-start.4 = (f32[46,128]{1,0:T(8,128)S(1)}, f32[46,128]{1,0:T(8,128)S(1)}, u32[]{:S(2)}, u32[]{:S(2)}) collective-permute-start(f32[46,128]{1,0:T(8,128)S(1)} %get-tuple-element.21), channel_id=1, source_target_pairs={{0,31},{1,18},{2,17},{3,20},{4,19},{5,22},{6,21},{7,24},{8,23},{9,... | collective-permute-start | bytes 70664 | tf_op jit(solution)/shard_map/ppermute | solution.py:681

commit v6 on v5

--- a/solution.py
+++ b/solution.py
@@ -106,6 +106,11 @@
             if a & bit:
                 continue
             low, high = arrays[a], arrays[a | bit]
+            if 2 * bit == count:
+                crossed = pltpu.roll(jnp.where(upper, low, high), LANES // 2, 1)
+                turned[a] = jnp.where(upper, crossed, low)
+                turned[a | bit] = jnp.where(upper, high, crossed)
+                continue
             turned[a] = jnp.where(upper, pltpu.roll(high, bit * granule, 1), low)
             turned[a | bit] = jnp.where(upper, high, pltpu.roll(low, LANES - bit * granule, 1))
         arrays = turned
@@ -374,15 +379,15 @@
             for x in (2 * coarse, 2 * coarse + 1):
                 now = shifted_rows(plan, grid, x, whole) * central_at(plan, pot, x, c, whole)
                 total = now if total is None else total + now
-            at = c * (plan.xc + 4) + coarse + 2
-            pooled[at] = total
+            own_scratch = pooled[c * (plan.xc + 4) + coarse + 2]
+            own_scratch[...] = total
             even_rows, odd_rows = pl.ds(0, pairs, stride=2), pl.ds(1, pairs, stride=2)
-            total = pooled[at, even_rows, :] + pooled[at, odd_rows, :]
+            total = own_scratch[even_rows, :] + own_scratch[odd_rows, :]
             total = total + jnp.where(odd, roll(total, 1, 1), roll(total, -1, 1))
             total = total * (-0.25 * force_unit / 8.0)
-            pooled[at, even_rows, :] = total
-            pooled[at, odd_rows, :] = total
-            force.append(pooled[at, inner, :])
+            own_scratch[even_rows, :] = total
+            own_scratch[odd_rows, :] = total
+            force.append(own_scratch[inner, :])
             if 0 <= coarse < plan.xc:
                 push[c, coarse] = force[c]
         for x in (2 * coarse, 2 * coarse + 1):
@@ -435,44 +440,60 @@
     first_substep(plan, density, halo, base, slope, drift, push, grid, lap, pot, pooled)
 
 
-def solvent_part(plan, place, received, field, member, out, grid, lap, pot, pooled, forces):
+def solvent_part(plan, place, received, field, member, out, grid, lap, pot, pooled, forces, tail):
     width, layers = plan.planes, plan.layers
     senders = LANES // plan.yb
 
     pitch = plan.pitch
 
     def load(source, parity, z, shift=0):
-        first = z * pitch + 1 + shift
-        parts = [source[parity, k, first : first + layers, :] for k in range(width)]
+        first = z % ROWS * pitch + 1 + shift
+        tile = source[z // ROWS][parity]
+        parts = [tile[k, first : first + layers, :] for k in range(width)]
         return parts[0] if width == 1 else jnp.concatenate(parts, axis=1)
 
     def save(target, parity, z, value):
-        first = z * pitch + 1
+        first = z % ROWS * pitch + 1
+        tile = target[z // ROWS][parity]
         for k in range(width):
             part = value[:, k * LANES : (k + 1) * LANES]
-            target[parity, k, first : first + layers, :] = part
+            tile[k, first : first + layers, :] = part
             if plan.pair:
-                target[parity, k, first - 1 : first, :] = part[layers - 1 :]
-                target[parity, k, first + layers : first + layers + 1, :] = part[:1]
+                tile[k, first - 1 : first, :] = part[layers - 1 :]
+                tile[k, first + layers : first + layers + 1, :] = part[:1]
+
+    def unpack(arrays, tile, plane, count, parts):
+        for g, value in enumerate(butterfly(arrays, plan.yb)):
+            for block, start in parts:
+                layer = block * plan.x + g // 2
+                places = [layer + 1]
+                if plan.pair and layer == 0:
+                    places.append(layers + 1)
+                if plan.pair and layer == layers - 1:
+                    places.append(0)
+                for row in places:
+                    grid[tile][g % 2][plane, pl.ds(row, count, stride=pitch), :] = value[start : start + count]
 
     for tile in range(pl.cdiv(plan.window, ROWS)):
-        count = min(ROWS, plan.window - tile * ROWS)
-        for block in range(plan.blocks):
-            for plane in range(width):
+        first = tile * ROWS
+        count = min(ROWS, plan.window - first)
+        for plane in range(width):
+            sender = plane * senders
+            if count * plan.blocks <= ROWS:
+                arrays = []
+                for t in range(senders):
+                    for block in range(plan.blocks):
+                        tail[sender + t, block * count : (block + 1) * count, :] = received[
+                            place(block), sender + t, first : first + count, :
+                        ]
+                    arrays.append(tail[sender + t])
+                unpack(arrays, tile, plane, count, [(block, block * count) for block in range(plan.blocks)])
+                continue
+            for block in range(plan.blocks):
                 arrays = [
-                    received[place(block), plane * senders + t, tile * ROWS : tile * ROWS + count, :]
-                    for t in range(senders)
+                    received[place(block), sender + t, first : first + count, :] for t in range(senders)
                 ]
-                for g, value in enumerate(butterfly(arrays, plan.yb)):
-                    layer = block * plan.x + g // 2
-                    places = [layer + 1]
-                    if plan.pair and layer == 0:
-                        places.append(layers + 1)
-                    if plan.pair and layer == layers - 1:
-                        places.append(0)
-                    for row in places:
-                        first = tile * ROWS * pitch + row
-                        grid[g % 2, plane, pl.ds(first, count, stride=pitch), :] = value
+                unpack(arrays, tile, plane, count, [(block, 0)])
 
     def laplace(source, z):
         even, odd = load(source, 0, z), load(source, 1, z)
@@ -517,13 +538,13 @@
             total = now if total is None else tuple(a + b for a, b in zip(total, now))
         for c in range(3):
             for k in range(width):
-                at = (c * width + k) * layers
-                pooled[coarse % ROWS, at : at + layers, :] = total[c][:, k * LANES : (k + 1) * LANES]
+                own_scratch = pooled[coarse + 1][c * width + k]
+                own_scratch[...] = total[c][:, k * LANES : (k + 1) * LANES]
                 value = (
-                    pooled[coarse % ROWS, pl.ds(at, coarse_layers, stride=2), :]
-                    + pooled[coarse % ROWS, pl.ds(at + 1, coarse_layers, stride=2), :]
+                    own_scratch[pl.ds(0, coarse_layers, stride=2), :]
+                    + own_scratch[pl.ds(1, coarse_layers, stride=2), :]
                 )
-                forces[c, k, pl.ds(coarse % ROWS, coarse_layers, stride=ROWS + 1), :] = value * scale
+                forces[c][k, pl.ds(coarse % ROWS, coarse_layers, stride=ROWS + 1), :] = value * scale
 
     rate = 1.0 / relax_time
     gain = 1.0 - 0.5 / relax_time
@@ -532,7 +553,7 @@
         at = plan.coarse_layer(x) * (ROWS + 1)
         force = []
         for c in range(3):
-            parts = [forces[c, k, at : at + ROWS, :] for k in range(width)]
+            parts = [forces[c][k, at : at + ROWS, :] for k in range(width)]
             force.append(parts[0] if width == 1 else jnp.concatenate(parts, axis=1))
         mass = field[0, slot]
         inverse = 1.0 / mass
@@ -568,60 +589,68 @@
             emit(q + 1, even, -odd)
 
 
-def density_part(plan, place, received, base, slope, drift, push, out, flow, column, beside, grid, lap, pot):
-    def spread(source, period, offset):
-        count = source.shape[0]
-        row = lax.broadcasted_iota(jnp.int32, (count, plan.z), 0)
-        cell = lax.broadcasted_iota(jnp.int32, (count, plan.z), 1) // 2
-        chosen = (row // period) * plan.zc + row % period + offset == cell
-        return lax.dot_general(
-            source.T,
-            chosen.astype(jnp.float32),
-            (((1,), (0,)), ((), ())),
-            precision=lax.Precision.HIGHEST,
+def density_part(plan, place, received, base, slope, drift, push, out, flow, column, grid, lap, pot):
+    own_rows, beside_rows = plan.zc * plan.gy, plan.half * plan.gy
+    row = lax.broadcasted_iota(jnp.int32, (own_rows, plan.z), 0)
+    cell = lax.broadcasted_iota(jnp.int32, (own_rows, plan.z), 1) // 2
+    own_chosen = (row == cell).astype(jnp.float32)
+    row = lax.broadcasted_iota(jnp.int32, (beside_rows, plan.z), 0)
+    cell = lax.broadcasted_iota(jnp.int32, (beside_rows, plan.z), 1) // 2
+    first_cell = (row // plan.half) * plan.zc + row % plan.half
+    chosen = [(first_cell + offset == cell).astype(jnp.float32) for offset in (0, plan.half)]
+
+    def spread(source, matrix):
+        turned = source.T
+        high = turned.astype(jnp.bfloat16)
+        low = (turned - high.astype(jnp.float32)).astype(jnp.bfloat16)
+        both = jnp.dot(
+            jnp.concatenate([high, low], axis=0),
+            matrix.astype(jnp.bfloat16),
             preferred_element_type=jnp.float32,
         )
+        return both[:LANES] + both[LANES:]
 
     own_row = ROWS // 2
     yb = plan.yb
     for block in range(plan.blocks):
         at = plan.window
         for j in range(plan.gy):
-            column[j * plan.zc : (j + 1) * plan.zc, :] = received[place(block), j, at : at + plan.zc, :]
-            beside[j * plan.half : (j + 1) * plan.half, :] = received[
+            column[block][j * plan.zc : (j + 1) * plan.zc, :] = received[place(block), j, at : at + plan.zc, :]
+            start = own_rows + j * plan.half
+            column[block][start : start + plan.half, :] = received[
                 place(block), j, at + plan.zc : at + plan.zc + plan.half, :
             ]
-        own = spread(column[...], plan.zc, 0)
-        first = spread(beside[...], plan.half, 0)
-        second = spread(beside[...], plan.half, plan.half)
+        own = spread(column[block][:own_rows], own_chosen)
+        beside = spread(column[block][own_rows:], jnp.concatenate(chosen, axis=1))
+        first, second = beside[:, : plan.z], beside[:, plan.z :]
         for f in range(MOMENTS):
             for x in range(plan.xc):
                 at = (f * plan.xc + x) * yb
-                lead = (f, block * plan.xc + x)
+                target = flow[f][block * plan.xc + x]
                 after = first[at : at + 2] + second[at + 2 : at + 4]
                 before = first[at + yb - 2 : at + yb] + second[at + yb - 4 : at + yb - 2]
                 for parity in range(2):
-                    flow[lead + (pl.ds(own_row + parity, yb, stride=2),)] = own[at : at + yb]
-                    flow[lead + (pl.ds(own_row + plan.y + parity, 2, stride=2),)] = after
-                    flow[lead + (pl.ds(own_row - 4 + parity, 2, stride=2),)] = before
+                    target[pl.ds(own_row + parity, yb, stride=2), :] = own[at : at + yb]
+                    target[pl.ds(own_row + plan.y + parity, 2, stride=2), :] = after
+                    target[pl.ds(own_row - 4 + parity, 2, stride=2), :] = before
 
     reach = 3 * (DENSITY_SUBSTEPS - 1)
     inverses = {}
     for x in plan.span(-reach, plan.x + reach):
         here, slot = plan.layer(x), plan.coarse_layer(x // 2)
         if slot not in inverses:
-            inverses[slot] = 1.0 / flow[0, slot]
+            inverses[slot] = 1.0 / flow[0][slot][...]
         advection = drift[here]
         for c in range(3):
-            advection = advection + flow[c + 1, slot] * slope[c, here]
+            advection = advection + flow[c + 1][slot][...] * slope[c, here]
         grid[here, ROWS : ROWS + plan.frame] = base[here] - advection * inverses[slot]
     whole = slice(0, plan.frame)
     inner = slice(own_row, own_row + plan.y)
     potential_at(plan, grid, lap, pot, 2, whole)
     for coarse in range(plan.xc):
         slot = plan.coarse_layer(coarse)
-        scaled = (0.5 * speed_unit) / flow[0, slot, inner]
-        speed = [(flow[c + 1, slot, inner] + push[c, coarse, inner]) * scaled for c in range(3)]
+        scaled = (0.5 * speed_unit) / flow[0][slot][inner, :]
+        speed = [(flow[c + 1][slot][inner, :] + push[c, coarse, inner]) * scaled for c in range(3)]
         for x in (2 * coarse, 2 * coarse + 1):
             change = laplace_at(plan, pot, x, inner)
             for c in range(3):
@@ -631,7 +660,7 @@
 
 def update_kernel(plan, received, base, slope, drift, push, field, member, *rest):
     density_next, populations_next = rest[:2]
-    side_grid, side_lap, side_pot, pooled, forces, flow, column, beside, grid, lap, pot = rest[2:13]
+    side_grid, side_lap, side_pot, pooled, forces, tail, flow, column, grid, lap, pot = rest[2:13]
     density_out, populations_out, sems = rest[13:]
     mine = lax.axis_index("gx")
 
@@ -641,12 +670,12 @@
         return mine if block == 0 else 1 - mine
 
     solvent_part(
-        plan, place, received, field, member, populations_out, side_grid, side_lap, side_pot, pooled, forces
+        plan, place, received, field, member, populations_out, side_grid, side_lap, side_pot, pooled, forces, tail
     )
     give_populations = pltpu.make_async_copy(populations_out, populations_next, sems.at[0])
     give_populations.start()
     density_part(
-        plan, place, received, base, slope, drift, push, density_out, flow, column, beside, grid, lap, pot
+        plan, place, received, base, slope, drift, push, density_out, flow, column, grid, lap, pot
     )
     give_density = pltpu.make_async_copy(density_out, density_next, sems.at[1])
     give_density.start()
@@ -655,6 +684,10 @@
 
 
 VMEM, HBM = pltpu.VMEM, pltpu.HBM
+
+
+def buffers(shapes):
+    return [buffers(s) if isinstance(s, list) else pltpu.VMEM(s, jnp.float32) for s in shapes]
 
 
 def call(kernel, arguments, outputs, scratch, sems=0, limit=16 * 1024 * 1024):
@@ -663,7 +696,7 @@
         out_shape=[jax.ShapeDtypeStruct(shape, jnp.float32) for shape, _ in outputs],
         in_specs=[pl.BlockSpec(memory_space=space) for _, space in arguments],
         out_specs=[pl.BlockSpec(memory_space=space) for _, space in outputs],
-        scratch_shapes=[pltpu.VMEM(shape, jnp.float32) for shape in scratch]
+        scratch_shapes=buffers(scratch)
         + ([pltpu.SemaphoreType.DMA((sems,))] if sems else []),
         compiler_params=pltpu.CompilerParams(vmem_limit_bytes=limit),
     )(*[value for value, _ in arguments])
@@ -759,9 +792,9 @@
             ((MOMENTS, plan.xc + 2, ROWS, plan.yc), VMEM),
             ((len(SPEEDS), plan.xc + 2, ROWS, plan.yc), VMEM),
         ],
-        [tall, tall, tall, (3 * (plan.xc + 4), plan.y + 2 * ROWS, plan.z)],
+        [tall, tall, tall, [(plan.y + 2 * ROWS, plan.z)] * (3 * (plan.xc + 4))],
     )
-    side = (2, plan.planes, plan.window * plan.pitch, LANES)
+    side = [[(plan.planes, ROWS * plan.pitch, LANES)] * 2] * pl.cdiv(plan.window, ROWS)
     return call(
         functools.partial(update_kernel, plan),
         [(received, VMEM)] + [(value, VMEM) for value in prepared],
@@ -770,11 +803,11 @@
             side,
             side,
             side,
-            (ROWS, 3 * plan.planes * plan.layers, LANES),
-            (3, plan.planes, plan.coarse_layers * (ROWS + 1), LANES),
-            (MOMENTS, plan.coarse_layers, plan.frame, plan.z),
-            (plan.zc * plan.gy, LANES),
-            (plan.half * plan.gy, LANES),
+            [[(plan.layers, LANES)] * (3 * plan.planes)] * (plan.zc + 2),
+            [(plan.planes, plan.coarse_layers * (ROWS + 1), LANES)] * 3,
+            (plan.gy, ROWS, LANES),
+            [[(plan.frame, plan.z)] * plan.coarse_layers] * MOMENTS,
+            [((plan.zc + plan.half) * plan.gy, LANES)] * plan.blocks,
             spare,
             spare,
             spare,

time: 28.8 us -> 28.5 us (0.990)
  Pallas kernels: 6.91 us -> 6.6 us
    pallas_call x4, Pallas kernels: 6.91 us -> 6.6 us  [call(): pl.pallas_call(kernel, out_shape=[jax.ShapeDtypeStruct(shape, jnp.float32...]
where the time goes in v6:
time: 28.5 us; the launch traced here: 28.2 us
  starting transfers between devices  15.3 us (54%)
  Pallas kernels  6.6 us (23%)
  waiting for transfers between devices  5.62 us (20%)
  between operations  0.72 us (3%)
    ppermute x5, starting transfers between devices, shifted(): return lax.ppermute(value, everywhere, pairs)  7.94 us
    all_to_all x1, starting transfers between devices, exchange(): lax.all_to_all(send.reshape(plan.gx * plan.gy, plan.rows, LANES), everywh...  7.33 us
    pallas_call x4, Pallas kernels, call(): pl.pallas_call(kernel, out_shape=[jax.ShapeDtypeStruct(shape, jnp.float32...  6.6 us
    ppermute x5, waiting for transfers between devices, shifted(): return lax.ppermute(value, everywhere, pairs)  5.62 us
  transfers between devices with their start and end apart: 6, of which 2 were waited for; matrix products, arithmetic and copies ran while one was open for 0% of the time, Pallas kernels for 5%

profile of v6, /device:TPU:0, one launch (start us, length us, event | category | flops | bytes accessed | tf_op | source)
XLA Modules:
  0.0 28.2 jit_solution(3012978638860503567)
XLA Ops:
  0.6 2.7 %shard_map.41 = (f32[2,16,24,128]{3,2,1,0:T(8,128)}, f32[4,4,4,128]{3,2,1,0:T(4,128)}) custom-call(f32[8,16,128]{2,1,0:T(8,128)} %density.3, f32[19,4,4,128]{3,2,1,0:T(4,128)} %populations.3), custom_call_target="tpu_custom_call" | custom-call | tf_op jit(solution)/shard_map/pallas_call | solution.py:694
  3.3 0.0 copy-start
  3.4 0.0 copy-start.1
  3.4 0.0 copy-start.2
  3.4 7.3 %all-to-all-start = ((f32[32,24,128]{2,1,0:T(8,128)}), f32[32,24,128]{2,1,0:T(8,128)S(1)}, u32[]{:S(2)}, u32[]{:S(2)}) async-start(f32[32,24,128]{2,1,0:T(8,128)} %bitcast.3), calls=%async_computation | async-start | bytes 786432 | tf_op jit(solution)/shard_map/all_to_all | solution.py:726
  10.7 0.0 copy-done
  10.7 0.0 copy-done.1
  10.7 0.0 copy-done.2
  10.7 0.1 shard_map.42
  10.8 1.8 %collective-permute-start = (f32[200,128]{1,0:T(8,128)S(1)}, f32[200,128]{1,0:T(8,128)S(1)}, u32[]{:S(2)}, u32[]{:S(2)}) collective-permute-start(f32[200,128]{1,0:T(8,128)S(1)} %get-tuple-element.17), channel_id=1, source_target_pairs={{0,16},{1,17},{2,18},{3,19},{4,20},{5,21},{6,22},{7,23},{8,24},{9,... | collective-permute-start | bytes 307208 | tf_op jit(solution)/shard_map/ppermute | solution.py:714
  12.6 0.0 collective-permute-start.1
  12.6 4.4 %collective-permute-start.2 = (f32[92,128]{1,0:T(8,128)S(1)}, f32[92,128]{1,0:T(8,128)S(1)}, u32[]{:S(2)}, u32[]{:S(2)}) collective-permute-start(f32[92,128]{1,0:T(8,128)S(1)} %get-tuple-element.19), channel_id=1, source_target_pairs={{0,15},{1,2},{2,1},{3,4},{4,3},{5,6},{6,5},{7,8},{8,7},{9,10},{10,... | collective-permute-start | bytes 141320 | tf_op jit(solution)/shard_map/ppermute | solution.py:714
  17.0 0.0 collective-permute-start.3
  17.0 1.7 %collective-permute-start.4 = (f32[46,128]{1,0:T(8,128)S(1)}, f32[46,128]{1,0:T(8,128)S(1)}, u32[]{:S(2)}, u32[]{:S(2)}) collective-permute-start(f32[46,128]{1,0:T(8,128)S(1)} %get-tuple-element.21), channel_id=1, source_target_pairs={{0,31},{1,18},{2,17},{3,20},{4,19},{5,22},{6,21},{7,24},{8,23},{9,... | collective-permute-start | bytes 70664 | tf_op jit(solution)/shard_map/ppermute | solution.py:714
  18.8 1.5 %collective-permute-done.3.rest_3_ = f32[46,128]{1,0:T(8,128)S(1)} collective-permute-done((f32[46,128]{1,0:T(8,128)S(1)}, f32[46,128]{1,0:T(8,128)S(1)}, u32[]{:S(2)}, u32[]{:S(2)}) %collective-permute-start.3) | collective-permute-done | bytes 23584 | tf_op jit(solution)/shard_map/ppermute | solution.py:714
  20.3 4.1 %collective-permute-done.4.rest_4_ = f32[46,128]{1,0:T(8,128)S(1)} collective-permute-done((f32[46,128]{1,0:T(8,128)S(1)}, f32[46,128]{1,0:T(8,128)S(1)}, u32[]{:S(2)}, u32[]{:S(2)}) %collective-permute-start.4) | collective-permute-done | bytes 23584 | tf_op jit(solution)/shard_map/ppermute | solution.py:714
  24.4 0.0 collective-permute-done.1.rest_1_
  24.4 0.0 collective-permute-done.2.rest_2_
  24.4 0.0 collective-permute-done.rest_0_
  24.4 1.4 %shard_map.43 = (f32[16,24,128]{2,1,0:T(8,128)S(1)}, f32[3,16,24,128]{3,2,1,0:T(8,128)S(1)}, f32[16,24,128]{2,1,0:T(8,128)S(1)}, f32[3,4,24,128]{3,2,1,0:T(8,128...) custom-call(f32[8,16,128]{2,1,0:T(8,128)S(1)} %copy-done.1, f32[19,4,4,128]{3,2,1,0:T(4,128)S(1)} %copy-done, ...), custom_call_target="tpu_custom_call" | custom-call | tf_op jit(solution)/shard_map/pallas_call | solution.py:694
  25.7 0.0 all-to-all-done
  25.8 2.5 %shard_map.44 = (f32[8,16,128]{2,1,0:T(8,128)}, f32[19,4,4,128]{3,2,1,0:T(4,128)}) custom-call(f32[2,16,24,128]{3,2,1,0:T(8,128)S(1)} %bitcast.2, f32[16,24,128]{2,1,0:T(8,128)S(1)} %get-tuple-element.22.base, f32[3,16,24,128]{3,2,1,0:T(8,128)S(1)} %get-tuple-element.23.slope, f32[16,24,128]{2,1,0:T(8,128)S(1)} %get-tuple-element.24.drift, ...), custom_call_target="tpu_custom_call" | custom-call | tf_op jit(solution)/shard_map/pallas_call | solution.py:694
Async XLA Ops:
  3.3 7.4 %copy-start = (f32[19,4,4,128]{3,2,1,0:T(4,128)S(1)}, f32[19,4,4,128]{3,2,1,0:T(4,128)}, u32[]{:S(2)}) copy-start(f32[19,4,4,128]{3,2,1,0:T(4,128)} %populations.3) | copy-start | bytes 466948
  3.4 7.4 %copy-start.1 = (f32[8,16,128]{2,1,0:T(8,128)S(1)}, f32[8,16,128]{2,1,0:T(8,128)}, u32[]{:S(2)}) copy-start(f32[8,16,128]{2,1,0:T(8,128)} %density.3) | copy-start | bytes 196612
  3.4 7.4 %copy-start.2 = (f32[4,4,4,128]{3,2,1,0:T(4,128)S(1)}, f32[4,4,4,128]{3,2,1,0:T(4,128)}, u32[]{:S(2)}) copy-start(f32[4,4,4,128]{3,2,1,0:T(4,128)} %get-tuple-element.16.moments) | copy-start | bytes 98308
  3.4 22.4 %all-to-all-start = ((f32[32,24,128]{2,1,0:T(8,128)}), f32[32,24,128]{2,1,0:T(8,128)S(1)}, u32[]{:S(2)}, u32[]{:S(2)}) async-start(f32[32,24,128]{2,1,0:T(8,128)} %bitcast.3), calls=%async_computation | async-start | bytes 786432 | tf_op jit(solution)/shard_map/all_to_all | solution.py:726
  10.8 13.6 %collective-permute-start = (f32[200,128]{1,0:T(8,128)S(1)}, f32[200,128]{1,0:T(8,128)S(1)}, u32[]{:S(2)}, u32[]{:S(2)}) collective-permute-start(f32[200,128]{1,0:T(8,128)S(1)} %get-tuple-element.17), channel_id=1, source_target_pairs={{0,16},{1,17},{2,18},{3,19},{4,20},{5,21},{6,22},{7,23},{8,24},{9,... | collective-permute-start | bytes 307208 | tf_op jit(solution)/shard_map/ppermute | solution.py:714
  12.6 11.7 %collective-permute-start.1 = (f32[92,128]{1,0:T(8,128)S(1)}, f32[92,128]{1,0:T(8,128)S(1)}, u32[]{:S(2)}, u32[]{:S(2)}) collective-permute-start(f32[92,128]{1,0:T(8,128)S(1)} %get-tuple-element.18), channel_id=1, source_target_pairs={{0,1},{1,0},{2,3},{3,2},{4,5},{5,4},{6,7},{7,6},{8,9},{9,8},{10,11... | collective-permute-start | bytes 141320 | tf_op jit(solution)/shard_map/ppermute | solution.py:714
  12.6 11.7 %collective-permute-start.2 = (f32[92,128]{1,0:T(8,128)S(1)}, f32[92,128]{1,0:T(8,128)S(1)}, u32[]{:S(2)}, u32[]{:S(2)}) collective-permute-start(f32[92,128]{1,0:T(8,128)S(1)} %get-tuple-element.19), channel_id=1, source_target_pairs={{0,15},{1,2},{2,1},{3,4},{4,3},{5,6},{6,5},{7,8},{8,7},{9,10},{10,... | collective-permute-start | bytes 141320 | tf_op jit(solution)/shard_map/ppermute | solution.py:714
  17.0 3.3 %collective-permute-start.3 = (f32[46,128]{1,0:T(8,128)S(1)}, f32[46,128]{1,0:T(8,128)S(1)}, u32[]{:S(2)}, u32[]{:S(2)}) collective-permute-start(f32[46,128]{1,0:T(8,128)S(1)} %get-tuple-element.20), channel_id=1, source_target_pairs={{0,17},{1,16},{2,19},{3,18},{4,21},{5,20},{6,23},{7,22},{8,25},{9,... | collective-permute-start | bytes 70664 | tf_op jit(solution)/shard_map/ppermute | solution.py:714
  17.0 7.3 %collective-permute-start.4 = (f32[46,128]{1,0:T(8,128)S(1)}, f32[46,128]{1,0:T(8,128)S(1)}, u32[]{:S(2)}, u32[]{:S(2)}) collective-permute-start(f32[46,128]{1,0:T(8,128)S(1)} %get-tuple-element.21), channel_id=1, source_target_pairs={{0,31},{1,18},{2,17},{3,20},{4,19},{5,22},{6,21},{7,24},{8,23},{9,... | collective-permute-start | bytes 70664 | tf_op jit(solution)/shard_map/ppermute | solution.py:714

commit v7 on v6

--- a/solution.py
+++ b/solution.py
@@ -95,26 +95,17 @@
         return list(seen.values())
 
 
-def butterfly(arrays, granule):
+def transpose_granules(arrays, granule):
     count = LANES // granule
     lane = lax.broadcasted_iota(jnp.int32, arrays[0].shape, 1) // granule
-    bit = 1
-    while bit < count:
-        upper = (lane & bit) != 0
-        turned = list(arrays)
-        for a in range(count):
-            if a & bit:
-                continue
-            low, high = arrays[a], arrays[a | bit]
-            if 2 * bit == count:
-                crossed = pltpu.roll(jnp.where(upper, low, high), LANES // 2, 1)
-                turned[a] = jnp.where(upper, crossed, low)
-                turned[a | bit] = jnp.where(upper, high, crossed)
-                continue
-            turned[a] = jnp.where(upper, pltpu.roll(high, bit * granule, 1), low)
-            turned[a | bit] = jnp.where(upper, high, pltpu.roll(low, LANES - bit * granule, 1))
-        arrays = turned
-        bit *= 2
+    bits = [1 << k for k in range(count.bit_length() - 1)]
+    chosen = [(lane & bit) != 0 for bit in bits]
+    for bit, mask in zip(bits, chosen):
+        arrays = [jnp.where(mask, arrays[(d + bit) % count], arrays[d]) for d in range(count)]
+    arrays = [arrays[0]] + [pltpu.roll(arrays[d], d * granule, 1) for d in range(1, count)]
+    arrays = [arrays[-k % count] for k in range(count)]
+    for bit, mask in zip(bits, chosen):
+        arrays = [jnp.where(mask, arrays[(k - bit) % count], arrays[k]) for k in range(count)]
     return arrays
 
 
@@ -226,7 +217,7 @@
     turned = []
     for plane in range(plan.planes):
         span = slice(plane * LANES, (plane + 1) * LANES)
-        turned += butterfly([value[:, span] for row in fields for value in row], plan.yb)
+        turned += transpose_granules([value[:, span] for row in fields for value in row], plan.yb)
     y = lax.broadcasted_iota(jnp.int32, (plan.half, LANES), 1) % plan.yb
     y_all = lax.broadcasted_iota(jnp.int32, (plan.zc, LANES), 1) % plan.yb
     for target in range(plan.gy):
@@ -313,38 +304,48 @@
     return source[plan.layer(x), ROWS + part.start + shift : ROWS + part.stop + shift, :]
 
 
-def laplace_at(plan, source, x, part):
+def along_z(value):
+    after, before = roll(value, -1, 1), roll(value, 1, 1)
+    return after + before, after - before
+
+
+def laplace_at(plan, source, x, part, beside=None):
     value = shifted_rows(plan, source, x, part)
     running = -6.0 * value + shifted_rows(plan, source, x - 1, part) + shifted_rows(plan, source, x + 1, part)
     running = running + shifted_rows(plan, source, x, part, 1) + shifted_rows(plan, source, x, part, -1)
-    return running + roll(value, 1, 1) + roll(value, -1, 1)
-
-
-def potential_at(plan, grid, lap, pot, reach, part):
+    return running + (along_z(value)[0] if beside is None else beside)
+
+
+def potential_at(plan, grid, lap, pot, reach, part, grid_slope, pot_beside=None, pot_slope=None):
     rows = slice(ROWS + part.start, ROWS + part.stop)
     for x in plan.span(-reach, plan.x + reach):
-        lap[plan.layer(x), rows] = laplace_at(plan, grid, x, part)
+        here = plan.layer(x)
+        beside, grid_slope[here, rows] = along_z(grid[here, rows])
+        lap[here, rows] = laplace_at(plan, grid, x, part, beside)
     for x in plan.span(1 - reach, plan.x + reach - 1):
         here = plan.layer(x)
         value = grid[here, rows]
-        pot[here, rows] = (
+        value = (
             (quench_depth + 1.0) * value
             + 2.0 * lap[here, rows]
             + laplace_at(plan, lap, x, part)
             + value * value * value
         )
-
-
-def central_at(plan, source, x, c, part):
+        pot[here, rows] = value
+        if pot_slope is not None:
+            pot_beside[here, rows], pot_slope[here, rows] = along_z(value)
+
+
+def central_at(plan, source, slope, x, c, part):
     if c == 0:
         return shifted_rows(plan, source, x + 1, part) - shifted_rows(plan, source, x - 1, part)
     if c == 1:
         return shifted_rows(plan, source, x, part, 1) - shifted_rows(plan, source, x, part, -1)
-    value = shifted_rows(plan, source, x, part)
-    return roll(value, -1, 1) - roll(value, 1, 1)
-
-
-def first_substep(plan, density, halo, base, slope, drift, push, grid, lap, pot, pooled):
+    return shifted_rows(plan, slope, x, part)
+
+
+def first_substep(plan, density, halo, base, slope, drift, push, arrays, pooled):
+    grid, lap, pot, grid_slope, pot_beside, pot_slope = arrays
     from_low, from_high, from_below, from_above, below_low, below_high, above_low, above_high = halo
     sets = [(0, None, from_below, from_above)]
     if plan.pair:
@@ -366,7 +367,7 @@
             grid[here, own + plan.y : own + plan.y + rows] = above(start, rows, 1)
     whole = slice(0, plan.y + 2 * ROWS)
     inner = slice(ROWS // 2, ROWS // 2 + plan.frame)
-    potential_at(plan, grid, lap, pot, 6, whole)
+    potential_at(plan, grid, lap, pot, 6, whole, grid_slope, pot_beside, pot_slope)
     pairs = (plan.y + 2 * ROWS) // 2
     odd = (lax.broadcasted_iota(jnp.int32, (pairs, plan.z), 1) & 1) != 0
     reach = 3 * (DENSITY_SUBSTEPS - 1)
@@ -377,7 +378,7 @@
         for c in range(3):
             total = None
             for x in (2 * coarse, 2 * coarse + 1):
-                now = shifted_rows(plan, grid, x, whole) * central_at(plan, pot, x, c, whole)
+                now = shifted_rows(plan, grid, x, whole) * central_at(plan, pot, pot_slope, x, c, whole)
                 total = now if total is None else total + now
             own_scratch = pooled[c * (plan.xc + 4) + coarse + 2]
             own_scratch[...] = total
@@ -395,10 +396,13 @@
             if here not in wanted or here in done:
                 continue
             done.add(here)
-            base[here] = shifted_rows(plan, grid, x, inner) + coupled_time_step * laplace_at(plan, pot, x, inner)
+            beside = shifted_rows(plan, pot_beside, x, inner)
+            base[here] = shifted_rows(plan, grid, x, inner) + coupled_time_step * laplace_at(
+                plan, pot, x, inner, beside
+            )
             total = None
             for c in range(3):
-                scaled = central_at(plan, grid, x, c, inner) * (0.5 * speed_unit * coupled_time_step)
+                scaled = central_at(plan, grid, grid_slope, x, c, inner) * (0.5 * speed_unit * coupled_time_step)
                 slope[c, here] = scaled
                 now = force[c] * scaled
                 total = now if total is None else total + now
@@ -408,7 +412,7 @@
 def prepare_kernel(plan, density, populations, moments, *rest):
     neighbours = 5 if plan.pair else 8
     buffers, rest = rest[:neighbours], rest[neighbours:]
-    base, slope, drift, push, field, member, grid, lap, pot, pooled = rest
+    base, slope, drift, push, field, member, arrays, pooled = rest
     even = lax.axis_index("gy") % 2 == 0
 
     def plain(ref):
@@ -437,7 +441,7 @@
         either(near_high, far_high),
     )
     gather_solvent(plan, populations, moments, halo, field, member)
-    first_substep(plan, density, halo, base, slope, drift, push, grid, lap, pot, pooled)
+    first_substep(plan, density, halo, base, slope, drift, push, arrays, pooled)
 
 
 def solvent_part(plan, place, received, field, member, out, grid, lap, pot, pooled, forces, tail):
@@ -463,7 +467,7 @@
                 tile[k, first + layers : first + layers + 1, :] = part[:1]
 
     def unpack(arrays, tile, plane, count, parts):
-        for g, value in enumerate(butterfly(arrays, plan.yb)):
+        for g, value in enumerate(transpose_granules(arrays, plan.yb)):
             for block, start in parts:
                 layer = block * plan.x + g // 2
                 places = [layer + 1]
@@ -589,7 +593,8 @@
             emit(q + 1, even, -odd)
 
 
-def density_part(plan, place, received, base, slope, drift, push, out, flow, column, grid, lap, pot):
+def density_part(plan, place, received, base, slope, drift, push, out, flow, column, arrays):
+    grid, lap, pot, grid_slope = arrays
     own_rows, beside_rows = plan.zc * plan.gy, plan.half * plan.gy
     row = lax.broadcasted_iota(jnp.int32, (own_rows, plan.z), 0)
     cell = lax.broadcasted_iota(jnp.int32, (own_rows, plan.z), 1) // 2
@@ -646,7 +651,7 @@
         grid[here, ROWS : ROWS + plan.frame] = base[here] - advection * inverses[slot]
     whole = slice(0, plan.frame)
     inner = slice(own_row, own_row + plan.y)
-    potential_at(plan, grid, lap, pot, 2, whole)
+    potential_at(plan, grid, lap, pot, 2, whole, grid_slope)
     for coarse in range(plan.xc):
         slot = plan.coarse_layer(coarse)
         scaled = (0.5 * speed_unit) / flow[0][slot][inner, :]
@@ -654,14 +659,14 @@
         for x in (2 * coarse, 2 * coarse + 1):
             change = laplace_at(plan, pot, x, inner)
             for c in range(3):
-                change = change - speed[c] * central_at(plan, grid, x, c, inner)
+                change = change - speed[c] * central_at(plan, grid, grid_slope, x, c, inner)
             out[x] = shifted_rows(plan, grid, x, inner) + coupled_time_step * change
 
 
 def update_kernel(plan, received, base, slope, drift, push, field, member, *rest):
     density_next, populations_next = rest[:2]
-    side_grid, side_lap, side_pot, pooled, forces, tail, flow, column, grid, lap, pot = rest[2:13]
-    density_out, populations_out, sems = rest[13:]
+    side_grid, side_lap, side_pot, pooled, forces, tail, flow, column, arrays = rest[2:11]
+    density_out, populations_out, sems = rest[11:]
     mine = lax.axis_index("gx")
 
     def place(block):
@@ -675,7 +680,7 @@
     give_populations = pltpu.make_async_copy(populations_out, populations_next, sems.at[0])
     give_populations.start()
     density_part(
-        plan, place, received, base, slope, drift, push, density_out, flow, column, grid, lap, pot
+        plan, place, received, base, slope, drift, push, density_out, flow, column, arrays
     )
     give_density = pltpu.make_async_copy(density_out, density_next, sems.at[1])
     give_density.start()
@@ -792,7 +797,7 @@
             ((MOMENTS, plan.xc + 2, ROWS, plan.yc), VMEM),
             ((len(SPEEDS), plan.xc + 2, ROWS, plan.yc), VMEM),
         ],
-        [tall, tall, tall, [(plan.y + 2 * ROWS, plan.z)] * (3 * (plan.xc + 4))],
+        [[tall] * 6, [(plan.y + 2 * ROWS, plan.z)] * (3 * (plan.xc + 4))],
     )
     side = [[(plan.planes, ROWS * plan.pitch, LANES)] * 2] * pl.cdiv(plan.window, ROWS)
     return call(
@@ -808,9 +813,7 @@
             (plan.gy, ROWS, LANES),
             [[(plan.frame, plan.z)] * plan.coarse_layers] * MOMENTS,
             [((plan.zc + plan.half) * plan.gy, LANES)] * plan.blocks,
-            spare,
-            spare,
-            spare,
+            [spare] * 4,
             density.shape,
             populations.shape,
         ],

time: 28.5 us -> 28 us (0.982)
  Pallas kernels: 6.6 us -> 6.17 us
    pallas_call x4, Pallas kernels: 6.6 us -> 6.17 us  [call(): pl.pallas_call(kernel, out_shape=[jax.ShapeDtypeStruct(shape, jnp.float32...]
  transfers between devices with their start and end apart: 6 -> 6, of which waited for: 2 -> 2; matrix products, arithmetic and copies ran while one was open for 0% -> 0% of each run, Pallas kernels for 5% -> 7%
where the time goes in v7:
time: 28 us; the launch traced here: 27.8 us
  starting transfers between devices  15.3 us (55%)
  Pallas kernels  6.17 us (22%)
  waiting for transfers between devices  5.62 us (20%)
  between operations  0.72 us (3%)
    ppermute x5, starting transfers between devices, shifted(): return lax.ppermute(value, everywhere, pairs)  7.94 us
    all_to_all x1, starting transfers between devices, exchange(): lax.all_to_all(send.reshape(plan.gx * plan.gy, plan.rows, LANES), everywh...  7.33 us
    pallas_call x4, Pallas kernels, call(): pl.pallas_call(kernel, out_shape=[jax.ShapeDtypeStruct(shape, jnp.float32...  6.17 us
    ppermute x5, waiting for transfers between devices, shifted(): return lax.ppermute(value, everywhere, pairs)  5.62 us
  transfers between devices with their start and end apart: 6, of which 2 were waited for; matrix products, arithmetic and copies ran while one was open for 0% of the time, Pallas kernels for 7%

profile of v7, /device:TPU:0, one launch (start us, length us, event | category | flops | bytes accessed | tf_op | source)
XLA Modules:
  0.0 27.8 jit_solution(7582994502723053307)
XLA Ops:
  0.6 2.5 %shard_map.41 = (f32[2,16,24,128]{3,2,1,0:T(8,128)}, f32[4,4,4,128]{3,2,1,0:T(4,128)}) custom-call(f32[8,16,128]{2,1,0:T(8,128)} %density.3, f32[19,4,4,128]{3,2,1,0:T(4,128)} %populations.3), custom_call_target="tpu_custom_call" | custom-call | tf_op jit(solution)/shard_map/pallas_call | solution.py:699
  3.1 0.0 copy-start
  3.2 0.0 copy-start.1
  3.2 0.0 copy-start.2
  3.2 7.3 %all-to-all-start = ((f32[32,24,128]{2,1,0:T(8,128)}), f32[32,24,128]{2,1,0:T(8,128)S(1)}, u32[]{:S(2)}, u32[]{:S(2)}) async-start(f32[32,24,128]{2,1,0:T(8,128)} %bitcast.3), calls=%async_computation | async-start | bytes 786432 | tf_op jit(solution)/shard_map/all_to_all | solution.py:731
  10.5 0.0 copy-done
  10.5 0.0 copy-done.1
  10.5 0.0 copy-done.2
  10.6 0.1 shard_map.42
  10.6 1.8 %collective-permute-start = (f32[200,128]{1,0:T(8,128)S(1)}, f32[200,128]{1,0:T(8,128)S(1)}, u32[]{:S(2)}, u32[]{:S(2)}) collective-permute-start(f32[200,128]{1,0:T(8,128)S(1)} %get-tuple-element.17), channel_id=1, source_target_pairs={{0,16},{1,17},{2,18},{3,19},{4,20},{5,21},{6,22},{7,23},{8,24},{9,... | collective-permute-start | bytes 307208 | tf_op jit(solution)/shard_map/ppermute | solution.py:719
  12.5 0.0 collective-permute-start.1
  12.5 4.4 %collective-permute-start.2 = (f32[92,128]{1,0:T(8,128)S(1)}, f32[92,128]{1,0:T(8,128)S(1)}, u32[]{:S(2)}, u32[]{:S(2)}) collective-permute-start(f32[92,128]{1,0:T(8,128)S(1)} %get-tuple-element.19), channel_id=1, source_target_pairs={{0,15},{1,2},{2,1},{3,4},{4,3},{5,6},{6,5},{7,8},{8,7},{9,10},{10,... | collective-permute-start | bytes 141320 | tf_op jit(solution)/shard_map/ppermute | solution.py:719
  16.8 0.0 collective-permute-start.3
  16.8 1.7 %collective-permute-start.4 = (f32[46,128]{1,0:T(8,128)S(1)}, f32[46,128]{1,0:T(8,128)S(1)}, u32[]{:S(2)}, u32[]{:S(2)}) collective-permute-start(f32[46,128]{1,0:T(8,128)S(1)} %get-tuple-element.21), channel_id=1, source_target_pairs={{0,31},{1,18},{2,17},{3,20},{4,19},{5,22},{6,21},{7,24},{8,23},{9,... | collective-permute-start | bytes 70664 | tf_op jit(solution)/shard_map/ppermute | solution.py:719
  18.6 1.5 %collective-permute-done.3.rest_3_ = f32[46,128]{1,0:T(8,128)S(1)} collective-permute-done((f32[46,128]{1,0:T(8,128)S(1)}, f32[46,128]{1,0:T(8,128)S(1)}, u32[]{:S(2)}, u32[]{:S(2)}) %collective-permute-start.3) | collective-permute-done | bytes 23584 | tf_op jit(solution)/shard_map/ppermute | solution.py:719
  20.1 4.1 %collective-permute-done.4.rest_4_ = f32[46,128]{1,0:T(8,128)S(1)} collective-permute-done((f32[46,128]{1,0:T(8,128)S(1)}, f32[46,128]{1,0:T(8,128)S(1)}, u32[]{:S(2)}, u32[]{:S(2)}) %collective-permute-start.4) | collective-permute-done | bytes 23584 | tf_op jit(solution)/shard_map/ppermute | solution.py:719
  24.2 0.0 collective-permute-done.1.rest_1_
  24.2 0.0 collective-permute-done.2.rest_2_
  24.2 0.0 collective-permute-done.rest_0_
  24.2 1.8 %shard_map.43 = (f32[16,24,128]{2,1,0:T(8,128)S(1)}, f32[3,16,24,128]{3,2,1,0:T(8,128)S(1)}, f32[16,24,128]{2,1,0:T(8,128)S(1)}, f32[3,4,24,128]{3,2,1,0:T(8,128...) custom-call(f32[8,16,128]{2,1,0:T(8,128)S(1)} %copy-done.1, f32[19,4,4,128]{3,2,1,0:T(4,128)S(1)} %copy-done, ...), custom_call_target="tpu_custom_call" | custom-call | tf_op jit(solution)/shard_map/pallas_call | solution.py:699
  26.0 0.0 all-to-all-done
  26.0 1.8 %shard_map.44 = (f32[8,16,128]{2,1,0:T(8,128)}, f32[19,4,4,128]{3,2,1,0:T(4,128)}) custom-call(f32[2,16,24,128]{3,2,1,0:T(8,128)S(1)} %bitcast.2, f32[16,24,128]{2,1,0:T(8,128)S(1)} %get-tuple-element.22.base, f32[3,16,24,128]{3,2,1,0:T(8,128)S(1)} %get-tuple-element.23.slope, f32[16,24,128]{2,1,0:T(8,128)S(1)} %get-tuple-element.24.drift, ...), custom_call_target="tpu_custom_call" | custom-call | tf_op jit(solution)/shard_map/pallas_call | solution.py:699
Async XLA Ops:
  3.1 7.4 %copy-start = (f32[19,4,4,128]{3,2,1,0:T(4,128)S(1)}, f32[19,4,4,128]{3,2,1,0:T(4,128)}, u32[]{:S(2)}) copy-start(f32[19,4,4,128]{3,2,1,0:T(4,128)} %populations.3) | copy-start | bytes 466948
  3.2 7.4 %copy-start.1 = (f32[8,16,128]{2,1,0:T(8,128)S(1)}, f32[8,16,128]{2,1,0:T(8,128)}, u32[]{:S(2)}) copy-start(f32[8,16,128]{2,1,0:T(8,128)} %density.3) | copy-start | bytes 196612
  3.2 7.4 %copy-start.2 = (f32[4,4,4,128]{3,2,1,0:T(4,128)S(1)}, f32[4,4,4,128]{3,2,1,0:T(4,128)}, u32[]{:S(2)}) copy-start(f32[4,4,4,128]{3,2,1,0:T(4,128)} %get-tuple-element.16.moments) | copy-start | bytes 98308
  3.2 22.8 %all-to-all-start = ((f32[32,24,128]{2,1,0:T(8,128)}), f32[32,24,128]{2,1,0:T(8,128)S(1)}, u32[]{:S(2)}, u32[]{:S(2)}) async-start(f32[32,24,128]{2,1,0:T(8,128)} %bitcast.3), calls=%async_computation | async-start | bytes 786432 | tf_op jit(solution)/shard_map/all_to_all | solution.py:731
  10.6 13.6 %collective-permute-start = (f32[200,128]{1,0:T(8,128)S(1)}, f32[200,128]{1,0:T(8,128)S(1)}, u32[]{:S(2)}, u32[]{:S(2)}) collective-permute-start(f32[200,128]{1,0:T(8,128)S(1)} %get-tuple-element.17), channel_id=1, source_target_pairs={{0,16},{1,17},{2,18},{3,19},{4,20},{5,21},{6,22},{7,23},{8,24},{9,... | collective-permute-start | bytes 307208 | tf_op jit(solution)/shard_map/ppermute | solution.py:719
  12.5 11.7 %collective-permute-start.1 = (f32[92,128]{1,0:T(8,128)S(1)}, f32[92,128]{1,0:T(8,128)S(1)}, u32[]{:S(2)}, u32[]{:S(2)}) collective-permute-start(f32[92,128]{1,0:T(8,128)S(1)} %get-tuple-element.18), channel_id=1, source_target_pairs={{0,1},{1,0},{2,3},{3,2},{4,5},{5,4},{6,7},{7,6},{8,9},{9,8},{10,11... | collective-permute-start | bytes 141320 | tf_op jit(solution)/shard_map/ppermute | solution.py:719
  12.5 11.7 %collective-permute-start.2 = (f32[92,128]{1,0:T(8,128)S(1)}, f32[92,128]{1,0:T(8,128)S(1)}, u32[]{:S(2)}, u32[]{:S(2)}) collective-permute-start(f32[92,128]{1,0:T(8,128)S(1)} %get-tuple-element.19), channel_id=1, source_target_pairs={{0,15},{1,2},{2,1},{3,4},{4,3},{5,6},{6,5},{7,8},{8,7},{9,10},{10,... | collective-permute-start | bytes 141320 | tf_op jit(solution)/shard_map/ppermute | solution.py:719
  16.8 3.3 %collective-permute-start.3 = (f32[46,128]{1,0:T(8,128)S(1)}, f32[46,128]{1,0:T(8,128)S(1)}, u32[]{:S(2)}, u32[]{:S(2)}) collective-permute-start(f32[46,128]{1,0:T(8,128)S(1)} %get-tuple-element.20), channel_id=1, source_target_pairs={{0,17},{1,16},{2,19},{3,18},{4,21},{5,20},{6,23},{7,22},{8,25},{9,... | collective-permute-start | bytes 70664 | tf_op jit(solution)/shard_map/ppermute | solution.py:719
  16.8 7.3 %collective-permute-start.4 = (f32[46,128]{1,0:T(8,128)S(1)}, f32[46,128]{1,0:T(8,128)S(1)}, u32[]{:S(2)}, u32[]{:S(2)}) collective-permute-start(f32[46,128]{1,0:T(8,128)S(1)} %get-tuple-element.21), channel_id=1, source_target_pairs={{0,31},{1,18},{2,17},{3,20},{4,19},{5,22},{6,21},{7,24},{8,23},{9,... | collective-permute-start | bytes 70664 | tf_op jit(solution)/shard_map/ppermute | solution.py:719

commit v8 on v7

--- a/solution.py
+++ b/solution.py
@@ -316,36 +316,35 @@
     return running + (along_z(value)[0] if beside is None else beside)
 
 
-def potential_at(plan, grid, lap, pot, reach, part, grid_slope, pot_beside=None, pot_slope=None):
+def potential_at(plan, grid, lap, pot, reach, part, slope):
     rows = slice(ROWS + part.start, ROWS + part.stop)
     for x in plan.span(-reach, plan.x + reach):
         here = plan.layer(x)
-        beside, grid_slope[here, rows] = along_z(grid[here, rows])
+        beside, slope[here, rows] = along_z(grid[here, rows])
         lap[here, rows] = laplace_at(plan, grid, x, part, beside)
     for x in plan.span(1 - reach, plan.x + reach - 1):
         here = plan.layer(x)
         value = grid[here, rows]
-        value = (
+        pot[here, rows] = (
             (quench_depth + 1.0) * value
             + 2.0 * lap[here, rows]
             + laplace_at(plan, lap, x, part)
             + value * value * value
         )
-        pot[here, rows] = value
-        if pot_slope is not None:
-            pot_beside[here, rows], pot_slope[here, rows] = along_z(value)
-
-
-def central_at(plan, source, slope, x, c, part):
+
+
+def central_at(plan, source, x, c, part, slope=None):
     if c == 0:
         return shifted_rows(plan, source, x + 1, part) - shifted_rows(plan, source, x - 1, part)
     if c == 1:
         return shifted_rows(plan, source, x, part, 1) - shifted_rows(plan, source, x, part, -1)
+    if slope is None:
+        return along_z(shifted_rows(plan, source, x, part))[1]
     return shifted_rows(plan, slope, x, part)
 
 
 def first_substep(plan, density, halo, base, slope, drift, push, arrays, pooled):
-    grid, lap, pot, grid_slope, pot_beside, pot_slope = arrays
+    grid, lap, pot, grid_slope = arrays
     from_low, from_high, from_below, from_above, below_low, below_high, above_low, above_high = halo
     sets = [(0, None, from_below, from_above)]
     if plan.pair:
@@ -367,7 +366,7 @@
             grid[here, own + plan.y : own + plan.y + rows] = above(start, rows, 1)
     whole = slice(0, plan.y + 2 * ROWS)
     inner = slice(ROWS // 2, ROWS // 2 + plan.frame)
-    potential_at(plan, grid, lap, pot, 6, whole, grid_slope, pot_beside, pot_slope)
+    potential_at(plan, grid, lap, pot, 6, whole, grid_slope)
     pairs = (plan.y + 2 * ROWS) // 2
     odd = (lax.broadcasted_iota(jnp.int32, (pairs, plan.z), 1) & 1) != 0
     reach = 3 * (DENSITY_SUBSTEPS - 1)
@@ -378,7 +377,7 @@
         for c in range(3):
             total = None
             for x in (2 * coarse, 2 * coarse + 1):
-                now = shifted_rows(plan, grid, x, whole) * central_at(plan, pot, pot_slope, x, c, whole)
+                now = shifted_rows(plan, grid, x, whole) * central_at(plan, pot, x, c, whole)
                 total = now if total is None else total + now
             own_scratch = pooled[c * (plan.xc + 4) + coarse + 2]
             own_scratch[...] = total
@@ -396,13 +395,10 @@
             if here not in wanted or here in done:
                 continue
             done.add(here)
-            beside = shifted_rows(plan, pot_beside, x, inner)
-            base[here] = shifted_rows(plan, grid, x, inner) + coupled_time_step * laplace_at(
-                plan, pot, x, inner, beside
-            )
+            base[here] = shifted_rows(plan, grid, x, inner) + coupled_time_step * laplace_at(plan, pot, x, inner)
             total = None
             for c in range(3):
-                scaled = central_at(plan, grid, grid_slope, x, c, inner) * (0.5 * speed_unit * coupled_time_step)
+                scaled = central_at(plan, grid, x, c, inner, grid_slope) * (0.5 * speed_unit * coupled_time_step)
                 slope[c, here] = scaled
                 now = force[c] * scaled
                 total = now if total is None else total + now
@@ -659,7 +655,7 @@
         for x in (2 * coarse, 2 * coarse + 1):
             change = laplace_at(plan, pot, x, inner)
             for c in range(3):
-                change = change - speed[c] * central_at(plan, grid, grid_slope, x, c, inner)
+                change = change - speed[c] * central_at(plan, grid, x, c, inner, grid_slope)
             out[x] = shifted_rows(plan, grid, x, inner) + coupled_time_step * change
 
 
@@ -797,7 +793,7 @@
             ((MOMENTS, plan.xc + 2, ROWS, plan.yc), VMEM),
             ((len(SPEEDS), plan.xc + 2, ROWS, plan.yc), VMEM),
         ],
-        [[tall] * 6, [(plan.y + 2 * ROWS, plan.z)] * (3 * (plan.xc + 4))],
+        [[tall] * 4, [(plan.y + 2 * ROWS, plan.z)] * (3 * (plan.xc + 4))],
     )
     side = [[(plan.planes, ROWS * plan.pitch, LANES)] * 2] * pl.cdiv(plan.window, ROWS)
     return call(

time: 28 us -> 27.5 us (0.982)
  Pallas kernels: 6.17 us -> 5.66 us
    pallas_call x4, Pallas kernels: 6.17 us -> 5.66 us  [call(): pl.pallas_call(kernel, out_shape=[jax.ShapeDtypeStruct(shape, jnp.float32...]
  transfers between devices with their start and end apart: 6 -> 6, of which waited for: 2 -> 2; matrix products, arithmetic and copies ran while one was open for 0% -> 0% of each run, Pallas kernels for 7% -> 5%
where the time goes in v8:
time: 27.5 us; the launch traced here: 27.3 us
  starting transfers between devices  15.3 us (56%)
  Pallas kernels  5.66 us (21%)
  waiting for transfers between devices  5.62 us (20%)
  between operations  0.72 us (3%)
    ppermute x5, starting transfers between devices, shifted(): return lax.ppermute(value, everywhere, pairs)  7.94 us
    all_to_all x1, starting transfers between devices, exchange(): lax.all_to_all(send.reshape(plan.gx * plan.gy, plan.rows, LANES), everywh...  7.33 us
    pallas_call x4, Pallas kernels, call(): pl.pallas_call(kernel, out_shape=[jax.ShapeDtypeStruct(shape, jnp.float32...  5.66 us
    ppermute x5, waiting for transfers between devices, shifted(): return lax.ppermute(value, everywhere, pairs)  5.62 us
  transfers between devices with their start and end apart: 6, of which 2 were waited for; matrix products, arithmetic and copies ran while one was open for 0% of the time, Pallas kernels for 5%

profile of v8, /device:TPU:0, one launch (start us, length us, event | category | flops | bytes accessed | tf_op | source)
XLA Modules:
  0.0 27.3 jit_solution(15291407115032497121)
XLA Ops:
  0.6 2.5 %shard_map.41 = (f32[2,16,24,128]{3,2,1,0:T(8,128)}, f32[4,4,4,128]{3,2,1,0:T(4,128)}) custom-call(f32[8,16,128]{2,1,0:T(8,128)} %density.3, f32[19,4,4,128]{3,2,1,0:T(4,128)} %populations.3), custom_call_target="tpu_custom_call" | custom-call | tf_op jit(solution)/shard_map/pallas_call | solution.py:695
  3.1 0.0 copy-start
  3.2 0.0 copy-start.1
  3.2 0.0 copy-start.2
  3.2 7.3 %all-to-all-start = ((f32[32,24,128]{2,1,0:T(8,128)}), f32[32,24,128]{2,1,0:T(8,128)S(1)}, u32[]{:S(2)}, u32[]{:S(2)}) async-start(f32[32,24,128]{2,1,0:T(8,128)} %bitcast.3), calls=%async_computation | async-start | bytes 786432 | tf_op jit(solution)/shard_map/all_to_all | solution.py:727
  10.5 0.0 copy-done
  10.5 0.0 copy-done.1
  10.5 0.0 copy-done.2
  10.6 0.1 shard_map.42
  10.6 1.8 %collective-permute-start = (f32[200,128]{1,0:T(8,128)S(1)}, f32[200,128]{1,0:T(8,128)S(1)}, u32[]{:S(2)}, u32[]{:S(2)}) collective-permute-start(f32[200,128]{1,0:T(8,128)S(1)} %get-tuple-element.17), channel_id=1, source_target_pairs={{0,16},{1,17},{2,18},{3,19},{4,20},{5,21},{6,22},{7,23},{8,24},{9,... | collective-permute-start | bytes 307208 | tf_op jit(solution)/shard_map/ppermute | solution.py:715
  12.5 0.0 collective-permute-start.1
  12.5 4.4 %collective-permute-start.2 = (f32[92,128]{1,0:T(8,128)S(1)}, f32[92,128]{1,0:T(8,128)S(1)}, u32[]{:S(2)}, u32[]{:S(2)}) collective-permute-start(f32[92,128]{1,0:T(8,128)S(1)} %get-tuple-element.19), channel_id=1, source_target_pairs={{0,15},{1,2},{2,1},{3,4},{4,3},{5,6},{6,5},{7,8},{8,7},{9,10},{10,... | collective-permute-start | bytes 141320 | tf_op jit(solution)/shard_map/ppermute | solution.py:715
  16.8 0.0 collective-permute-start.3
  16.8 1.7 %collective-permute-start.4 = (f32[46,128]{1,0:T(8,128)S(1)}, f32[46,128]{1,0:T(8,128)S(1)}, u32[]{:S(2)}, u32[]{:S(2)}) collective-permute-start(f32[46,128]{1,0:T(8,128)S(1)} %get-tuple-element.21), channel_id=1, source_target_pairs={{0,31},{1,18},{2,17},{3,20},{4,19},{5,22},{6,21},{7,24},{8,23},{9,... | collective-permute-start | bytes 70664 | tf_op jit(solution)/shard_map/ppermute | solution.py:715
  18.6 1.5 %collective-permute-done.3.rest_3_ = f32[46,128]{1,0:T(8,128)S(1)} collective-permute-done((f32[46,128]{1,0:T(8,128)S(1)}, f32[46,128]{1,0:T(8,128)S(1)}, u32[]{:S(2)}, u32[]{:S(2)}) %collective-permute-start.3) | collective-permute-done | bytes 23584 | tf_op jit(solution)/shard_map/ppermute | solution.py:715
  20.1 4.1 %collective-permute-done.4.rest_4_ = f32[46,128]{1,0:T(8,128)S(1)} collective-permute-done((f32[46,128]{1,0:T(8,128)S(1)}, f32[46,128]{1,0:T(8,128)S(1)}, u32[]{:S(2)}, u32[]{:S(2)}) %collective-permute-start.4) | collective-permute-done | bytes 23584 | tf_op jit(solution)/shard_map/ppermute | solution.py:715
  24.2 0.0 collective-permute-done.1.rest_1_
  24.2 0.0 collective-permute-done.2.rest_2_
  24.2 0.0 collective-permute-done.rest_0_
  24.2 1.3 %shard_map.43 = (f32[16,24,128]{2,1,0:T(8,128)S(1)}, f32[3,16,24,128]{3,2,1,0:T(8,128)S(1)}, f32[16,24,128]{2,1,0:T(8,128)S(1)}, f32[3,4,24,128]{3,2,1,0:T(8,128...) custom-call(f32[8,16,128]{2,1,0:T(8,128)S(1)} %copy-done.1, f32[19,4,4,128]{3,2,1,0:T(4,128)S(1)} %copy-done, ...), custom_call_target="tpu_custom_call" | custom-call | tf_op jit(solution)/shard_map/pallas_call | solution.py:695
  25.5 0.0 all-to-all-done
  25.5 1.8 %shard_map.44 = (f32[8,16,128]{2,1,0:T(8,128)}, f32[19,4,4,128]{3,2,1,0:T(4,128)}) custom-call(f32[2,16,24,128]{3,2,1,0:T(8,128)S(1)} %bitcast.2, f32[16,24,128]{2,1,0:T(8,128)S(1)} %get-tuple-element.22.base, f32[3,16,24,128]{3,2,1,0:T(8,128)S(1)} %get-tuple-element.23.slope, f32[16,24,128]{2,1,0:T(8,128)S(1)} %get-tuple-element.24.drift, ...), custom_call_target="tpu_custom_call" | custom-call | tf_op jit(solution)/shard_map/pallas_call | solution.py:695
Async XLA Ops:
  3.1 7.4 %copy-start = (f32[19,4,4,128]{3,2,1,0:T(4,128)S(1)}, f32[19,4,4,128]{3,2,1,0:T(4,128)}, u32[]{:S(2)}) copy-start(f32[19,4,4,128]{3,2,1,0:T(4,128)} %populations.3) | copy-start | bytes 466948
  3.2 7.4 %copy-start.1 = (f32[8,16,128]{2,1,0:T(8,128)S(1)}, f32[8,16,128]{2,1,0:T(8,128)}, u32[]{:S(2)}) copy-start(f32[8,16,128]{2,1,0:T(8,128)} %density.3) | copy-start | bytes 196612
  3.2 7.4 %copy-start.2 = (f32[4,4,4,128]{3,2,1,0:T(4,128)S(1)}, f32[4,4,4,128]{3,2,1,0:T(4,128)}, u32[]{:S(2)}) copy-start(f32[4,4,4,128]{3,2,1,0:T(4,128)} %get-tuple-element.16.moments) | copy-start | bytes 98308
  3.2 22.3 %all-to-all-start = ((f32[32,24,128]{2,1,0:T(8,128)}), f32[32,24,128]{2,1,0:T(8,128)S(1)}, u32[]{:S(2)}, u32[]{:S(2)}) async-start(f32[32,24,128]{2,1,0:T(8,128)} %bitcast.3), calls=%async_computation | async-start | bytes 786432 | tf_op jit(solution)/shard_map/all_to_all | solution.py:727
  10.6 13.6 %collective-permute-start = (f32[200,128]{1,0:T(8,128)S(1)}, f32[200,128]{1,0:T(8,128)S(1)}, u32[]{:S(2)}, u32[]{:S(2)}) collective-permute-start(f32[200,128]{1,0:T(8,128)S(1)} %get-tuple-element.17), channel_id=1, source_target_pairs={{0,16},{1,17},{2,18},{3,19},{4,20},{5,21},{6,22},{7,23},{8,24},{9,... | collective-permute-start | bytes 307208 | tf_op jit(solution)/shard_map/ppermute | solution.py:715
  12.5 11.7 %collective-permute-start.1 = (f32[92,128]{1,0:T(8,128)S(1)}, f32[92,128]{1,0:T(8,128)S(1)}, u32[]{:S(2)}, u32[]{:S(2)}) collective-permute-start(f32[92,128]{1,0:T(8,128)S(1)} %get-tuple-element.18), channel_id=1, source_target_pairs={{0,1},{1,0},{2,3},{3,2},{4,5},{5,4},{6,7},{7,6},{8,9},{9,8},{10,11... | collective-permute-start | bytes 141320 | tf_op jit(solution)/shard_map/ppermute | solution.py:715
  12.5 11.7 %collective-permute-start.2 = (f32[92,128]{1,0:T(8,128)S(1)}, f32[92,128]{1,0:T(8,128)S(1)}, u32[]{:S(2)}, u32[]{:S(2)}) collective-permute-start(f32[92,128]{1,0:T(8,128)S(1)} %get-tuple-element.19), channel_id=1, source_target_pairs={{0,15},{1,2},{2,1},{3,4},{4,3},{5,6},{6,5},{7,8},{8,7},{9,10},{10,... | collective-permute-start | bytes 141320 | tf_op jit(solution)/shard_map/ppermute | solution.py:715
  16.8 3.3 %collective-permute-start.3 = (f32[46,128]{1,0:T(8,128)S(1)}, f32[46,128]{1,0:T(8,128)S(1)}, u32[]{:S(2)}, u32[]{:S(2)}) collective-permute-start(f32[46,128]{1,0:T(8,128)S(1)} %get-tuple-element.20), channel_id=1, source_target_pairs={{0,17},{1,16},{2,19},{3,18},{4,21},{5,20},{6,23},{7,22},{8,25},{9,... | collective-permute-start | bytes 70664 | tf_op jit(solution)/shard_map/ppermute | solution.py:715
  16.8 7.3 %collective-permute-start.4 = (f32[46,128]{1,0:T(8,128)S(1)}, f32[46,128]{1,0:T(8,128)S(1)}, u32[]{:S(2)}, u32[]{:S(2)}) collective-permute-start(f32[46,128]{1,0:T(8,128)S(1)} %get-tuple-element.21), channel_id=1, source_target_pairs={{0,31},{1,18},{2,17},{3,20},{4,19},{5,22},{6,21},{7,24},{8,23},{9,... | collective-permute-start | bytes 70664 | tf_op jit(solution)/shard_map/ppermute | solution.py:715

commit v9 on v8

--- a/solution.py
+++ b/solution.py
@@ -373,11 +373,15 @@
     wanted = {plan.layer(x): x for x in plan.span(-reach, plan.x + reach)}
     done = set()
     for coarse in range(-2, plan.xc + 2):
+        pair = (2 * coarse, 2 * coarse + 1)
+        beside = {x: along_z(shifted_rows(plan, pot, x, whole)) for x in pair}
         force = []
         for c in range(3):
             total = None
-            for x in (2 * coarse, 2 * coarse + 1):
-                now = shifted_rows(plan, grid, x, whole) * central_at(plan, pot, x, c, whole)
+            for x in pair:
+                now = shifted_rows(plan, grid, x, whole) * (
+                    beside[x][1] if c == 2 else central_at(plan, pot, x, c, whole)
+                )
                 total = now if total is None else total + now
             own_scratch = pooled[c * (plan.xc + 4) + coarse + 2]
             own_scratch[...] = total
@@ -390,12 +394,14 @@
             force.append(own_scratch[inner, :])
             if 0 <= coarse < plan.xc:
                 push[c, coarse] = force[c]
-        for x in (2 * coarse, 2 * coarse + 1):
+        for x in pair:
             here = plan.layer(x)
             if here not in wanted or here in done:
                 continue
             done.add(here)
-            base[here] = shifted_rows(plan, grid, x, inner) + coupled_time_step * laplace_at(plan, pot, x, inner)
+            base[here] = shifted_rows(plan, grid, x, whole) + coupled_time_step * laplace_at(
+                plan, pot, x, whole, beside[x][0]
+            )
             total = None
             for c in range(3):
                 scaled = central_at(plan, grid, x, c, inner, grid_slope) * (0.5 * speed_unit * coupled_time_step)
@@ -644,7 +650,8 @@
         advection = drift[here]
         for c in range(3):
             advection = advection + flow[c + 1][slot][...] * slope[c, here]
-        grid[here, ROWS : ROWS + plan.frame] = base[here] - advection * inverses[slot]
+        start = base[here, own_row : own_row + plan.frame]
+        grid[here, ROWS : ROWS + plan.frame] = start - advection * inverses[slot]
     whole = slice(0, plan.frame)
     inner = slice(own_row, own_row + plan.y)
     potential_at(plan, grid, lap, pot, 2, whole, grid_slope)
@@ -786,7 +793,7 @@
         functools.partial(prepare_kernel, plan),
         own + [(value, VMEM) for value in halo],
         [
-            (short, VMEM),
+            ((plan.layers, plan.y + 2 * ROWS, plan.z), VMEM),
             ((3,) + short, VMEM),
             (short, VMEM),
             ((3, plan.xc, plan.frame, plan.z), VMEM),

time: 27.5 us -> 27.3 us (level)
  transfers between devices with their start and end apart: 6 -> 6, of which waited for: 2 -> 2; matrix products, arithmetic and copies ran while one was open for 0% -> 0% of each run, Pallas kernels for 5% -> 4%
where the time goes in v9:
time: 27.3 us; the launch traced here: 27.1 us
  starting transfers between devices  15.3 us (56%)
  waiting for transfers between devices  5.62 us (21%)
  Pallas kernels  5.47 us (20%)
  between operations  0.72 us (3%)
    ppermute x5, starting transfers between devices, shifted(): return lax.ppermute(value, everywhere, pairs)  7.94 us
    all_to_all x1, starting transfers between devices, exchange(): lax.all_to_all(send.reshape(plan.gx * plan.gy, plan.rows, LANES), everywh...  7.33 us
    ppermute x5, waiting for transfers between devices, shifted(): return lax.ppermute(value, everywhere, pairs)  5.62 us
    pallas_call x4, Pallas kernels, call(): pl.pallas_call(kernel, out_shape=[jax.ShapeDtypeStruct(shape, jnp.float32...  5.47 us
  transfers between devices with their start and end apart: 6, of which 2 were waited for; matrix products, arithmetic and copies ran while one was open for 0% of the time, Pallas kernels for 4%

profile of v9, /device:TPU:0, one launch (start us, length us, event | category | flops | bytes accessed | tf_op | source)
XLA Modules:
  0.0 27.1 jit_solution(13314121666130560855)
XLA Ops:
  0.6 2.5 %shard_map.41 = (f32[2,16,24,128]{3,2,1,0:T(8,128)}, f32[4,4,4,128]{3,2,1,0:T(4,128)}) custom-call(f32[8,16,128]{2,1,0:T(8,128)} %density.3, f32[19,4,4,128]{3,2,1,0:T(4,128)} %populations.3), custom_call_target="tpu_custom_call" | custom-call | tf_op jit(solution)/shard_map/pallas_call | solution.py:702
  3.1 0.0 copy-start
  3.2 0.0 copy-start.1
  3.2 0.0 copy-start.2
  3.2 7.3 %all-to-all-start = ((f32[32,24,128]{2,1,0:T(8,128)}), f32[32,24,128]{2,1,0:T(8,128)S(1)}, u32[]{:S(2)}, u32[]{:S(2)}) async-start(f32[32,24,128]{2,1,0:T(8,128)} %bitcast.3), calls=%async_computation | async-start | bytes 786432 | tf_op jit(solution)/shard_map/all_to_all | solution.py:734
  10.5 0.0 copy-done
  10.5 0.0 copy-done.1
  10.5 0.0 copy-done.2
  10.6 0.1 shard_map.42
  10.6 1.8 %collective-permute-start = (f32[200,128]{1,0:T(8,128)S(1)}, f32[200,128]{1,0:T(8,128)S(1)}, u32[]{:S(2)}, u32[]{:S(2)}) collective-permute-start(f32[200,128]{1,0:T(8,128)S(1)} %get-tuple-element.17), channel_id=1, source_target_pairs={{0,16},{1,17},{2,18},{3,19},{4,20},{5,21},{6,22},{7,23},{8,24},{9,... | collective-permute-start | bytes 307208 | tf_op jit(solution)/shard_map/ppermute | solution.py:722
  12.5 0.0 collective-permute-start.1
  12.5 4.4 %collective-permute-start.2 = (f32[92,128]{1,0:T(8,128)S(1)}, f32[92,128]{1,0:T(8,128)S(1)}, u32[]{:S(2)}, u32[]{:S(2)}) collective-permute-start(f32[92,128]{1,0:T(8,128)S(1)} %get-tuple-element.19), channel_id=1, source_target_pairs={{0,15},{1,2},{2,1},{3,4},{4,3},{5,6},{6,5},{7,8},{8,7},{9,10},{10,... | collective-permute-start | bytes 141320 | tf_op jit(solution)/shard_map/ppermute | solution.py:722
  16.8 0.0 collective-permute-start.3
  16.8 1.7 %collective-permute-start.4 = (f32[46,128]{1,0:T(8,128)S(1)}, f32[46,128]{1,0:T(8,128)S(1)}, u32[]{:S(2)}, u32[]{:S(2)}) collective-permute-start(f32[46,128]{1,0:T(8,128)S(1)} %get-tuple-element.21), channel_id=1, source_target_pairs={{0,31},{1,18},{2,17},{3,20},{4,19},{5,22},{6,21},{7,24},{8,23},{9,... | collective-permute-start | bytes 70664 | tf_op jit(solution)/shard_map/ppermute | solution.py:722
  18.6 1.5 %collective-permute-done.3.rest_3_ = f32[46,128]{1,0:T(8,128)S(1)} collective-permute-done((f32[46,128]{1,0:T(8,128)S(1)}, f32[46,128]{1,0:T(8,128)S(1)}, u32[]{:S(2)}, u32[]{:S(2)}) %collective-permute-start.3) | collective-permute-done | bytes 23584 | tf_op jit(solution)/shard_map/ppermute | solution.py:722
  20.1 4.1 %collective-permute-done.4.rest_4_ = f32[46,128]{1,0:T(8,128)S(1)} collective-permute-done((f32[46,128]{1,0:T(8,128)S(1)}, f32[46,128]{1,0:T(8,128)S(1)}, u32[]{:S(2)}, u32[]{:S(2)}) %collective-permute-start.4) | collective-permute-done | bytes 23584 | tf_op jit(solution)/shard_map/ppermute | solution.py:722
  24.2 0.0 collective-permute-done.1.rest_1_
  24.2 0.0 collective-permute-done.2.rest_2_
  24.2 0.0 collective-permute-done.rest_0_
  24.2 1.1 %shard_map.43 = (f32[16,32,128]{2,1,0:T(8,128)S(1)}, f32[3,16,24,128]{3,2,1,0:T(8,128)S(1)}, f32[16,24,128]{2,1,0:T(8,128)S(1)}, f32[3,4,24,128]{3,2,1,0:T(8,128...) custom-call(f32[8,16,128]{2,1,0:T(8,128)S(1)} %copy-done.1, f32[19,4,4,128]{3,2,1,0:T(4,128)S(1)} %copy-done, ...), custom_call_target="tpu_custom_call" | custom-call | tf_op jit(solution)/shard_map/pallas_call | solution.py:702
  25.3 0.0 all-to-all-done
  25.3 1.8 %shard_map.44 = (f32[8,16,128]{2,1,0:T(8,128)}, f32[19,4,4,128]{3,2,1,0:T(4,128)}) custom-call(f32[2,16,24,128]{3,2,1,0:T(8,128)S(1)} %bitcast.2, f32[16,32,128]{2,1,0:T(8,128)S(1)} %get-tuple-element.22.base, f32[3,16,24,128]{3,2,1,0:T(8,128)S(1)} %get-tuple-element.23.slope, f32[16,24,128]{2,1,0:T(8,128)S(1)} %get-tuple-element.24.drift, ...), custom_call_target="tpu_custom_call" | custom-call | tf_op jit(solution)/shard_map/pallas_call | solution.py:702
Async XLA Ops:
  3.1 7.4 %copy-start = (f32[19,4,4,128]{3,2,1,0:T(4,128)S(1)}, f32[19,4,4,128]{3,2,1,0:T(4,128)}, u32[]{:S(2)}) copy-start(f32[19,4,4,128]{3,2,1,0:T(4,128)} %populations.3) | copy-start | bytes 466948
  3.2 7.4 %copy-start.1 = (f32[8,16,128]{2,1,0:T(8,128)S(1)}, f32[8,16,128]{2,1,0:T(8,128)}, u32[]{:S(2)}) copy-start(f32[8,16,128]{2,1,0:T(8,128)} %density.3) | copy-start | bytes 196612
  3.2 7.4 %copy-start.2 = (f32[4,4,4,128]{3,2,1,0:T(4,128)S(1)}, f32[4,4,4,128]{3,2,1,0:T(4,128)}, u32[]{:S(2)}) copy-start(f32[4,4,4,128]{3,2,1,0:T(4,128)} %get-tuple-element.16.moments) | copy-start | bytes 98308
  3.2 22.1 %all-to-all-start = ((f32[32,24,128]{2,1,0:T(8,128)}), f32[32,24,128]{2,1,0:T(8,128)S(1)}, u32[]{:S(2)}, u32[]{:S(2)}) async-start(f32[32,24,128]{2,1,0:T(8,128)} %bitcast.3), calls=%async_computation | async-start | bytes 786432 | tf_op jit(solution)/shard_map/all_to_all | solution.py:734
  10.6 13.6 %collective-permute-start = (f32[200,128]{1,0:T(8,128)S(1)}, f32[200,128]{1,0:T(8,128)S(1)}, u32[]{:S(2)}, u32[]{:S(2)}) collective-permute-start(f32[200,128]{1,0:T(8,128)S(1)} %get-tuple-element.17), channel_id=1, source_target_pairs={{0,16},{1,17},{2,18},{3,19},{4,20},{5,21},{6,22},{7,23},{8,24},{9,... | collective-permute-start | bytes 307208 | tf_op jit(solution)/shard_map/ppermute | solution.py:722
  12.5 11.7 %collective-permute-start.1 = (f32[92,128]{1,0:T(8,128)S(1)}, f32[92,128]{1,0:T(8,128)S(1)}, u32[]{:S(2)}, u32[]{:S(2)}) collective-permute-start(f32[92,128]{1,0:T(8,128)S(1)} %get-tuple-element.18), channel_id=1, source_target_pairs={{0,1},{1,0},{2,3},{3,2},{4,5},{5,4},{6,7},{7,6},{8,9},{9,8},{10,11... | collective-permute-start | bytes 141320 | tf_op jit(solution)/shard_map/ppermute | solution.py:722
  12.5 11.7 %collective-permute-start.2 = (f32[92,128]{1,0:T(8,128)S(1)}, f32[92,128]{1,0:T(8,128)S(1)}, u32[]{:S(2)}, u32[]{:S(2)}) collective-permute-start(f32[92,128]{1,0:T(8,128)S(1)} %get-tuple-element.19), channel_id=1, source_target_pairs={{0,15},{1,2},{2,1},{3,4},{4,3},{5,6},{6,5},{7,8},{8,7},{9,10},{10,... | collective-permute-start | bytes 141320 | tf_op jit(solution)/shard_map/ppermute | solution.py:722
  16.8 3.3 %collective-permute-start.3 = (f32[46,128]{1,0:T(8,128)S(1)}, f32[46,128]{1,0:T(8,128)S(1)}, u32[]{:S(2)}, u32[]{:S(2)}) collective-permute-start(f32[46,128]{1,0:T(8,128)S(1)} %get-tuple-element.20), channel_id=1, source_target_pairs={{0,17},{1,16},{2,19},{3,18},{4,21},{5,20},{6,23},{7,22},{8,25},{9,... | collective-permute-start | bytes 70664 | tf_op jit(solution)/shard_map/ppermute | solution.py:722
  16.8 7.3 %collective-permute-start.4 = (f32[46,128]{1,0:T(8,128)S(1)}, f32[46,128]{1,0:T(8,128)S(1)}, u32[]{:S(2)}, u32[]{:S(2)}) collective-permute-start(f32[46,128]{1,0:T(8,128)S(1)} %get-tuple-element.21), channel_id=1, source_target_pairs={{0,31},{1,18},{2,17},{3,20},{4,19},{5,22},{6,21},{7,24},{8,23},{9,... | collective-permute-start | bytes 70664 | tf_op jit(solution)/shard_map/ppermute | solution.py:722

commit v10 on v9

--- a/solution.py
+++ b/solution.py
@@ -227,7 +227,7 @@
         packed = jnp.where(
             (y < 2) | (y >= plan.yb - 2),
             first,
-            jnp.where(y < 4, roll(second, 2, 1), roll(second, -2, 1)),
+            roll(second, plan.yb // 2, 1),
         )
         at = plan.window
         pieces[target, at : at + plan.zc, :] = turned[target]
@@ -634,8 +634,9 @@
             for x in range(plan.xc):
                 at = (f * plan.xc + x) * yb
                 target = flow[f][block * plan.xc + x]
-                after = first[at : at + 2] + second[at + 2 : at + 4]
-                before = first[at + yb - 2 : at + yb] + second[at + yb - 4 : at + yb - 2]
+                further = (at + yb - 2 + yb // 2) % LANES
+                after = first[at : at + 2] + second[at + yb // 2 : at + yb // 2 + 2]
+                before = first[at + yb - 2 : at + yb] + second[further : further + 2]
                 for parity in range(2):
                     target[pl.ds(own_row + parity, yb, stride=2), :] = own[at : at + yb]
                     target[pl.ds(own_row + plan.y + parity, 2, stride=2), :] = after

time: 27.3 us -> 27.3 us (level)
  no operation moved by 1% of the time
where the time goes in v10:
time: 27.3 us; the launch traced here: 27.1 us
  starting transfers between devices  15.3 us (56%)
  waiting for transfers between devices  5.62 us (21%)
  Pallas kernels  5.47 us (20%)
  between operations  0.72 us (3%)
    ppermute x5, starting transfers between devices, shifted(): return lax.ppermute(value, everywhere, pairs)  7.94 us
    all_to_all x1, starting transfers between devices, exchange(): lax.all_to_all(send.reshape(plan.gx * plan.gy, plan.rows, LANES), everywh...  7.33 us
    ppermute x5, waiting for transfers between devices, shifted(): return lax.ppermute(value, everywhere, pairs)  5.62 us
    pallas_call x4, Pallas kernels, call(): pl.pallas_call(kernel, out_shape=[jax.ShapeDtypeStruct(shape, jnp.float32...  5.47 us
  transfers between devices with their start and end apart: 6, of which 2 were waited for; matrix products, arithmetic and copies ran while one was open for 0% of the time, Pallas kernels for 4%

profile of v10, /device:TPU:0, one launch (start us, length us, event | category | flops | bytes accessed | tf_op | source)
XLA Modules:
  0.0 27.1 jit_solution(2526377320333895797)
XLA Ops:
  0.6 2.5 %shard_map.41 = (f32[2,16,24,128]{3,2,1,0:T(8,128)}, f32[4,4,4,128]{3,2,1,0:T(4,128)}) custom-call(f32[8,16,128]{2,1,0:T(8,128)} %density.3, f32[19,4,4,128]{3,2,1,0:T(4,128)} %populations.3), custom_call_target="tpu_custom_call" | custom-call | tf_op jit(solution)/shard_map/pallas_call | solution.py:703
  3.1 0.0 copy-start
  3.1 0.0 copy-start.1
  3.2 0.0 copy-start.2
  3.2 7.3 %all-to-all-start = ((f32[32,24,128]{2,1,0:T(8,128)}), f32[32,24,128]{2,1,0:T(8,128)S(1)}, u32[]{:S(2)}, u32[]{:S(2)}) async-start(f32[32,24,128]{2,1,0:T(8,128)} %bitcast.3), calls=%async_computation | async-start | bytes 786432 | tf_op jit(solution)/shard_map/all_to_all | solution.py:735
  10.5 0.0 copy-done
  10.5 0.0 copy-done.1
  10.5 0.0 copy-done.2
  10.5 0.1 shard_map.42
  10.6 1.8 %collective-permute-start = (f32[200,128]{1,0:T(8,128)S(1)}, f32[200,128]{1,0:T(8,128)S(1)}, u32[]{:S(2)}, u32[]{:S(2)}) collective-permute-start(f32[200,128]{1,0:T(8,128)S(1)} %get-tuple-element.17), channel_id=1, source_target_pairs={{0,16},{1,17},{2,18},{3,19},{4,20},{5,21},{6,22},{7,23},{8,24},{9,... | collective-permute-start | bytes 307208 | tf_op jit(solution)/shard_map/ppermute | solution.py:723
  12.4 0.0 collective-permute-start.1
  12.4 4.4 %collective-permute-start.2 = (f32[92,128]{1,0:T(8,128)S(1)}, f32[92,128]{1,0:T(8,128)S(1)}, u32[]{:S(2)}, u32[]{:S(2)}) collective-permute-start(f32[92,128]{1,0:T(8,128)S(1)} %get-tuple-element.19), channel_id=1, source_target_pairs={{0,15},{1,2},{2,1},{3,4},{4,3},{5,6},{6,5},{7,8},{8,7},{9,10},{10,... | collective-permute-start | bytes 141320 | tf_op jit(solution)/shard_map/ppermute | solution.py:723
  16.8 0.0 collective-permute-start.3
  16.8 1.7 %collective-permute-start.4 = (f32[46,128]{1,0:T(8,128)S(1)}, f32[46,128]{1,0:T(8,128)S(1)}, u32[]{:S(2)}, u32[]{:S(2)}) collective-permute-start(f32[46,128]{1,0:T(8,128)S(1)} %get-tuple-element.21), channel_id=1, source_target_pairs={{0,31},{1,18},{2,17},{3,20},{4,19},{5,22},{6,21},{7,24},{8,23},{9,... | collective-permute-start | bytes 70664 | tf_op jit(solution)/shard_map/ppermute | solution.py:723
  18.5 1.5 %collective-permute-done.3.rest_3_ = f32[46,128]{1,0:T(8,128)S(1)} collective-permute-done((f32[46,128]{1,0:T(8,128)S(1)}, f32[46,128]{1,0:T(8,128)S(1)}, u32[]{:S(2)}, u32[]{:S(2)}) %collective-permute-start.3) | collective-permute-done | bytes 23584 | tf_op jit(solution)/shard_map/ppermute | solution.py:723
  20.1 4.1 %collective-permute-done.4.rest_4_ = f32[46,128]{1,0:T(8,128)S(1)} collective-permute-done((f32[46,128]{1,0:T(8,128)S(1)}, f32[46,128]{1,0:T(8,128)S(1)}, u32[]{:S(2)}, u32[]{:S(2)}) %collective-permute-start.4) | collective-permute-done | bytes 23584 | tf_op jit(solution)/shard_map/ppermute | solution.py:723
  24.2 0.0 collective-permute-done.1.rest_1_
  24.2 0.0 collective-permute-done.2.rest_2_
  24.2 0.0 collective-permute-done.rest_0_
  24.2 1.1 %shard_map.43 = (f32[16,32,128]{2,1,0:T(8,128)S(1)}, f32[3,16,24,128]{3,2,1,0:T(8,128)S(1)}, f32[16,24,128]{2,1,0:T(8,128)S(1)}, f32[3,4,24,128]{3,2,1,0:T(8,128...) custom-call(f32[8,16,128]{2,1,0:T(8,128)S(1)} %copy-done.1, f32[19,4,4,128]{3,2,1,0:T(4,128)S(1)} %copy-done, ...), custom_call_target="tpu_custom_call" | custom-call | tf_op jit(solution)/shard_map/pallas_call | solution.py:703
  25.3 0.0 all-to-all-done
  25.3 1.8 %shard_map.44 = (f32[8,16,128]{2,1,0:T(8,128)}, f32[19,4,4,128]{3,2,1,0:T(4,128)}) custom-call(f32[2,16,24,128]{3,2,1,0:T(8,128)S(1)} %bitcast.2, f32[16,32,128]{2,1,0:T(8,128)S(1)} %get-tuple-element.22.base, f32[3,16,24,128]{3,2,1,0:T(8,128)S(1)} %get-tuple-element.23.slope, f32[16,24,128]{2,1,0:T(8,128)S(1)} %get-tuple-element.24.drift, ...), custom_call_target="tpu_custom_call" | custom-call | tf_op jit(solution)/shard_map/pallas_call | solution.py:703
Async XLA Ops:
  3.1 7.4 %copy-start = (f32[19,4,4,128]{3,2,1,0:T(4,128)S(1)}, f32[19,4,4,128]{3,2,1,0:T(4,128)}, u32[]{:S(2)}) copy-start(f32[19,4,4,128]{3,2,1,0:T(4,128)} %populations.3) | copy-start | bytes 466948
  3.1 7.4 %copy-start.1 = (f32[8,16,128]{2,1,0:T(8,128)S(1)}, f32[8,16,128]{2,1,0:T(8,128)}, u32[]{:S(2)}) copy-start(f32[8,16,128]{2,1,0:T(8,128)} %density.3) | copy-start | bytes 196612
  3.2 7.4 %copy-start.2 = (f32[4,4,4,128]{3,2,1,0:T(4,128)S(1)}, f32[4,4,4,128]{3,2,1,0:T(4,128)}, u32[]{:S(2)}) copy-start(f32[4,4,4,128]{3,2,1,0:T(4,128)} %get-tuple-element.16.moments) | copy-start | bytes 98308
  3.2 22.1 %all-to-all-start = ((f32[32,24,128]{2,1,0:T(8,128)}), f32[32,24,128]{2,1,0:T(8,128)S(1)}, u32[]{:S(2)}, u32[]{:S(2)}) async-start(f32[32,24,128]{2,1,0:T(8,128)} %bitcast.3), calls=%async_computation | async-start | bytes 786432 | tf_op jit(solution)/shard_map/all_to_all | solution.py:735
  10.6 13.6 %collective-permute-start = (f32[200,128]{1,0:T(8,128)S(1)}, f32[200,128]{1,0:T(8,128)S(1)}, u32[]{:S(2)}, u32[]{:S(2)}) collective-permute-start(f32[200,128]{1,0:T(8,128)S(1)} %get-tuple-element.17), channel_id=1, source_target_pairs={{0,16},{1,17},{2,18},{3,19},{4,20},{5,21},{6,22},{7,23},{8,24},{9,... | collective-permute-start | bytes 307208 | tf_op jit(solution)/shard_map/ppermute | solution.py:723
  12.4 11.7 %collective-permute-start.1 = (f32[92,128]{1,0:T(8,128)S(1)}, f32[92,128]{1,0:T(8,128)S(1)}, u32[]{:S(2)}, u32[]{:S(2)}) collective-permute-start(f32[92,128]{1,0:T(8,128)S(1)} %get-tuple-element.18), channel_id=1, source_target_pairs={{0,1},{1,0},{2,3},{3,2},{4,5},{5,4},{6,7},{7,6},{8,9},{9,8},{10,11... | collective-permute-start | bytes 141320 | tf_op jit(solution)/shard_map/ppermute | solution.py:723
  12.4 11.7 %collective-permute-start.2 = (f32[92,128]{1,0:T(8,128)S(1)}, f32[92,128]{1,0:T(8,128)S(1)}, u32[]{:S(2)}, u32[]{:S(2)}) collective-permute-start(f32[92,128]{1,0:T(8,128)S(1)} %get-tuple-element.19), channel_id=1, source_target_pairs={{0,15},{1,2},{2,1},{3,4},{4,3},{5,6},{6,5},{7,8},{8,7},{9,10},{10,... | collective-permute-start | bytes 141320 | tf_op jit(solution)/shard_map/ppermute | solution.py:723
  16.8 3.3 %collective-permute-start.3 = (f32[46,128]{1,0:T(8,128)S(1)}, f32[46,128]{1,0:T(8,128)S(1)}, u32[]{:S(2)}, u32[]{:S(2)}) collective-permute-start(f32[46,128]{1,0:T(8,128)S(1)} %get-tuple-element.20), channel_id=1, source_target_pairs={{0,17},{1,16},{2,19},{3,18},{4,21},{5,20},{6,23},{7,22},{8,25},{9,... | collective-permute-start | bytes 70664 | tf_op jit(solution)/shard_map/ppermute | solution.py:723
  16.8 7.3 %collective-permute-start.4 = (f32[46,128]{1,0:T(8,128)S(1)}, f32[46,128]{1,0:T(8,128)S(1)}, u32[]{:S(2)}, u32[]{:S(2)}) collective-permute-start(f32[46,128]{1,0:T(8,128)S(1)} %get-tuple-element.21), channel_id=1, source_target_pairs={{0,31},{1,18},{2,17},{3,20},{4,19},{5,22},{6,21},{7,24},{8,23},{9,... | collective-permute-start | bytes 70664 | tf_op jit(solution)/shard_map/ppermute | solution.py:723
